TPU v7x, 512 devices: a whole 4x8x8 slice. The times are simulated.
512 devices in a mesh: grp: 16 (over y, core), dev: 32 (over x, z).
Axes of the slice: x: 4, y: 8, z: 8, core: 2. Of those that a mesh axis runs over, the one named last changes fastest.
Arguments:
- memory: float32 [262144, 256], P(('grp', 'dev')), may hold values from -4 to 4
- want_end: int32 [512, 512, 2], P(('grp', 'dev')), may hold values from -1 to 511, as said below
- want_near: int32 [512, 512, 16], P(('grp', 'dev')), may hold values from -1 to 511, as said below
- end_slot: int32 [65536, 2], P(('grp', 'dev')), may hold values from 0 to 1023, as said below
- near_slot: int32 [65536, 20], P(('grp', 'dev')), may hold values from 0 to 8191, as said below
- near_count: int32 [65536, 2], P(('grp', 'dev')), may hold values from 1 to 10
- event_time: int32 [65536], P(('grp', 'dev')), may hold values from 1024 to 131071
- near_time: int32 [65536, 20], P(('grp', 'dev')), may hold values from 1 to 131071, as said below
- frequency: float32 [128], replicated, may hold values from 0.001 to 0.5
- phases: float32 [128], replicated, may hold values from -3.140625 to 3.140625
- query_weight: bfloat16 [384, 256], replicated, may hold values from -0.3125 to 0.3125
- key_weight: bfloat16 [384, 256], replicated, may hold values from -0.3125 to 0.3125
- value_weight: bfloat16 [384, 256], replicated, may hold values from -0.3125 to 0.3125
- out_weight: bfloat16 [512, 256], replicated, may hold values from -0.25 to 0.25
- out_bias: float32 [256], replicated, may hold values from -4 to 4
- message_in: bfloat16 [512, 256], replicated, may hold values from -0.25 to 0.25
- message_out: bfloat16 [256, 256], replicated, may hold values from -0.375 to 0.375
- input_weight: bfloat16 [256, 768], replicated, may hold values from -0.375 to 0.375
- state_weight: bfloat16 [256, 768], replicated, may hold values from -0.375 to 0.375
- update_bias: float32 [768], replicated, may hold values from -4 to 4
Outputs:
- new_memory: float32 [262144, 256], P(('grp', 'dev'))
- event_embed: bfloat16 [65536, 512], P(('grp', 'dev'))
Inputs may be any that keep to these rules, and one draw needn't show every extreme that they name: `want_end`: for each asking device a quarter of the owners get 2 filled slots, half get 1, a quarter none, chosen by the draw; filled slots come first and hold a row of the owner's 512 rows, empty slots hold -1. `want_near`: all devices of one grp index ask each owner for the same slots. 64 owners, the same for every asking device, get all 16 slots filled; every other owner gets 16 // 2 to 15 filled slots; filled slots come first and hold a row of the owner's rows, empty slots hold -1. `end_slot`: the value o * 2 + s names slot s of owner o in the event's own device's want_end, always a filled slot. `near_slot`: the value o * 16 + s names slot s of owner o in the event's own device's want_near, always a filled slot. near_time[e, i] lies in event_time[e] - 1023 to event_time[e].
All inputs are finite; a program needn't handle non-finite values.
Results may differ from a plain program's by a relative error of at most 0.0042.
Values may be sent and summed in bfloat16 or wider, within the bound.
No kernel may reach another device: no remote copies, remote signals or barrier semaphores. Data moves between devices by JAX's collectives and lax.ppermute only.
A program may use at most 64 MiB of HBM per device.

v0:
```python
import math

import jax
import jax.numpy as jnp
from jax import lax
from jax.sharding import PartitionSpec as P

HEADS = 2
K = 10
CAP_E = 2
CAP_N = 16


def look_up(table, wanted):
    clipped = jnp.maximum(wanted, 0)
    fetched = jnp.take(table, clipped, axis=0)
    return jnp.where((wanted >= 0)[..., None], fetched, jnp.zeros_like(fetched))


def event_block(
    end_rows,
    near_rows,
    elapsed,
    near_count,
    frequency,
    phases,
    query_weight,
    key_weight,
    value_weight,
    out_weight,
    out_bias,
    message_in,
    message_out,
):
    events = end_rows.shape[1]
    row_width = end_rows.shape[-1]
    head_size = row_width // HEADS
    fixed_code = jnp.broadcast_to(
        jnp.cos(phases).astype(jnp.bfloat16), (2, events, phases.shape[0])
    )
    near_code = jnp.cos(elapsed[..., None] * frequency + phases).astype(jnp.bfloat16)
    query_in = jnp.concatenate([end_rows, fixed_code], -1)
    queries = jnp.einsum("jec,cd->jed", query_in, query_weight, preferred_element_type=jnp.float32)
    near_in = jnp.concatenate([near_rows, near_code], -1)
    key_rows = jnp.einsum("jkec,cd->jked", near_in, key_weight, preferred_element_type=jnp.float32)
    values = jnp.einsum("jkec,cd->jked", near_in, value_weight, preferred_element_type=jnp.float32)
    usable = jnp.arange(K)[None, :, None] < near_count[:, None, :]
    pieces = []
    for head in range(HEADS):
        low = head * head_size
        high = low + head_size
        scores = jnp.sum(
            queries[:, None, :, low:high] * key_rows[..., low:high], axis=-1
        ) / math.sqrt(head_size)
        exponent = jnp.where(usable, jnp.exp(scores), jnp.zeros_like(scores))
        weight = exponent / jnp.sum(exponent, axis=1, keepdims=True)
        pieces.append(jnp.sum(weight[..., None] * values[..., low:high], axis=1))
    attended = jnp.concatenate(pieces, -1).astype(jnp.bfloat16)
    joined = jnp.concatenate([attended, end_rows], -1)
    embedded = jax.nn.relu(
        jnp.einsum("jec,cd->jed", joined, out_weight, preferred_element_type=jnp.float32) + out_bias
    ).astype(jnp.bfloat16)
    paired = jnp.concatenate([embedded, embedded[::-1]], -1)
    hidden = jax.nn.relu(
        jnp.einsum("jec,cd->jed", paired, message_in, preferred_element_type=jnp.float32)
    ).astype(jnp.bfloat16)
    message = jnp.einsum("jec,cd->jed", hidden, message_out, preferred_element_type=jnp.float32)
    return (embedded, message)


def gru_update(memory, mem_half, totals, counts, input_weight, state_weight, update_bias):
    row_width = memory.shape[1]
    averaged = (totals / jnp.maximum(counts, 1.0)[:, None]).astype(jnp.bfloat16)
    from_msg = jnp.dot(averaged, input_weight, preferred_element_type=jnp.float32)
    from_state = jnp.dot(mem_half, state_weight, preferred_element_type=jnp.float32)
    update_gate = jax.nn.sigmoid(
        from_msg[:, :row_width] + from_state[:, :row_width] + update_bias[:row_width]
    )
    reset_gate = jax.nn.sigmoid(
        from_msg[:, row_width : 2 * row_width]
        + from_state[:, row_width : 2 * row_width]
        + update_bias[row_width : 2 * row_width]
    )
    candidate = jnp.tanh(
        from_msg[:, 2 * row_width :]
        + update_bias[2 * row_width :]
        + reset_gate * from_state[:, 2 * row_width :]
    )
    updated = (1.0 - update_gate) * candidate + update_gate * memory
    return jnp.where((counts > 0)[:, None], updated, memory)


def local(
    memory,
    want_end,
    want_near,
    end_slot,
    near_slot,
    near_count,
    event_time,
    near_time,
    frequency,
    phases,
    query_weight,
    key_weight,
    value_weight,
    out_weight,
    out_bias,
    message_in,
    message_out,
    input_weight,
    state_weight,
    update_bias,
):
    groups = lax.axis_size("grp")
    members = lax.axis_size("dev")
    row_width = memory.shape[1]
    events = end_slot.shape[0]
    ask_end = want_end.reshape(groups, members, CAP_E)
    ask_near = want_near.reshape(groups, members, CAP_N)
    mem_half = memory.astype(jnp.bfloat16)
    got_end, got_near = (
        lax.all_to_all(
            lax.all_to_all(ask_end, "grp", split_axis=0, concat_axis=0, tiled=True),
            "dev",
            split_axis=1,
            concat_axis=1,
            tiled=True,
        ),
        lax.all_to_all(
            lax.all_to_all(ask_near, "grp", split_axis=0, concat_axis=0, tiled=True),
            "dev",
            split_axis=1,
            concat_axis=1,
            tiled=True,
        ),
    )
    fetched_end, fetched_near = (
        lax.all_to_all(
            lax.all_to_all(
                look_up(mem_half, got_end), "grp", split_axis=0, concat_axis=0, tiled=True
            ),
            "dev",
            split_axis=1,
            concat_axis=1,
            tiled=True,
        ),
        lax.all_to_all(
            lax.all_to_all(
                look_up(mem_half, got_near), "grp", split_axis=0, concat_axis=0, tiled=True
            ),
            "dev",
            split_axis=1,
            concat_axis=1,
            tiled=True,
        ),
    )
    end_index = jnp.transpose(end_slot)
    near_index = jnp.transpose(near_slot).reshape(2, K, events)
    end_rows = jnp.take(fetched_end.reshape(-1, row_width), end_index, axis=0)
    near_rows = jnp.take(fetched_near.reshape(-1, row_width), near_index, axis=0)
    elapsed = (
        (event_time[None, :] - jnp.transpose(near_time)).astype(jnp.float32).reshape(2, K, events)
    )
    embedded, message = event_block(
        end_rows,
        near_rows,
        elapsed,
        jnp.transpose(near_count),
        frequency,
        phases,
        query_weight,
        key_weight,
        value_weight,
        out_weight,
        out_bias,
        message_in,
        message_out,
    )
    flat_slots = end_index.reshape(-1)
    slot_sum = (
        jnp.zeros((groups * members * CAP_E, row_width), jnp.float32)
        .at[flat_slots]
        .add(message.reshape(-1, row_width))
    )
    slot_count = (
        jnp.zeros((groups * members * CAP_E,), jnp.float32)
        .at[flat_slots]
        .add(jnp.ones(flat_slots.shape, jnp.float32))
    )
    slot_sum = slot_sum.reshape(groups, members, CAP_E, row_width)
    slot_count = slot_count.reshape(groups, members, CAP_E)
    news_sum, news_count = (
        lax.all_to_all(
            lax.all_to_all(
                slot_sum.astype(jnp.bfloat16), "grp", split_axis=0, concat_axis=0, tiled=True
            ),
            "dev",
            split_axis=1,
            concat_axis=1,
            tiled=True,
        ).astype(slot_sum.dtype),
        lax.all_to_all(
            lax.all_to_all(
                slot_count.astype(jnp.bfloat16), "grp", split_axis=0, concat_axis=0, tiled=True
            ),
            "dev",
            split_axis=1,
            concat_axis=1,
            tiled=True,
        ).astype(slot_count.dtype),
    )
    owned_rows = jnp.maximum(got_end, 0).reshape(-1)
    totals = (
        jnp.zeros((memory.shape[0], row_width), jnp.float32)
        .at[owned_rows]
        .add(news_sum.reshape(-1, row_width))
    )
    counts = jnp.zeros((memory.shape[0],), jnp.float32).at[owned_rows].add(news_count.reshape(-1))
    new_memory = gru_update(
        memory, mem_half, totals, counts, input_weight, state_weight, update_bias
    )
    return (new_memory, jnp.concatenate([embedded[0], embedded[1]], 1))


def solution(mesh):
    in_specs = (
        P(("grp", "dev"), None),
        P(("grp", "dev"), None, None),
        P(("grp", "dev"), None, None),
        P(("grp", "dev"), None),
        P(("grp", "dev"), None),
        P(("grp", "dev"), None),
        P(("grp", "dev")),
        P(("grp", "dev"), None),
        P(),
        P(),
        P(),
        P(),
        P(),
        P(),
        P(),
        P(),
        P(),
        P(),
        P(),
        P(),
    )
    out_specs = (P(("grp", "dev"), None), P(("grp", "dev"), None))
    return jax.shard_map(local, mesh=mesh, in_specs=in_specs, out_specs=out_specs, check_vma=False)
```

profile of v0, /device:TPU:1, one launch (start us, length us, event | category | flops | bytes accessed | tf_op | source)
XLA Modules:
  0.0 442.1 jit_solution(9678170120008122707)
XLA Ops:
  1.5 16.6 %all_to_all.60 = s32[16,32,2]{1,2,0:T(2,128)S(1)} all-to-all(s32[16,32,2]{1,2,0:T(2,128)S(1)} %copy.80), channel_id=1, replica_groups=mesh['grp'=16,'dev'=32] {'grp'}, dimensions={0} | all-to-all | bytes 8192 | tf_op jit(solution)/shard_map/all_to_all | solution.py:124
  18.8 12.0 %all-to-all-start.1 = ((s32[16,32,2]{0,2,1:T(2,128)}), s32[16,32,2]{0,2,1:T(2,128)S(1)}, u32[]{:S(2)}, u32[]{:S(2)}) async-start(s32[16,32,2]{0,2,1:T(2,128)} %copy.81), calls=%async_computation.1 | async-start | bytes 65536 | tf_op jit(solution)/shard_map/all_to_all | solution.py:123
  34.2 2.3 scatter_custom_fusion
  39.6 5.1 %all-to-all-start.6 = ((s32[16,1,512]{2,1,0:T(1,128)}), s32[16,1,512]{2,1,0:T(1,128)S(1)}, u32[]{:S(2)}, u32[]{:S(2)}) async-start(s32[16,1,512]{2,1,0:T(1,128)} %reshape.289), calls=%async_computation.6 | async-start | bytes 65536 | tf_op jit(solution)/shard_map/all_to_all | solution.py:131
  45.1 3.9 gather_fusion
  49.7 2.4 all-to-all-done.6
  54.3 6.4 %all-to-all-start.7 = ((s32[32,1,256]{2,1,0:T(1,128)}), s32[32,1,256]{2,1,0:T(1,128)S(1)}, u32[]{:S(2)}, u32[]{:S(2)}) async-start(s32[32,1,256]{2,1,0:T(1,128)} %reshape.291), calls=%async_computation.7 | async-start | bytes 65536 | tf_op jit(solution)/shard_map/all_to_all | solution.py:130
  60.7 2.4 broadcast_select_fusion.2
  63.0 6.4 %all-to-all-done.7 = s32[32,1,256]{2,1,0:T(1,128)S(1)} async-done(((s32[32,1,256]{2,1,0:T(1,128)}), s32[32,1,256]{2,1,0:T(1,128)S(1)}, u32[]{:S(2)}, u32[]{:S(2)}) %all-to-all-start.7) | async-done | bytes 32800 | tf_op jit(solution)/shard_map/all_to_all | solution.py:130
  69.4 6.2 %all-to-all-start.2 = ((bf16[16,32,2]{1,2,0:T(2,128)(2,1)}), bf16[16,32,2]{1,2,0:T(2,128)(2,1)S(1)}, u32[]{:S(2)}, u32[]{:S(2)}) async-start(bf16[16,32,2]{1,2,0:T(2,128)(2,1)} %copy.84), calls=%async_computation.2 | async-start | bytes 16384 | tf_op jit(solution)/shard_map/all_to_all | solution.py:204
  76.9 5.8 %all-to-all-done.2 = bf16[16,32,2]{1,2,0:T(2,128)(2,1)S(1)} async-done(((bf16[16,32,2]{1,2,0:T(2,128)(2,1)}), bf16[16,32,2]{1,2,0:T(2,128)(2,1)S(1)}, u32[]{:S(2)}, u32[]{:S(2)}) %all-to-all-start.2) | async-done | bytes 2080 | tf_op jit(solution)/shard_map/all_to_all | solution.py:204
  82.7 4.0 all-to-all-start.4
  86.8 33.1 %gather_fusion.2 = bf16[8192,256]{1,0:T(8,128)(2,1)} fusion(bf16[512,256]{1,0:T(8,128)(2,1)S(1)} %convert_element_type.41, s32[8192]{0:T(1024)S(1)} %broadcast_clamp_fusion), kind=kCustom, calls=%fused_computation.2 | custom fusion | bytes 8421376 | tf_op jit(solution)/shard_map/jit(_take)/gather | solution.py:16
  120.2 7.7 %select_select_fusion = bf16[16,32,16,256]{3,2,1,0:T(8,128)(2,1)} fusion(bf16[16,32,16,256]{3,2,1,0:T(8,128)(2,1)} %bitcast.64, pred[16,32,16]{2,1,0:T(8,128)(4,1)S(1)} %copy.99, pred[16,32,16]{2,1,0:T(8,128)(4,1)S(1)} %copy.97), kind=kLoop, calls=%fused_computation.8 | loop fusion | flops 4194304 | bytes 8404992 | tf_op jit(solution)/shard_map/jit(_where)/select_n | solution.py:17
  127.9 7.3 %all-to-all-start.8 = ((bf16[16,32,16,256]{3,2,1,0:T(8,128)(2,1)}), bf16[16,32,16,256]{3,2,1,0:T(8,128)(2,1)}, u32[]{:S(2)}, u32[]{:S(2)}) async-start(bf16[16,32,16,256]{3,2,1,0:T(8,128)(2,1)} %select_select_fusion), calls=%async_computation.8 | async-start | bytes 8388608 | tf_op jit(solution)/shard_map/all_to_all | solution.py:149
  136.5 92.2 %all-to-all-done.8 = bf16[16,32,16,256]{3,2,1,0:T(8,128)(2,1)} async-done(((bf16[16,32,16,256]{3,2,1,0:T(8,128)(2,1)}), bf16[16,32,16,256]{3,2,1,0:T(8,128)(2,1)}, u32[]{:S(2)}, u32[]{:S(2)}) %all-to-all-start.8) | async-done | bytes 4194336 | tf_op jit(solution)/shard_map/all_to_all | solution.py:149
  228.7 3.9 all-to-all-start.5
  232.6 4.7 %copy.101 = bf16[16,32,16,256]{3,2,0,1:T(8,128)(2,1)} copy(bf16[16,32,16,256]{3,2,1,0:T(8,128)(2,1)} %all-to-all-done.8) | data formatting | bytes 8388608 | tf_op jit(solution)/shard_map/all_to_all | solution.py:149
  237.4 9.8 %all-to-all-done.5 = bf16[16,32,2,256]{3,2,0,1:T(2,128)(2,1)S(1)} async-done(((bf16[16,32,2,256]{3,2,0,1:T(2,128)(2,1)}), bf16[16,32,2,256]{3,2,0,1:T(2,128)(2,1)S(1)}, u32[]{:S(2)}, u32[]{:S(2)}) %all-to-all-start.5) | async-done | bytes 524320 | tf_op jit(solution)/shard_map/all_to_all | solution.py:139
  247.2 7.4 %all-to-all-start.9 = ((bf16[16,32,16,256]{3,2,0,1:T(8,128)(2,1)}), bf16[16,32,16,256]{3,2,0,1:T(8,128)(2,1)}, u32[]{:S(2)}, u32[]{:S(2)}) async-start(bf16[16,32,16,256]{3,2,0,1:T(8,128)(2,1)} %copy.101), calls=%async_computation.9 | async-start | bytes 8388608 | tf_op jit(solution)/shard_map/all_to_all | solution.py:148
  254.8 4.7 %cosine_convert_fusion = bf16[2,10,128,128]{3,2,1,0:T(8,128)(2,1)S(1)} fusion(f32[128]{0:T(128)S(1)} %copy-done.15, f32[128]{0:T(128)S(1)} %copy-done.16, f32[2,10,128]{2,1,0:T(8,128)S(1)} %mul.57), kind=kLoop, calls=%fused_computation.18 | loop fusion | flops 983040 | bytes 666624 | tf_op jit(solution)/shard_map/convert_element_type | solution.py:41
  262.4 88.0 %all-to-all-done.9 = bf16[16,32,16,256]{3,2,0,1:T(8,128)(2,1)} async-done(((bf16[16,32,16,256]{3,2,0,1:T(8,128)(2,1)}), bf16[16,32,16,256]{3,2,0,1:T(8,128)(2,1)}, u32[]{:S(2)}, u32[]{:S(2)}) %all-to-all-start.9) | async-done | bytes 4194336 | tf_op jit(solution)/shard_map/all_to_all | solution.py:148
  350.4 6.3 %all-to-all-start.3 = ((bf16[16,32,2]{0,2,1:T(2,128)(2,1)}), bf16[16,32,2]{0,2,1:T(2,128)(2,1)S(1)}, u32[]{:S(2)}, u32[]{:S(2)}) async-start(bf16[16,32,2]{0,2,1:T(2,128)(2,1)} %copy.85), calls=%async_computation.3 | async-start | bytes 32768 | tf_op jit(solution)/shard_map/all_to_all | solution.py:203
  356.8 4.6 %copy.102 = bf16[16,32,16,256]{3,2,1,0:T(8,128)(2,1)} copy(bf16[16,32,16,256]{3,2,0,1:T(8,128)(2,1)} %all-to-all-done.9) | data formatting | bytes 8388608 | tf_op jit(solution)/shard_map/all_to_all | solution.py:148
  361.4 8.5 %gather_fusion.3 = bf16[2560,256]{1,0:T(8,128)(2,1)S(1)} fusion(bf16[8192,256]{1,0:T(8,128)(2,1)} %bitcast.63, s32[3072]{0:T(1024)S(1)} %pad_clamp_fusion), kind=kCustom, calls=%fused_computation.3 | custom fusion | bytes 2631680 | tf_op jit(solution)/shard_map/jit(_take)/gather | solution.py:161
  375.0 2.3 scatter_custom_fusion.2
  378.4 6.7 %all-to-all-start.10 = ((bf16[16,32,2,256]{3,2,1,0:T(2,128)(2,1)}), bf16[16,32,2,256]{3,2,1,0:T(2,128)(2,1)S(1)}, u32[]{:S(2)}, u32[]{:S(2)}) async-start(bf16[16,32,2,256]{3,2,1,0:T(2,128)(2,1)} %convert_element_type.49), calls=%async_computation.10 | async-start | bytes 1048576 | tf_op jit(solution)/shard_map/all_to_all | solution.py:195
  386.7 15.6 %all-to-all-done.10 = bf16[16,32,2,256]{3,2,1,0:T(2,128)(2,1)S(1)} async-done(((bf16[16,32,2,256]{3,2,1,0:T(2,128)(2,1)}), bf16[16,32,2,256]{3,2,1,0:T(2,128)(2,1)S(1)}, u32[]{:S(2)}, u32[]{:S(2)}) %all-to-all-start.10) | async-done | bytes 524320 | tf_op jit(solution)/shard_map/all_to_all | solution.py:195
  403.7 9.5 %all-to-all-start.11 = ((bf16[16,32,2,256]{3,2,0,1:T(2,128)(2,1)}), bf16[16,32,2,256]{3,2,0,1:T(2,128)(2,1)S(1)}, u32[]{:S(2)}, u32[]{:S(2)}) async-start(bf16[16,32,2,256]{3,2,0,1:T(2,128)(2,1)} %copy.103), calls=%async_computation.11 | async-start | bytes 1048576 | tf_op jit(solution)/shard_map/all_to_all | solution.py:194
  413.2 7.8 %scatter_custom_fusion.1 = f32[512]{0:T(512)S(1)} fusion(s32[1024]{0:T(1024)S(1)} %bitcast.75, f32[1024]{0:T(1024)S(1)} %reshape.246, f32[]{:T(128)} %constant.44.clone.1), kind=kCustom, calls=%fused_computation.109 | custom fusion | flops 1024 | bytes 2052 | tf_op jit(solution)/shard_map/scatter-add | solution.py:219
  421.8 8.1 %all-to-all-done.11 = bf16[16,32,2,256]{3,2,0,1:T(2,128)(2,1)S(1)} async-done(((bf16[16,32,2,256]{3,2,0,1:T(2,128)(2,1)}), bf16[16,32,2,256]{3,2,0,1:T(2,128)(2,1)S(1)}, u32[]{:S(2)}, u32[]{:S(2)}) %all-to-all-start.11) | async-done | bytes 524320 | tf_op jit(solution)/shard_map/all_to_all | solution.py:194
  432.7 6.7 %scatter_custom_fusion.3 = f32[512,256]{1,0:T(8,128)S(1)} fusion(s32[1024]{0:T(1024)S(1)} %bitcast.76, f32[1024,256]{1,0:T(8,128)} %reshape.262, f32[]{:T(128)} %constant.44.clone.1), kind=kCustom, calls=%fused_computation.65 | custom fusion | flops 262144 | bytes 524800 | tf_op jit(solution)/shard_map/scatter-add | solution.py:217
  (131 shorter events, 32.2 us)
Async XLA Ops:
  0.6 385.1 %copy-start = (bf16[256,768]{1,0:T(8,128)(2,1)S(1)}, bf16[256,768]{1,0:T(8,128)(2,1)}, u32[]{:S(2)}) copy-start(bf16[256,768]{1,0:T(8,128)(2,1)} %param.38) | copy-start | bytes 1179652
  18.8 20.8 %all-to-all-start.1 = ((s32[16,32,2]{0,2,1:T(2,128)}), s32[16,32,2]{0,2,1:T(2,128)S(1)}, u32[]{:S(2)}, u32[]{:S(2)}) async-start(s32[16,32,2]{0,2,1:T(2,128)} %copy.81), calls=%async_computation.1 | async-start | bytes 65536 | tf_op jit(solution)/shard_map/all_to_all | solution.py:123
  31.5 5.0 %copy-start.13 = (s32[256,1]{0,1:T(1,128)}, s32[256,1]{0,1:T(1,128)S(1)}, u32[]{:S(2)}) copy-start(s32[256,1]{0,1:T(1,128)S(1)} %compare_select_fusion.3) | copy-start | bytes 3076
  39.6 12.5 %all-to-all-start.6 = ((s32[16,1,512]{2,1,0:T(1,128)}), s32[16,1,512]{2,1,0:T(1,128)S(1)}, u32[]{:S(2)}, u32[]{:S(2)}) async-start(s32[16,1,512]{2,1,0:T(1,128)} %reshape.289), calls=%async_computation.6 | async-start | bytes 65536 | tf_op jit(solution)/shard_map/all_to_all | solution.py:131
  54.3 15.2 %all-to-all-start.7 = ((s32[32,1,256]{2,1,0:T(1,128)}), s32[32,1,256]{2,1,0:T(1,128)S(1)}, u32[]{:S(2)}, u32[]{:S(2)}) async-start(s32[32,1,256]{2,1,0:T(1,128)} %reshape.291), calls=%async_computation.7 | async-start | bytes 65536 | tf_op jit(solution)/shard_map/all_to_all | solution.py:130
  69.4 13.3 %all-to-all-start.2 = ((bf16[16,32,2]{1,2,0:T(2,128)(2,1)}), bf16[16,32,2]{1,2,0:T(2,128)(2,1)S(1)}, u32[]{:S(2)}, u32[]{:S(2)}) async-start(bf16[16,32,2]{1,2,0:T(2,128)(2,1)} %copy.84), calls=%async_computation.2 | async-start | bytes 16384 | tf_op jit(solution)/shard_map/all_to_all | solution.py:204
  82.7 45.2 %all-to-all-start.4 = ((bf16[16,32,2,256]{3,2,1,0:T(2,128)(2,1)}), bf16[16,32,2,256]{3,2,1,0:T(2,128)(2,1)S(1)}, u32[]{:S(2)}, u32[]{:S(2)}) async-start(bf16[16,32,2,256]{3,2,1,0:T(2,128)(2,1)} %broadcast_select_fusion.2), calls=%async_computation.4 | async-start | bytes 1048576 | tf_op jit(solution)/shard_map/all_to_all | solution.py:140
  127.9 100.8 %all-to-all-start.8 = ((bf16[16,32,16,256]{3,2,1,0:T(8,128)(2,1)}), bf16[16,32,16,256]{3,2,1,0:T(8,128)(2,1)}, u32[]{:S(2)}, u32[]{:S(2)}) async-start(bf16[16,32,16,256]{3,2,1,0:T(8,128)(2,1)} %select_select_fusion), calls=%async_computation.8 | async-start | bytes 8388608 | tf_op jit(solution)/shard_map/all_to_all | solution.py:149
  228.7 18.5 %all-to-all-start.5 = ((bf16[16,32,2,256]{3,2,0,1:T(2,128)(2,1)}), bf16[16,32,2,256]{3,2,0,1:T(2,128)(2,1)S(1)}, u32[]{:S(2)}, u32[]{:S(2)}) async-start(bf16[16,32,2,256]{3,2,0,1:T(2,128)(2,1)} %copy.92), calls=%async_computation.5 | async-start | bytes 1048576 | tf_op jit(solution)/shard_map/all_to_all | solution.py:139
  237.3 17.2 %copy-start.5 = (s32[128,20]{0,1:T(8,128)S(1)}, s32[128,20]{0,1:T(8,128)}, u32[]{:S(2)}) copy-start(s32[128,20]{0,1:T(8,128)} %param.24) | copy-start | bytes 30724
  237.3 17.3 %copy-start.6 = (s32[128,20]{0,1:T(8,128)S(1)}, s32[128,20]{0,1:T(8,128)}, u32[]{:S(2)}) copy-start(s32[128,20]{0,1:T(8,128)} %param.27) | copy-start | bytes 30724
  237.3 17.3 %copy-start.14 = (s32[128]{0:T(128)S(1)}, s32[128]{0:T(128)}, u32[]{:S(2)}) copy-start(s32[128]{0:T(128)} %param.26) | copy-start | bytes 1540
  237.3 17.3 %copy-start.15 = (f32[128]{0:T(128)S(1)}, f32[128]{0:T(128)}, u32[]{:S(2)}) copy-start(f32[128]{0:T(128)} %param.29) | copy-start | bytes 1540
  237.3 17.4 %copy-start.11 = (s32[128,2]{0,1:T(2,128)S(1)}, s32[128,2]{0,1:T(2,128)}, u32[]{:S(2)}) copy-start(s32[128,2]{0,1:T(2,128)} %param.23) | copy-start | bytes 3076
  237.3 17.4 %copy-start.16 = (f32[128]{0:T(128)S(1)}, f32[128]{0:T(128)}, u32[]{:S(2)}) copy-start(f32[128]{0:T(128)} %param.28) | copy-start | bytes 1540
  247.2 103.3 %all-to-all-start.9 = ((bf16[16,32,16,256]{3,2,0,1:T(8,128)(2,1)}), bf16[16,32,16,256]{3,2,0,1:T(8,128)(2,1)}, u32[]{:S(2)}, u32[]{:S(2)}) async-start(bf16[16,32,16,256]{3,2,0,1:T(8,128)(2,1)} %copy.101), calls=%async_computation.9 | async-start | bytes 8388608 | tf_op jit(solution)/shard_map/all_to_all | solution.py:148
  254.8 7.4 %copy-start.4 = (bf16[384,256]{1,0:T(8,128)(2,1)S(1)}, bf16[384,256]{1,0:T(8,128)(2,1)}, u32[]{:S(2)}) copy-start(bf16[384,256]{1,0:T(8,128)(2,1)} %param.30) | copy-start | bytes 589828
  350.4 28.0 %all-to-all-start.3 = ((bf16[16,32,2]{0,2,1:T(2,128)(2,1)}), bf16[16,32,2]{0,2,1:T(2,128)(2,1)S(1)}, u32[]{:S(2)}, u32[]{:S(2)}) async-start(bf16[16,32,2]{0,2,1:T(2,128)(2,1)} %copy.85), calls=%async_computation.3 | async-start | bytes 32768 | tf_op jit(solution)/shard_map/all_to_all | solution.py:203
  369.9 0.9 copy-start.2
  370.8 0.9 copy-start.3
  372.6 0.8 copy-start.7
  373.3 1.0 copy-start.17
  373.4 1.0 copy-start.20
  373.4 1.2 copy-start.18
  373.5 1.2 copy-start.19
  377.4 7.8 %copy-start.12 = (f32[768]{0:T(1024)S(1)}, f32[768]{0:T(1024)}, u32[]{:S(2)}) copy-start(f32[768]{0:T(1024)} %param.39) | copy-start | bytes 9220
  378.4 23.9 %all-to-all-start.10 = ((bf16[16,32,2,256]{3,2,1,0:T(2,128)(2,1)}), bf16[16,32,2,256]{3,2,1,0:T(2,128)(2,1)S(1)}, u32[]{:S(2)}, u32[]{:S(2)}) async-start(bf16[16,32,2,256]{3,2,1,0:T(2,128)(2,1)} %convert_element_type.49), calls=%async_computation.10 | async-start | bytes 1048576 | tf_op jit(solution)/shard_map/all_to_all | solution.py:195
  403.7 26.1 %all-to-all-start.11 = ((bf16[16,32,2,256]{3,2,0,1:T(2,128)(2,1)}), bf16[16,32,2,256]{3,2,0,1:T(2,128)(2,1)S(1)}, u32[]{:S(2)}, u32[]{:S(2)}) async-start(bf16[16,32,2,256]{3,2,0,1:T(2,128)(2,1)} %copy.103), calls=%async_computation.11 | async-start | bytes 1048576 | tf_op jit(solution)/shard_map/all_to_all | solution.py:194
  432.7 8.2 %copy-start.1 = (f32[512,256]{1,0:T(8,128)S(1)}, f32[512,256]{1,0:T(8,128)}, u32[]{:S(2)}) copy-start(f32[512,256]{1,0:T(8,128)} %param.20) | copy-start | bytes 1572868
  432.7 8.2 %copy-start.8 = (f32[256]{0:T(256)S(1)}, f32[256]{0:T(256)}, u32[]{:S(2)}) copy-start(f32[256]{0:T(256)} %get-tuple-element.16) | copy-start | bytes 3076
  432.7 8.2 %copy-start.9 = (f32[256]{0:T(256)S(1)}, f32[256]{0:T(256)}, u32[]{:S(2)}) copy-start(f32[256]{0:T(256)} %get-tuple-element.17) | copy-start | bytes 3076
  432.7 8.2 %copy-start.10 = (f32[256]{0:T(256)S(1)}, f32[256]{0:T(256)}, u32[]{:S(2)}) copy-start(f32[256]{0:T(256)} %get-tuple-element.18) | copy-start | bytes 3076
where the time goes:
time: 444 us; the launch traced here: 442 us
  waiting for transfers between devices  230 us (52%)
  starting transfers between devices  74.8 us (17%)
  local copies, waits for them, and re-layouts  73 us (16%)
  other arithmetic  41.7 us (9%)
  blocking collectives  16.6 us (4%)
    all_to_all x1, waiting for transfers between devices, local(): lax.all_to_all(look_up(mem_half, got_near), 'grp', split_axis=0, concat_a...  92.2 us
    all_to_all x1, waiting for transfers between devices, local(): lax.all_to_all(lax.all_to_all(look_up(mem_half, got_near), 'grp', split_a...  88 us
    gather x3, local copies, waits for them, and re-layouts, look_up(): fetched = jnp.take(table, clipped, axis=0)  37.2 us
    all_to_all x1, blocking collectives, local(): lax.all_to_all(ask_end, 'grp', split_axis=0, concat_axis=0, tiled=True)  16.6 us
    all_to_all x1, waiting for transfers between devices, local(): lax.all_to_all(slot_sum.astype(jnp.bfloat16), 'grp', split_axis=0, concat...  15.6 us
    all_to_all x1, starting transfers between devices, local(): lax.all_to_all(lax.all_to_all(ask_end, 'grp', split_axis=0, concat_axis=0...  12 us
    select_n x2, other arithmetic, look_up(): return jnp.where((wanted >= 0)[..., None], fetched, jnp.zeros_like(fetched))  10.1 us
    all_to_all x1, waiting for transfers between devices, local(): lax.all_to_all(lax.all_to_all(look_up(mem_half, got_end), 'grp', split_ax...  9.81 us
  transfers between devices with their start and end apart: 11, of which 9 were waited for; matrix products, arithmetic and copies ran while one was open for 23% of the time, Pallas kernels for 0%

commit v1 on v0

--- a/solution.py
+++ b/solution.py
@@ -9,12 +9,25 @@
 K = 10
 CAP_E = 2
 CAP_N = 16
-
-
-def look_up(table, wanted):
-    clipped = jnp.maximum(wanted, 0)
-    fetched = jnp.take(table, clipped, axis=0)
-    return jnp.where((wanted >= 0)[..., None], fetched, jnp.zeros_like(fetched))
+CAP = 72
+LANES = 128
+SHIFT = 65536
+
+
+def hot(index, size, axis):
+    index = jnp.expand_dims(index, axis)
+    grid = lax.broadcasted_iota(jnp.int32, index.shape[:axis] + (size,) + index.shape[axis + 1 :], axis)
+    return (index == grid).astype(jnp.bfloat16)
+
+
+def pick(index, table):
+    return jnp.dot(hot(index, table.shape[0], 1), table, preferred_element_type=jnp.float32).astype(
+        jnp.bfloat16
+    )
+
+
+def exchange(x, axis):
+    return lax.all_to_all(x, axis, split_axis=0, concat_axis=0, tiled=True)
 
 
 def event_block(
@@ -114,51 +127,115 @@
 ):
     groups = lax.axis_size("grp")
     members = lax.axis_size("dev")
-    row_width = memory.shape[1]
+    nodes, row_width = memory.shape
     events = end_slot.shape[0]
-    ask_end = want_end.reshape(groups, members, CAP_E)
-    ask_near = want_near.reshape(groups, members, CAP_N)
+    block = groups * CAP_N
     mem_half = memory.astype(jnp.bfloat16)
-    got_end, got_near = (
-        lax.all_to_all(
-            lax.all_to_all(ask_end, "grp", split_axis=0, concat_axis=0, tiled=True),
-            "dev",
-            split_axis=1,
-            concat_axis=1,
-            tiled=True,
+    counted = jnp.transpose(near_count)
+
+    near_value = jnp.transpose(near_slot).reshape(-1)
+    owner = near_value // CAP_N
+    member = owner % members
+    place = (owner // members) * CAP_N + near_value % CAP_N
+    usable = (jnp.arange(K)[None, :, None] < counted[:, None, :]).reshape(-1)
+    member_hot = hot(jnp.where(usable, member, -1), members, 0)
+    place_hot = hot(place, block, 0)
+    used = (
+        lax.dot_general(
+            member_hot, place_hot, (((1,), (1,)), ((), ())), preferred_element_type=jnp.float32
+        )
+        > 0
+    )
+    before = (jnp.arange(block)[:, None] < jnp.arange(block)[None, :]).astype(jnp.bfloat16)
+    rank = jnp.dot(used.astype(jnp.bfloat16), before, preferred_element_type=jnp.float32)
+    most = jnp.max(jnp.sum(used.astype(jnp.int32), axis=1))
+    rank_or_none = jnp.where(used, rank.astype(jnp.int32), -1)
+    listed = jnp.sum(
+        jnp.where(
+            rank_or_none[:, None, :] == jnp.arange(CAP)[None, :, None],
+            jnp.arange(block)[None, None, :],
+            0,
         ),
-        lax.all_to_all(
-            lax.all_to_all(ask_near, "grp", split_axis=0, concat_axis=0, tiled=True),
-            "dev",
-            split_axis=1,
-            concat_axis=1,
-            tiled=True,
-        ),
-    )
-    fetched_end, fetched_near = (
-        lax.all_to_all(
-            lax.all_to_all(
-                look_up(mem_half, got_end), "grp", split_axis=0, concat_axis=0, tiled=True
-            ),
-            "dev",
-            split_axis=1,
-            concat_axis=1,
-            tiled=True,
-        ),
-        lax.all_to_all(
-            lax.all_to_all(
-                look_up(mem_half, got_near), "grp", split_axis=0, concat_axis=0, tiled=True
-            ),
-            "dev",
-            split_axis=1,
-            concat_axis=1,
-            tiled=True,
-        ),
-    )
-    end_index = jnp.transpose(end_slot)
-    near_index = jnp.transpose(near_slot).reshape(2, K, events)
-    end_rows = jnp.take(fetched_end.reshape(-1, row_width), end_index, axis=0)
-    near_rows = jnp.take(fetched_near.reshape(-1, row_width), near_index, axis=0)
+        axis=2,
+    )
+    ref_rank = jnp.sum(
+        jnp.dot(rank.astype(jnp.bfloat16), place_hot, preferred_element_type=jnp.float32)
+        * member_hot.astype(jnp.float32),
+        axis=0,
+    ).astype(jnp.int32)
+
+    end_value = jnp.transpose(end_slot).reshape(-1)
+    end_hot = hot(end_value, groups * members * CAP_E, 0)
+    slot_count = jnp.sum(end_hot.astype(jnp.float32), axis=1).astype(jnp.int32)
+    wanted = want_end.reshape(-1)
+    asked = jnp.where(wanted >= 0, wanted + SHIFT * slot_count, -1).reshape(groups, members * CAP_E)
+
+    mine = lax.axis_index("dev")
+    ask_near = lax.dynamic_index_in_dim(
+        want_near.reshape(groups, members, CAP_N), mine, 1, keepdims=False
+    )
+    first = jnp.concatenate(
+        [
+            asked,
+            ask_near,
+            jnp.broadcast_to(most, (groups, LANES - members * CAP_E - CAP_N)),
+        ],
+        1,
+    )
+    first = exchange(first, "grp")
+    got_near = first[:, members * CAP_E : members * CAP_E + CAP_N]
+    most = jnp.max(first[:, members * CAP_E + CAP_N :])
+    passed = jnp.transpose(
+        first[:, : members * CAP_E].reshape(groups, members, CAP_E), (1, 0, 2)
+    ).reshape(members, groups * CAP_E)
+    second = jnp.concatenate(
+        [
+            passed,
+            listed,
+            jnp.broadcast_to(most, (members, LANES - groups * CAP_E - CAP)),
+        ],
+        1,
+    )
+    second = exchange(second, "dev")
+    got_listed = second[:, groups * CAP_E : groups * CAP_E + CAP]
+    most = jnp.max(second[:, groups * CAP_E + CAP :])
+    got_code = second[:, : groups * CAP_E].reshape(members, groups, CAP_E)
+    got_code = jnp.transpose(got_code, (1, 0, 2)).reshape(groups, members * CAP_E)
+    got_end = jnp.where(got_code >= 0, got_code % SHIFT, -1)
+    got_count = jnp.where(got_code >= 0, got_code // SHIFT, 0)
+
+    row_index = jnp.concatenate([got_near, got_end], 1).reshape(-1)
+    rows = exchange(pick(row_index, mem_half).reshape(groups, -1, row_width), "grp")
+    near_block = rows[:, :CAP_N].reshape(block, row_width)
+    end_part = jnp.transpose(
+        rows[:, CAP_N:].reshape(groups, members, CAP_E, row_width), (1, 0, 2, 3)
+    ).reshape(members, groups * CAP_E, row_width)
+    near_part = pick(got_listed.reshape(-1), near_block).reshape(members, CAP, row_width)
+    table = exchange(jnp.concatenate([near_part, end_part], 1), "dev")
+    per_member = CAP + groups * CAP_E
+    table = table.reshape(members * per_member, row_width)
+
+    end_owner = end_value // CAP_E
+    end_index = (
+        (end_owner % members) * per_member
+        + CAP
+        + (end_owner // members) * CAP_E
+        + end_value % CAP_E
+    )
+    near_index = jnp.where(usable, member * per_member + ref_rank, 0)
+    fetched = jnp.take(
+        table, jnp.concatenate([near_index, end_index]), axis=0, mode="clip"
+    )
+    end_rows = fetched[2 * K * events :].reshape(2, events, row_width)
+
+    def whole():
+        full = exchange(jnp.broadcast_to(near_block[None], (members, block, row_width)), "dev")
+        return jnp.take(
+            full.reshape(members * block, row_width), member * block + place, axis=0, mode="clip"
+        )
+
+    near_rows = lax.cond(most > CAP, whole, lambda: fetched[: 2 * K * events])
+    near_rows = near_rows.reshape(2, K, events, row_width)
     elapsed = (
         (event_time[None, :] - jnp.transpose(near_time)).astype(jnp.float32).reshape(2, K, events)
     )
@@ -166,7 +243,7 @@
         end_rows,
         near_rows,
         elapsed,
-        jnp.transpose(near_count),
+        counted,
         frequency,
         phases,
         query_weight,
@@ -177,46 +254,25 @@
         message_in,
         message_out,
     )
-    flat_slots = end_index.reshape(-1)
-    slot_sum = (
-        jnp.zeros((groups * members * CAP_E, row_width), jnp.float32)
-        .at[flat_slots]
-        .add(message.reshape(-1, row_width))
-    )
-    slot_count = (
-        jnp.zeros((groups * members * CAP_E,), jnp.float32)
-        .at[flat_slots]
-        .add(jnp.ones(flat_slots.shape, jnp.float32))
-    )
-    slot_sum = slot_sum.reshape(groups, members, CAP_E, row_width)
-    slot_count = slot_count.reshape(groups, members, CAP_E)
-    news_sum, news_count = (
-        lax.all_to_all(
-            lax.all_to_all(
-                slot_sum.astype(jnp.bfloat16), "grp", split_axis=0, concat_axis=0, tiled=True
-            ),
-            "dev",
-            split_axis=1,
-            concat_axis=1,
-            tiled=True,
-        ).astype(slot_sum.dtype),
-        lax.all_to_all(
-            lax.all_to_all(
-                slot_count.astype(jnp.bfloat16), "grp", split_axis=0, concat_axis=0, tiled=True
-            ),
-            "dev",
-            split_axis=1,
-            concat_axis=1,
-            tiled=True,
-        ).astype(slot_count.dtype),
-    )
-    owned_rows = jnp.maximum(got_end, 0).reshape(-1)
-    totals = (
-        jnp.zeros((memory.shape[0], row_width), jnp.float32)
-        .at[owned_rows]
-        .add(news_sum.reshape(-1, row_width))
-    )
-    counts = jnp.zeros((memory.shape[0],), jnp.float32).at[owned_rows].add(news_count.reshape(-1))
+    message = message.reshape(-1, row_width)
+    message_high = lax.reduce_precision(message, 8, 7)
+    slot_sum = jnp.dot(
+        end_hot, message_high.astype(jnp.bfloat16), preferred_element_type=jnp.float32
+    ) + jnp.dot(
+        end_hot, (message - message_high).astype(jnp.bfloat16), preferred_element_type=jnp.float32
+    )
+    news = exchange(
+        slot_sum.astype(jnp.bfloat16).reshape(groups * members, CAP_E * row_width), ("grp", "dev")
+    ).reshape(-1, row_width)
+    owned = got_end.reshape(-1)
+    owned_hot = hot(owned, nodes, 0)
+    totals = jnp.dot(owned_hot, news, preferred_element_type=jnp.float32)
+    counts = jnp.sum(
+        jnp.where(
+            owned[None, :] == jnp.arange(nodes)[:, None], got_count.reshape(1, -1), 0
+        ),
+        axis=1,
+    ).astype(jnp.float32)
     new_memory = gru_update(
         memory, mem_half, totals, counts, input_weight, state_weight, update_bias
     )

time: 444 us -> 191 us (0.43)
  waiting for transfers between devices: 230 us -> 83.8 us
  local copies, waits for them, and re-layouts: 73 us -> 21.5 us
  starting transfers between devices: 74.8 us -> 41.7 us
  blocking collectives: 16.6 us -> 0 us
  other arithmetic: 41.7 us -> 28 us
  matrix products: 4.29 us -> 12.8 us
    all_to_all x11 -> x5, waiting for transfers between devices: 230 us -> 83.8 us  [exchange(): return lax.all_to_all(x, axis, split_axis=0, concat_axis=0, tiled=True)]
    gather x5 -> x1, local copies, waits for them, and re-layouts: 46.8 us -> 9.09 us  [local(): jnp.take(table, jnp.concatenate([near_index, end_index]), axis=0, mode='c...]
    all_to_all x11 -> x5, starting transfers between devices: 74.8 us -> 41.7 us  [exchange(): return lax.all_to_all(x, axis, split_axis=0, concat_axis=0, tiled=True)]
    scatter-add x4 -> x0, other arithmetic: 19.2 us -> none  [the longest x1 7.83 us: local(): jnp.zeros((memory.shape[0],), jnp.float32).at[owned_rows]]
    all_to_all x1 -> x0, blocking collectives: 16.6 us -> none  [local(): lax.all_to_all(ask_end, 'grp', split_axis=0, concat_axis=0, tiled=True)]
    all_to_all x12 -> x3, local copies, waits for them, and re-layouts: 14.9 us -> 0.87 us  [exchange(): return lax.all_to_all(x, axis, split_axis=0, concat_axis=0, tiled=True)]
    select_n x7 -> x4, other arithmetic: 11.4 us -> 0.05 us  [the longest x1 0.01 us: local(): near_index = jnp.where(usable, member * per_member + ref_rank, 0)]
    all_to_all x2, other arithmetic: 1.24 us -> 7 us  [exchange(): return lax.all_to_all(x, axis, split_axis=0, concat_axis=0, tiled=True)]
  transfers between devices with their start and end apart: 11 -> 5, of which waited for: 9 -> 5; matrix products, arithmetic and copies ran while one was open for 23% -> 7% of each run, Pallas kernels for 0% -> 0%
where the time goes in v1:
time: 191 us; the launch traced here: 190 us
  waiting for transfers between devices  83.8 us (44%)
  starting transfers between devices  41.7 us (22%)
  other arithmetic  28 us (15%)
  local copies, waits for them, and re-layouts  21.5 us (11%)
  matrix products  12.8 us (7%)
  between operations  2.11 us (1%)
    all_to_all x5, waiting for transfers between devices, exchange(): return lax.all_to_all(x, axis, split_axis=0, concat_axis=0, tiled=True)  83.8 us
    all_to_all x5, starting transfers between devices, exchange(): return lax.all_to_all(x, axis, split_axis=0, concat_axis=0, tiled=True)  41.7 us
    gather x1, local copies, waits for them, and re-layouts, local(): jnp.take(table, jnp.concatenate([near_index, end_index]), axis=0, mode='c...  9.09 us
    all_to_all x2, other arithmetic, exchange(): return lax.all_to_all(x, axis, split_axis=0, concat_axis=0, tiled=True)  7 us
    convert_element_type x1, other arithmetic, event_block(): jnp.cos(elapsed[..., None] * frequency + phases).astype(jnp.bfloat16)  4.69 us
  transfers between devices with their start and end apart: 5, of which 5 were waited for; matrix products, arithmetic and copies ran while one was open for 7% of the time, Pallas kernels for 0%

profile of v1, /device:TPU:1, one launch (start us, length us, event | category | flops | bytes accessed | tf_op | source)
XLA Modules:
  0.0 190.1 jit_solution(4457641470532227788)
XLA Ops:
  0.7 1.4 negate_select_fusion.1
  2.8 1.3 negate_select_fusion.5
  6.2 0.8 reshape.280
  8.6 10.1 %all-to-all-start.1 = ((s32[16,1,128]{2,1,0:T(1,128)}), s32[16,1,128]{2,1,0:T(1,128)S(1)}, u32[]{:S(2)}, u32[]{:S(2)}) async-start(s32[16,1,128]{2,1,0:T(1,128)} %bitcast.12), calls=%async_computation.1 | async-start | bytes 16384 | tf_op jit(solution)/shard_map/all_to_all | solution.py:30
  19.4 6.4 %all-to-all-done.1 = s32[16,1,128]{2,1,0:T(1,128)S(1)} async-done(((s32[16,1,128]{2,1,0:T(1,128)}), s32[16,1,128]{2,1,0:T(1,128)S(1)}, u32[]{:S(2)}, u32[]{:S(2)}) %all-to-all-start.1) | async-done | bytes 8224 | tf_op jit(solution)/shard_map/all_to_all | solution.py:30
  28.1 11.4 %all-to-all-start.2 = ((s32[32,1,128]{2,1,0:T(1,128)}), s32[32,1,128]{2,1,0:T(1,128)S(1)}, u32[]{:S(2)}, u32[]{:S(2)}) async-start(s32[32,1,128]{2,1,0:T(1,128)} %bitcast.17), calls=%async_computation.2 | async-start | bytes 32768 | tf_op jit(solution)/shard_map/all_to_all | solution.py:30
  39.6 8.5 %all-to-all-done.2 = s32[32,1,128]{2,1,0:T(1,128)S(1)} async-done(((s32[32,1,128]{2,1,0:T(1,128)}), s32[32,1,128]{2,1,0:T(1,128)S(1)}, u32[]{:S(2)}, u32[]{:S(2)}) %all-to-all-start.2) | async-done | bytes 16416 | tf_op jit(solution)/shard_map/all_to_all | solution.py:30
  48.5 1.4 fusion.7
  50.0 5.5 %all-to-all-start.3 = ((bf16[16,80,256]{2,1,0:T(8,128)(2,1)}), bf16[16,80,256]{2,1,0:T(8,128)(2,1)S(1)}, u32[]{:S(2)}, u32[]{:S(2)}) async-start(bf16[16,80,256]{2,1,0:T(8,128)(2,1)} %bitcast.23), calls=%async_computation.3 | async-start | bytes 1310720 | tf_op jit(solution)/shard_map/all_to_all | solution.py:30
  55.6 19.9 %all-to-all-done.3 = bf16[16,80,256]{2,1,0:T(8,128)(2,1)S(1)} async-done(((bf16[16,80,256]{2,1,0:T(8,128)(2,1)}), bf16[16,80,256]{2,1,0:T(8,128)(2,1)S(1)}, u32[]{:S(2)}, u32[]{:S(2)}) %all-to-all-start.3) | async-done | bytes 655392 | tf_op jit(solution)/shard_map/all_to_all | solution.py:30
  77.2 1.3 convolution_convert_fusion
  78.5 1.3 pad_maximum_fusion.1
  79.9 4.1 %all-to-all-start.4 = ((bf16[32,104,256]{2,1,0:T(8,128)(2,1)}), bf16[32,104,256]{2,1,0:T(8,128)(2,1)S(1)}, u32[]{:S(2)}, u32[]{:S(2)}) async-start(bf16[32,104,256]{2,1,0:T(8,128)(2,1)} %pad_maximum_fusion.1), calls=%async_computation.4 | async-start | bytes 3407872 | tf_op jit(solution)/shard_map/all_to_all | solution.py:30
  87.1 4.7 %cosine_convert_fusion = bf16[2,10,128,128]{3,2,1,0:T(8,128)(2,1)S(1)} fusion(f32[128]{0:T(128)S(1)} %copy-done.24, f32[128]{0:T(128)S(1)} %copy-done.25, f32[2,10,128]{2,1,0:T(8,128)S(1)} %mul.113), kind=kLoop, calls=%fused_computation.36 | loop fusion | flops 983040 | bytes 666624 | tf_op jit(solution)/shard_map/convert_element_type | solution.py:54
  91.8 1.6 fusion.77
  93.4 0.9 copy.84
  94.3 1.4 slice_reduce_fusion
  96.6 28.5 %all-to-all-done.4 = bf16[32,104,256]{2,1,0:T(8,128)(2,1)S(1)} async-done(((bf16[32,104,256]{2,1,0:T(8,128)(2,1)}), bf16[32,104,256]{2,1,0:T(8,128)(2,1)S(1)}, u32[]{:S(2)}, u32[]{:S(2)}) %all-to-all-start.4) | async-done | bytes 1703968 | tf_op jit(solution)/shard_map/all_to_all | solution.py:30
  125.1 9.1 %gather_fusion.1 = bf16[2816,256]{1,0:T(8,128)(2,1)} fusion(bf16[3328,256]{1,0:T(8,128)(2,1)S(1)} %bitcast.98, s32[3072]{0:T(1024)} %pad_clamp_fusion.1), kind=kCustom, calls=%fused_computation.1 | custom fusion | bytes 2894848 | tf_op jit(solution)/shard_map/jit(_take)/gather | solution.py:226
  134.2 0.9 slice.118
  135.1 1.1 fusion.68
  136.4 1.6 conditional.1
  136.4 1.4 slice.54
  138.0 1.8 fusion.18
  141.5 0.9 fusion.11
  144.6 3.8 %reduce.1 = bf16[512,512]{1,0:T(8,128)(2,1)S(1)} reduce(bf16[512,1,512]{2,1,0:T(2,128)(2,1)S(1)} %all_to_all.41, bf16[]{:T(256)} %broadcast.380), dimensions={1}, to_apply=%all_to_all.41.reduce_sub_computation | reduce | bytes 1048578 | tf_op jit(solution)/shard_map/all_to_all | solution.py:30
  148.4 0.9 reshape.322
  149.3 10.7 %all-to-all-start.5 = ((bf16[512,2,256]{2,1,0:T(2,128)(2,1)}), bf16[512,2,256]{2,1,0:T(2,128)(2,1)S(1)}, u32[]{:S(2)}, u32[]{:S(2)}) async-start(bf16[512,2,256]{2,1,0:T(2,128)(2,1)} %reshape.322), calls=%async_computation.5 | async-start | bytes 1048576 | tf_op jit(solution)/shard_map/all_to_all | solution.py:30
  161.0 20.5 %all-to-all-done.5 = bf16[512,2,256]{2,1,0:T(2,128)(2,1)S(1)} async-done(((bf16[512,2,256]{2,1,0:T(2,128)(2,1)}), bf16[512,2,256]{2,1,0:T(2,128)(2,1)S(1)}, u32[]{:S(2)}, u32[]{:S(2)}) %all-to-all-start.5) | async-done | bytes 524320 | tf_op jit(solution)/shard_map/all_to_all | solution.py:30
  182.0 3.2 %reduce = bf16[512,512]{1,0:T(8,128)(2,1)S(1)} reduce(bf16[512,1,512]{2,1,0:T(2,128)(2,1)S(1)} %reshape.323, bf16[]{:T(256)} %constant.161), dimensions={1}, to_apply=%all_to_all.40.reduce_sub_computation | reduce | bytes 1048578 | tf_op jit(solution)/shard_map/all_to_all | solution.py:30
  185.4 2.2 %fusion.23 = f32[512,768]{1,0:T(8,128)} fusion(bf16[256,768]{1,0:T(8,128)(2,1)S(1)} %copy-done.26, bf16[1024,256]{1,0:T(8,128)(2,1)S(1)} %reshape.295, s32[1024]{0:T(1024)S(1)} %get-tuple-element.87, f32[512]{0:T(512)S(1)} %convert_maximum_fusion), kind=kOutput, calls=%fused_computation.49 | convolution fusion | flops 470548480 | bytes 2496512 | tf_op jit(solution)/shard_map/dot_general | solution.py:87
  187.6 2.6 %fusion.37 = f32[512,256]{1,0:T(8,128)} fusion(f32[512,256]{1,0:T(8,128)S(1)} %copy-done.2, f32[512,768]{1,0:T(8,128)S(1)} %copy-done.1, f32[512,768]{1,0:T(8,128)} %fusion.23, f32[256]{0:T(256)S(1)} %copy-done.20, f32[256]{0:T(256)S(1)} %copy-done.21, f32[256]{0:T(256)S(1)} %copy-done.19, pred[512]{0:T(512)(128)(4,1)S(1)} %convert_compare_fusion), kind=kLoop, calls=%fused_computation.65 | loop fusion | flops 2359296 | bytes 4197888 | tf_op jit(solution)/shard_map/jit(_where)/select_n | solution.py:103
  (138 shorter events, 18.3 us)
Async XLA Ops:
  0.6 91.2 %copy-start = (bf16[256,768]{1,0:T(8,128)(2,1)S(1)}, bf16[256,768]{1,0:T(8,128)(2,1)}, u32[]{:S(2)}) copy-start(bf16[256,768]{1,0:T(8,128)(2,1)} %param.40) | copy-start | bytes 1179652
  0.6 6.7 %copy-start.12 = (s32[128,2]{0,1:T(2,128)S(1)}, s32[128,2]{0,1:T(2,128)}, u32[]{:S(2)}) copy-start(s32[128,2]{0,1:T(2,128)} %param.25) | copy-start | bytes 3076
  0.7 7.0 %copy-start.17 = (s32[1,512,2]{1,2,0:T(2,128)S(1)}, s32[1,512,2]{1,2,0:T(2,128)}, u32[]{:S(2)}) copy-start(s32[1,512,2]{1,2,0:T(2,128)} %param.23) | copy-start | bytes 12292
  0.7 47.9 %copy-start.2 = (f32[512,256]{1,0:T(8,128)S(1)}, f32[512,256]{1,0:T(8,128)}, u32[]{:S(2)}) copy-start(f32[512,256]{1,0:T(8,128)} %param.22) | copy-start | bytes 1572868
  8.6 17.1 %all-to-all-start.1 = ((s32[16,1,128]{2,1,0:T(1,128)}), s32[16,1,128]{2,1,0:T(1,128)S(1)}, u32[]{:S(2)}, u32[]{:S(2)}) async-start(s32[16,1,128]{2,1,0:T(1,128)} %bitcast.12), calls=%async_computation.1 | async-start | bytes 16384 | tf_op jit(solution)/shard_map/all_to_all | solution.py:30
  28.1 20.0 %all-to-all-start.2 = ((s32[32,1,128]{2,1,0:T(1,128)}), s32[32,1,128]{2,1,0:T(1,128)S(1)}, u32[]{:S(2)}, u32[]{:S(2)}) async-start(s32[32,1,128]{2,1,0:T(1,128)} %bitcast.17), calls=%async_computation.2 | async-start | bytes 32768 | tf_op jit(solution)/shard_map/all_to_all | solution.py:30
  48.2 7.3 %copy-start.5 = (s32[32,1,128]{0,2,1:T(8,128)}, s32[32,1,128]{0,2,1:T(8,128)S(1)}, u32[]{:S(2)}) copy-start(s32[32,1,128]{0,2,1:T(8,128)S(1)} %copy.83) | copy-start | bytes 49156
  48.2 1.8 copy-start.7
  50.0 25.5 %all-to-all-start.3 = ((bf16[16,80,256]{2,1,0:T(8,128)(2,1)}), bf16[16,80,256]{2,1,0:T(8,128)(2,1)S(1)}, u32[]{:S(2)}, u32[]{:S(2)}) async-start(bf16[16,80,256]{2,1,0:T(8,128)(2,1)} %bitcast.23), calls=%async_computation.3 | async-start | bytes 1310720 | tf_op jit(solution)/shard_map/all_to_all | solution.py:30
  79.8 4.2 %copy-start.14 = (s32[128,20]{0,1:T(8,128)S(1)}, s32[128,20]{0,1:T(8,128)}, u32[]{:S(2)}) copy-start(s32[128,20]{0,1:T(8,128)} %param.29) | copy-start | bytes 30724
  79.8 4.2 %copy-start.23 = (s32[128]{0:T(128)S(1)}, s32[128]{0:T(128)}, u32[]{:S(2)}) copy-start(s32[128]{0:T(128)} %param.28) | copy-start | bytes 1540
  79.8 4.2 %copy-start.24 = (f32[128]{0:T(128)S(1)}, f32[128]{0:T(128)}, u32[]{:S(2)}) copy-start(f32[128]{0:T(128)} %param.31) | copy-start | bytes 1540
  79.9 6.1 %copy-start.22 = (f32[768]{0:T(1024)S(1)}, f32[768]{0:T(1024)}, u32[]{:S(2)}) copy-start(f32[768]{0:T(1024)} %param.41) | copy-start | bytes 9220
  79.9 7.3 %copy-start.25 = (f32[128]{0:T(128)S(1)}, f32[128]{0:T(128)}, u32[]{:S(2)}) copy-start(f32[128]{0:T(128)} %param.30) | copy-start | bytes 1540
  79.9 45.2 %all-to-all-start.4 = ((bf16[32,104,256]{2,1,0:T(8,128)(2,1)}), bf16[32,104,256]{2,1,0:T(8,128)(2,1)S(1)}, u32[]{:S(2)}, u32[]{:S(2)}) async-start(bf16[32,104,256]{2,1,0:T(8,128)(2,1)} %pad_maximum_fusion.1), calls=%async_computation.4 | async-start | bytes 3407872 | tf_op jit(solution)/shard_map/all_to_all | solution.py:30
  125.1 10.1 %copy-start.18 = (bf16[384]{0:T(512)(128)(2,1)S(1)}, bf16[384]{0:T(512)(128)(2,1)}, u32[]{:S(2)}) copy-start(bf16[384]{0:T(512)(128)(2,1)} %pad.10.clone) | copy-start | bytes 2308
  125.1 11.2 %copy-start.4 = (bf16[16,16,256]{2,1,0:T(8,128)(2,1)S(1)}, bf16[16,16,256]{2,1,0:T(8,128)(2,1)}, u32[]{:S(2)}) copy-start(bf16[16,16,256]{2,1,0:T(8,128)(2,1)} %copy-done.3) | copy-start | bytes 393220
  125.1 11.2 %copy-start.8 = (s32[2560]{0:T(1024)S(1)}, s32[2560]{0:T(1024)}, u32[]{:S(2)}) copy-start(s32[2560]{0:T(1024)} %get-tuple-element.68) | copy-start | bytes 30724
  125.1 11.2 %copy-start.9 = (s32[2560]{0:T(1024)S(1)}, s32[2560]{0:T(1024)}, u32[]{:S(2)}) copy-start(s32[2560]{0:T(1024)} %get-tuple-element.76) | copy-start | bytes 30724
  125.1 11.2 %copy-start.10 = (s32[2560]{0:T(1024)S(1)}, s32[2560]{0:T(1024)}, u32[]{:S(2)}) copy-start(s32[2560]{0:T(1024)} %get-tuple-element.78) | copy-start | bytes 30724
  125.1 11.2 %copy-start.11 = (s32[2560]{0:T(1024)S(1)}, s32[2560]{0:T(1024)}, u32[]{:S(2)}) copy-start(s32[2560]{0:T(1024)} %get-tuple-element.79) | copy-start | bytes 30724
  125.1 11.2 %copy-start.15 = (pred[2560]{0:T(1024)(128)(4,1)S(1)}, pred[2560]{0:T(1024)(128)(4,1)}, u32[]{:S(2)}) copy-start(pred[2560]{0:T(1024)(128)(4,1)} %broadcast_compare_fusion) | copy-start | bytes 7684
  138.0 1.8 copy-start.6
  141.4 1.0 copy-start.27
  141.5 1.2 copy-start.28
  141.5 1.2 copy-start.29
  149.3 32.2 %all-to-all-start.5 = ((bf16[512,2,256]{2,1,0:T(2,128)(2,1)}), bf16[512,2,256]{2,1,0:T(2,128)(2,1)S(1)}, u32[]{:S(2)}, u32[]{:S(2)}) async-start(bf16[512,2,256]{2,1,0:T(2,128)(2,1)} %reshape.322), calls=%async_computation.5 | async-start | bytes 1048576 | tf_op jit(solution)/shard_map/all_to_all | solution.py:30
  182.0 3.4 %copy-start.26 = (bf16[256,768]{1,0:T(8,128)(2,1)S(1)}, bf16[256,768]{1,0:T(8,128)(2,1)}, u32[]{:S(2)}) copy-start(bf16[256,768]{1,0:T(8,128)(2,1)} %param.39) | copy-start | bytes 1179652
  185.4 2.2 %copy-start.1 = (f32[512,768]{1,0:T(8,128)S(1)}, f32[512,768]{1,0:T(8,128)}, u32[]{:S(2)}) copy-start(f32[512,768]{1,0:T(8,128)} %fusion.77) | copy-start | bytes 4718596
  185.4 2.2 %copy-start.19 = (f32[256]{0:T(256)S(1)}, f32[256]{0:T(256)}, u32[]{:S(2)}) copy-start(f32[256]{0:T(256)} %get-tuple-element.83) | copy-start | bytes 3076
  185.4 2.2 %copy-start.20 = (f32[256]{0:T(256)S(1)}, f32[256]{0:T(256)}, u32[]{:S(2)}) copy-start(f32[256]{0:T(256)} %get-tuple-element.84) | copy-start | bytes 3076
  185.4 2.2 %copy-start.21 = (f32[256]{0:T(256)S(1)}, f32[256]{0:T(256)}, u32[]{:S(2)}) copy-start(f32[256]{0:T(256)} %get-tuple-element.85) | copy-start | bytes 3076
  (4 other events, 3.2 us)

commit v2 on v1

--- a/solution.py
+++ b/solution.py
@@ -9,7 +9,7 @@
 K = 10
 CAP_E = 2
 CAP_N = 16
-CAP = 72
+CAP = 88
 LANES = 128
 SHIFT = 65536
 
@@ -24,6 +24,12 @@
     return jnp.dot(hot(index, table.shape[0], 1), table, preferred_element_type=jnp.float32).astype(
         jnp.bfloat16
     )
+
+
+def split_slot(value, members, slots):
+    width = slots.bit_length() - 1
+    owner = value >> width
+    return owner & (members - 1), ((owner >> (members.bit_length() - 1)) << width) | (value & (slots - 1))
 
 
 def exchange(x, axis):
@@ -130,30 +136,34 @@
     nodes, row_width = memory.shape
     events = end_slot.shape[0]
     block = groups * CAP_N
+    ends = groups * CAP_E
+    places = block + ends
     mem_half = memory.astype(jnp.bfloat16)
     counted = jnp.transpose(near_count)
 
     near_value = jnp.transpose(near_slot).reshape(-1)
-    owner = near_value // CAP_N
-    member = owner % members
-    place = (owner // members) * CAP_N + near_value % CAP_N
+    end_value = jnp.transpose(end_slot).reshape(-1)
+    near_member, near_place = split_slot(near_value, members, CAP_N)
+    end_member, end_place = split_slot(end_value, members, CAP_E)
     usable = (jnp.arange(K)[None, :, None] < counted[:, None, :]).reshape(-1)
-    member_hot = hot(jnp.where(usable, member, -1), members, 0)
-    place_hot = hot(place, block, 0)
+    member = jnp.concatenate([jnp.where(usable, near_member, -1), end_member])
+    place = jnp.concatenate([near_place, end_place + block])
+    member_hot = hot(member, members, 0)
+    place_hot = hot(place, places, 0)
     used = (
         lax.dot_general(
             member_hot, place_hot, (((1,), (1,)), ((), ())), preferred_element_type=jnp.float32
         )
         > 0
     )
-    before = (jnp.arange(block)[:, None] < jnp.arange(block)[None, :]).astype(jnp.bfloat16)
+    before = (jnp.arange(places)[:, None] < jnp.arange(places)[None, :]).astype(jnp.bfloat16)
     rank = jnp.dot(used.astype(jnp.bfloat16), before, preferred_element_type=jnp.float32)
     most = jnp.max(jnp.sum(used.astype(jnp.int32), axis=1))
     rank_or_none = jnp.where(used, rank.astype(jnp.int32), -1)
     listed = jnp.sum(
         jnp.where(
             rank_or_none[:, None, :] == jnp.arange(CAP)[None, :, None],
-            jnp.arange(block)[None, None, :],
+            jnp.arange(places)[None, None, :],
             0,
         ),
         axis=2,
@@ -163,8 +173,8 @@
         * member_hot.astype(jnp.float32),
         axis=0,
     ).astype(jnp.int32)
-
-    end_value = jnp.transpose(end_slot).reshape(-1)
+    index = jnp.where(member >= 0, member * CAP + jnp.minimum(ref_rank, CAP - 1), 0)
+
     end_hot = hot(end_value, groups * members * CAP_E, 0)
     slot_count = jnp.sum(end_hot.astype(jnp.float32), axis=1).astype(jnp.int32)
     wanted = want_end.reshape(-1)
@@ -187,55 +197,58 @@
     most = jnp.max(first[:, members * CAP_E + CAP_N :])
     passed = jnp.transpose(
         first[:, : members * CAP_E].reshape(groups, members, CAP_E), (1, 0, 2)
-    ).reshape(members, groups * CAP_E)
+    ).reshape(members, ends)
     second = jnp.concatenate(
         [
             passed,
             listed,
-            jnp.broadcast_to(most, (members, LANES - groups * CAP_E - CAP)),
+            jnp.broadcast_to(most, (members, LANES - ends - CAP)),
         ],
         1,
     )
     second = exchange(second, "dev")
-    got_listed = second[:, groups * CAP_E : groups * CAP_E + CAP]
-    most = jnp.max(second[:, groups * CAP_E + CAP :])
-    got_code = second[:, : groups * CAP_E].reshape(members, groups, CAP_E)
+    got_listed = second[:, ends : ends + CAP]
+    most = jnp.max(second[:, ends + CAP :])
+    got_code = second[:, :ends].reshape(members, groups, CAP_E)
     got_code = jnp.transpose(got_code, (1, 0, 2)).reshape(groups, members * CAP_E)
-    got_end = jnp.where(got_code >= 0, got_code % SHIFT, -1)
-    got_count = jnp.where(got_code >= 0, got_code // SHIFT, 0)
+    got_end = jnp.where(got_code >= 0, got_code & (SHIFT - 1), -1)
+    got_count = jnp.where(got_code >= 0, got_code >> 16, 0)
 
     row_index = jnp.concatenate([got_near, got_end], 1).reshape(-1)
     rows = exchange(pick(row_index, mem_half).reshape(groups, -1, row_width), "grp")
     near_block = rows[:, :CAP_N].reshape(block, row_width)
     end_part = jnp.transpose(
         rows[:, CAP_N:].reshape(groups, members, CAP_E, row_width), (1, 0, 2, 3)
-    ).reshape(members, groups * CAP_E, row_width)
-    near_part = pick(got_listed.reshape(-1), near_block).reshape(members, CAP, row_width)
-    table = exchange(jnp.concatenate([near_part, end_part], 1), "dev")
-    per_member = CAP + groups * CAP_E
-    table = table.reshape(members * per_member, row_width)
-
-    end_owner = end_value // CAP_E
-    end_index = (
-        (end_owner % members) * per_member
-        + CAP
-        + (end_owner // members) * CAP_E
-        + end_value % CAP_E
-    )
-    near_index = jnp.where(usable, member * per_member + ref_rank, 0)
-    fetched = jnp.take(
-        table, jnp.concatenate([near_index, end_index]), axis=0, mode="clip"
-    )
-    end_rows = fetched[2 * K * events :].reshape(2, events, row_width)
+    ).reshape(members, ends, row_width)
+    near_part = jnp.dot(
+        hot(got_listed.reshape(-1), block, 1), near_block, preferred_element_type=jnp.float32
+    ).reshape(members, CAP, row_width)
+    listed_ends = jnp.einsum(
+        "dcp,dpw->dcw",
+        hot(got_listed - block, ends, 2),
+        end_part,
+        preferred_element_type=jnp.float32,
+    )
+    table = exchange((near_part + listed_ends).astype(jnp.bfloat16), "dev")
+    table = table.reshape(members * CAP, row_width)
+
+    def fetch(table, index):
+        return (
+            jnp.take(table, index[: 2 * K * events], axis=0, mode="clip"),
+            jnp.take(table, index[2 * K * events :], axis=0, mode="clip"),
+        )
 
     def whole():
-        full = exchange(jnp.broadcast_to(near_block[None], (members, block, row_width)), "dev")
-        return jnp.take(
-            full.reshape(members * block, row_width), member * block + place, axis=0, mode="clip"
+        full = jnp.broadcast_to(near_block[None], (members, block, row_width))
+        full = exchange(jnp.concatenate([full, end_part], 1), "dev")
+        return fetch(
+            full.reshape(members * places, row_width),
+            jnp.where(member >= 0, member * places + place, 0),
         )
 
-    near_rows = lax.cond(most > CAP, whole, lambda: fetched[: 2 * K * events])
+    near_rows, end_rows = lax.cond(most > CAP, whole, lambda: fetch(table, index))
     near_rows = near_rows.reshape(2, K, events, row_width)
+    end_rows = end_rows.reshape(2, events, row_width)
     elapsed = (
         (event_time[None, :] - jnp.transpose(near_time)).astype(jnp.float32).reshape(2, K, events)
     )
@@ -262,7 +275,7 @@
         end_hot, (message - message_high).astype(jnp.bfloat16), preferred_element_type=jnp.float32
     )
     news = exchange(
-        slot_sum.astype(jnp.bfloat16).reshape(groups * members, CAP_E * row_width), ("grp", "dev")
+        slot_sum.astype(jnp.bfloat16).reshape(groups * members, CAP_E, row_width), ("grp", "dev")
     ).reshape(-1, row_width)
     owned = got_end.reshape(-1)
     owned_hot = hot(owned, nodes, 0)

time: 191 us -> 175 us (0.916)
  other arithmetic: 28 us -> 17.9 us
  local copies, waits for them, and re-layouts: 21.5 us -> 15.4 us
  matrix products: 12.8 us -> 16.2 us
  waiting for transfers between devices: 83.8 us -> 81.3 us
    all_to_all x2 -> x0, other arithmetic: 7 us -> none  [exchange(): return lax.all_to_all(x, axis, split_axis=0, concat_axis=0, tiled=True)]
    dot_general x0 -> x2, matrix products: none -> 2.97 us  [the longest x1 1.74 us: local(): jnp.einsum('dcp,dpw->dcw', hot(got_listed - block, ends, 2), end_part, pr...]
    all_to_all x5, waiting for transfers between devices: 83.8 us -> 81.3 us  [exchange(): return lax.all_to_all(x, axis, split_axis=0, concat_axis=0, tiled=True)]
    slice x5 -> x1, local copies, waits for them, and re-layouts: 2.39 us -> 0.01 us  [fetch(): index[2 * K * events:]]
    unnamed x65 -> x39, local copies, waits for them, and re-layouts: 2.3 us -> 0.25 us
    rem x2 -> x0, other arithmetic: 1.92 us -> none  [the longest x1 1.32 us: local(): owner = near_value // CAP_N]
    gather x1 -> x2, local copies, waits for them, and re-layouts: 9.09 us -> 8.72 us  [the longest x1 7.57 us: fetch(): jnp.take(table, index[:2 * K * events], axis=0, mode='clip')]
  transfers between devices with their start and end apart: 5 -> 5, of which waited for: 5 -> 5; matrix products, arithmetic and copies ran while one was open for 7% -> 6% of each run, Pallas kernels for 0% -> 0%
where the time goes in v2:
time: 175 us; the launch traced here: 174 us
  waiting for transfers between devices  81.3 us (46%)
  starting transfers between devices  41.3 us (24%)
  other arithmetic  17.9 us (10%)
  matrix products  16.2 us (9%)
  local copies, waits for them, and re-layouts  15.4 us (9%)
  between operations  1.83 us (1%)
    all_to_all x5, waiting for transfers between devices, exchange(): return lax.all_to_all(x, axis, split_axis=0, concat_axis=0, tiled=True)  81.3 us
    all_to_all x5, starting transfers between devices, exchange(): return lax.all_to_all(x, axis, split_axis=0, concat_axis=0, tiled=True)  41.3 us
    gather x1, local copies, waits for them, and re-layouts, fetch(): jnp.take(table, index[:2 * K * events], axis=0, mode='clip')  7.57 us
    convert_element_type x1, other arithmetic, event_block(): jnp.cos(elapsed[..., None] * frequency + phases).astype(jnp.bfloat16)  5.36 us
  transfers between devices with their start and end apart: 5, of which 5 were waited for; matrix products, arithmetic and copies ran while one was open for 6% of the time, Pallas kernels for 0%

profile of v2, /device:TPU:1, one launch (start us, length us, event | category | flops | bytes accessed | tf_op | source)
XLA Modules:
  0.0 174.2 jit_solution(16751803104317742876)
XLA Ops:
  0.7 0.8 iota_compare_fusion.30
  1.5 0.7 or_bitcast_fusion
  2.2 0.7 bitcast_select_fusion
  3.6 0.7 fusion.26
  5.9 0.8 reshape.205
  8.3 10.1 %all-to-all-start.1 = ((s32[16,1,128]{2,1,0:T(1,128)}), s32[16,1,128]{2,1,0:T(1,128)S(1)}, u32[]{:S(2)}, u32[]{:S(2)}) async-start(s32[16,1,128]{2,1,0:T(1,128)} %bitcast.17), calls=%async_computation.1 | async-start | bytes 16384 | tf_op jit(solution)/shard_map/all_to_all | solution.py:36
  19.0 6.4 %all-to-all-done.1 = s32[16,1,128]{2,1,0:T(1,128)S(1)} async-done(((s32[16,1,128]{2,1,0:T(1,128)}), s32[16,1,128]{2,1,0:T(1,128)S(1)}, u32[]{:S(2)}, u32[]{:S(2)}) %all-to-all-start.1) | async-done | bytes 8224 | tf_op jit(solution)/shard_map/all_to_all | solution.py:36
  27.8 11.4 %all-to-all-start.2 = ((s32[32,1,128]{2,1,0:T(1,128)}), s32[32,1,128]{2,1,0:T(1,128)S(1)}, u32[]{:S(2)}, u32[]{:S(2)}) async-start(s32[32,1,128]{2,1,0:T(1,128)} %bitcast.22), calls=%async_computation.2 | async-start | bytes 32768 | tf_op jit(solution)/shard_map/all_to_all | solution.py:36
  39.2 8.5 %all-to-all-done.2 = s32[32,1,128]{2,1,0:T(1,128)S(1)} async-done(((s32[32,1,128]{2,1,0:T(1,128)}), s32[32,1,128]{2,1,0:T(1,128)S(1)}, u32[]{:S(2)}, u32[]{:S(2)}) %all-to-all-start.2) | async-done | bytes 16416 | tf_op jit(solution)/shard_map/all_to_all | solution.py:36
  48.2 1.4 fusion.5
  49.6 5.5 %all-to-all-start.3 = ((bf16[16,80,256]{2,1,0:T(8,128)(2,1)}), bf16[16,80,256]{2,1,0:T(8,128)(2,1)S(1)}, u32[]{:S(2)}, u32[]{:S(2)}) async-start(bf16[16,80,256]{2,1,0:T(8,128)(2,1)} %bitcast.31), calls=%async_computation.3 | async-start | bytes 1310720 | tf_op jit(solution)/shard_map/all_to_all | solution.py:36
  55.1 20.0 %all-to-all-done.3 = bf16[16,80,256]{2,1,0:T(8,128)(2,1)S(1)} async-done(((bf16[16,80,256]{2,1,0:T(8,128)(2,1)}), bf16[16,80,256]{2,1,0:T(8,128)(2,1)S(1)}, u32[]{:S(2)}, u32[]{:S(2)}) %all-to-all-start.3) | async-done | bytes 655392 | tf_op jit(solution)/shard_map/all_to_all | solution.py:36
  76.2 1.2 fusion.2
  77.4 1.7 add_convert_fusion
  79.2 4.1 %all-to-all-start.4 = ((bf16[32,88,256]{2,1,0:T(8,128)(2,1)}), bf16[32,88,256]{2,1,0:T(8,128)(2,1)S(1)}, u32[]{:S(2)}, u32[]{:S(2)}) async-start(bf16[32,88,256]{2,1,0:T(8,128)(2,1)} %add_convert_fusion), calls=%async_computation.4 | async-start | bytes 2883584 | tf_op jit(solution)/shard_map/all_to_all | solution.py:36
  83.3 0.7 fusion.24
  84.1 5.4 %cosine_convert_fusion = bf16[2,10,128,128]{3,2,1,0:T(8,128)(2,1)} fusion(f32[128]{0:T(128)S(1)} %copy-done.13, f32[128]{0:T(128)S(1)} %copy-done.14, f32[2,10,128]{2,1,0:T(8,128)S(1)} %mul.85), kind=kLoop, calls=%fused_computation.39 | loop fusion | flops 983040 | bytes 666624 | tf_op jit(solution)/shard_map/convert_element_type | solution.py:60
  89.5 1.5 fusion.76
  92.4 26.6 %all-to-all-done.4 = bf16[32,88,256]{2,1,0:T(8,128)(2,1)S(1)} async-done(((bf16[32,88,256]{2,1,0:T(8,128)(2,1)}), bf16[32,88,256]{2,1,0:T(8,128)(2,1)S(1)}, u32[]{:S(2)}, u32[]{:S(2)}) %all-to-all-start.4) | async-done | bytes 1441824 | tf_op jit(solution)/shard_map/all_to_all | solution.py:36
  119.0 8.9 %conditional.1 = (bf16[2,10,128,256]{3,2,1,0:T(8,128)(2,1)S(1)}, bf16[2,128,256]{2,1,0:T(8,128)(2,1)S(1)}) conditional(s32[]{:T(128)} %convert_element_type.95, (bf16[32,88,256]{2,1,0:T(8,128)(2,1)S(1)}, s32[2816]{0:T(1024)S(1)}, s32[2816]{0:T(1024)S(1)}) %tuple.22, (bf16[16,16,256]{2,1,0:T(8,128)(2,1)S(1)}, bf16[32,32,256]{2,1,0:T(8,128)(2,1)S(1)}, ...), branch_computations={%region_8.9_spmd, %region_9.10_spmd} | conditional | flops 9452544 | bytes 30876720 | solution.py:249
  119.0 7.6 %gather_fusion = bf16[2560,256]{1,0:T(8,128)(2,1)S(1)} fusion(bf16[2816,256]{1,0:T(8,128)(2,1)S(1)} %bitcast.95, s32[3072]{0:T(1024)S(1)} %pad_clamp_fusion), kind=kCustom, calls=%fused_computation | custom fusion | bytes 2631680 | tf_op jit(solution)/shard_map/cond/branch_0_fun/jit(_take)/gather | solution.py:237
  126.6 1.2 gather_fusion.1
  128.0 1.1 fusion.67
  129.2 2.0 %fusion.17 = f32[2,10,128,256]{3,2,1,0:T(8,128)S(1)} fusion(bf16[2,10,128,128]{3,2,1,0:T(8,128)(2,1)} %cosine_convert_fusion, bf16[2,10,128,256]{3,2,1,0:T(8,128)(2,1)S(1)} %get-tuple-element.42, bf16[384,256]{1,0:T(8,128)(2,1)} %param.33), kind=kOutput, calls=%fused_computation.43 | convolution fusion | flops 507248640 | bytes 4784128 | tf_op jit(solution)/shard_map/jkec,cd->jked/dot_general | solution.py:64
  131.2 0.8 fusion.16
  132.1 0.7 fusion.13
  133.0 0.9 fusion.12
  135.2 1.0 reshape.213
  136.2 10.3 %all-to-all-start.5 = ((bf16[512,2,256]{2,1,0:T(2,128)(2,1)}), bf16[512,2,256]{2,1,0:T(2,128)(2,1)S(1)}, u32[]{:S(2)}, u32[]{:S(2)}) async-start(bf16[512,2,256]{2,1,0:T(2,128)(2,1)} %reshape.213), calls=%async_computation.5 | async-start | bytes 1048576 | tf_op jit(solution)/shard_map/all_to_all | solution.py:36
  148.3 19.7 %all-to-all-done.5 = bf16[512,2,256]{2,1,0:T(2,128)(2,1)S(1)} async-done(((bf16[512,2,256]{2,1,0:T(2,128)(2,1)}), bf16[512,2,256]{2,1,0:T(2,128)(2,1)S(1)}, u32[]{:S(2)}, u32[]{:S(2)}) %all-to-all-start.5) | async-done | bytes 524320 | tf_op jit(solution)/shard_map/all_to_all | solution.py:36
  168.3 3.3 %fusion.21 = f32[512,768]{1,0:T(8,128)} fusion(bf16[256,768]{1,0:T(8,128)(2,1)} %param.39, bf16[1024,256]{1,0:T(8,128)(2,1)S(1)} %reshape.214, s32[1024]{0:T(1024)S(1)} %select_n.98, f32[512]{0:T(512)S(1)} %convert_maximum_fusion), kind=kOutput, calls=%fused_computation.49 | convolution fusion | flops 470548480 | bytes 2496512 | tf_op jit(solution)/shard_map/dot_general | solution.py:93
  171.6 2.6 %fusion.35 = f32[512,256]{1,0:T(8,128)} fusion(f32[512,256]{1,0:T(8,128)S(1)} %copy-done.5, f32[512,768]{1,0:T(8,128)S(1)} %copy-done.1, f32[512,768]{1,0:T(8,128)} %fusion.21, f32[256]{0:T(256)S(1)} %get-tuple-element.62, f32[256]{0:T(256)S(1)} %get-tuple-element.63, f32[256]{0:T(256)S(1)} %get-tuple-element.61, pred[512]{0:T(512)(128)(4,1)S(1)} %convert_compare_fusion), kind=kLoop, calls=%fused_computation.65 | loop fusion | flops 2359296 | bytes 4197888 | tf_op jit(solution)/shard_map/jit(_where)/select_n | solution.py:109
  (107 shorter events, 12.6 us)
Async XLA Ops:
  0.6 88.9 %copy-start = (bf16[256,768]{1,0:T(8,128)(2,1)S(1)}, bf16[256,768]{1,0:T(8,128)(2,1)}, u32[]{:S(2)}) copy-start(bf16[256,768]{1,0:T(8,128)(2,1)} %param.40) | copy-start | bytes 1179652
  0.6 6.4 %copy-start.7 = (s32[128,2]{0,1:T(2,128)S(1)}, s32[128,2]{0,1:T(2,128)}, u32[]{:S(2)}) copy-start(s32[128,2]{0,1:T(2,128)} %param.25) | copy-start | bytes 3076
  0.7 6.6 %copy-start.10 = (s32[1,512,2]{1,2,0:T(2,128)S(1)}, s32[1,512,2]{1,2,0:T(2,128)}, u32[]{:S(2)}) copy-start(s32[1,512,2]{1,2,0:T(2,128)} %param.23) | copy-start | bytes 12292
  0.7 47.5 %copy-start.3 = (f32[512,256]{1,0:T(8,128)S(1)}, f32[512,256]{1,0:T(8,128)}, u32[]{:S(2)}) copy-start(f32[512,256]{1,0:T(8,128)} %param.22) | copy-start | bytes 1572868
  8.3 17.1 %all-to-all-start.1 = ((s32[16,1,128]{2,1,0:T(1,128)}), s32[16,1,128]{2,1,0:T(1,128)S(1)}, u32[]{:S(2)}, u32[]{:S(2)}) async-start(s32[16,1,128]{2,1,0:T(1,128)} %bitcast.17), calls=%async_computation.1 | async-start | bytes 16384 | tf_op jit(solution)/shard_map/all_to_all | solution.py:36
  27.8 20.0 %all-to-all-start.2 = ((s32[32,1,128]{2,1,0:T(1,128)}), s32[32,1,128]{2,1,0:T(1,128)S(1)}, u32[]{:S(2)}, u32[]{:S(2)}) async-start(s32[32,1,128]{2,1,0:T(1,128)} %bitcast.22), calls=%async_computation.2 | async-start | bytes 32768 | tf_op jit(solution)/shard_map/all_to_all | solution.py:36
  49.6 25.5 %all-to-all-start.3 = ((bf16[16,80,256]{2,1,0:T(8,128)(2,1)}), bf16[16,80,256]{2,1,0:T(8,128)(2,1)S(1)}, u32[]{:S(2)}, u32[]{:S(2)}) async-start(bf16[16,80,256]{2,1,0:T(8,128)(2,1)} %bitcast.31), calls=%async_computation.3 | async-start | bytes 1310720 | tf_op jit(solution)/shard_map/all_to_all | solution.py:36
  79.2 4.9 %copy-start.8 = (s32[128,20]{0,1:T(8,128)S(1)}, s32[128,20]{0,1:T(8,128)}, u32[]{:S(2)}) copy-start(s32[128,20]{0,1:T(8,128)} %param.29) | copy-start | bytes 30724
  79.2 4.9 %copy-start.12 = (s32[128]{0:T(128)S(1)}, s32[128]{0:T(128)}, u32[]{:S(2)}) copy-start(s32[128]{0:T(128)} %param.28) | copy-start | bytes 1540
  79.2 4.9 %copy-start.13 = (f32[128]{0:T(128)S(1)}, f32[128]{0:T(128)}, u32[]{:S(2)}) copy-start(f32[128]{0:T(128)} %param.31) | copy-start | bytes 1540
  79.2 5.0 %copy-start.14 = (f32[128]{0:T(128)S(1)}, f32[128]{0:T(128)}, u32[]{:S(2)}) copy-start(f32[128]{0:T(128)} %param.30) | copy-start | bytes 1540
  79.2 10.3 %copy-start.4 = (f32[512,256]{1,0:T(8,128)S(1)}, f32[512,256]{1,0:T(8,128)}, u32[]{:S(2)}) copy-start(f32[512,256]{1,0:T(8,128)} %param.22) | copy-start | bytes 1572868
  79.2 39.8 %all-to-all-start.4 = ((bf16[32,88,256]{2,1,0:T(8,128)(2,1)}), bf16[32,88,256]{2,1,0:T(8,128)(2,1)S(1)}, u32[]{:S(2)}, u32[]{:S(2)}) async-start(bf16[32,88,256]{2,1,0:T(8,128)(2,1)} %add_convert_fusion), calls=%async_computation.4 | async-start | bytes 2883584 | tf_op jit(solution)/shard_map/all_to_all | solution.py:36
  129.2 2.1 %copy-start.2 = (bf16[2,10,128,128]{3,2,1,0:T(8,128)(2,1)S(1)}, bf16[2,10,128,128]{3,2,1,0:T(8,128)(2,1)}, u32[]{:S(2)}) copy-start(bf16[2,10,128,128]{3,2,1,0:T(8,128)(2,1)} %cosine_convert_fusion) | copy-start | bytes 1966084
  129.2 2.1 %copy-start.6 = (bf16[384,256]{1,0:T(8,128)(2,1)S(1)}, bf16[384,256]{1,0:T(8,128)(2,1)}, u32[]{:S(2)}) copy-start(bf16[384,256]{1,0:T(8,128)(2,1)} %param.34) | copy-start | bytes 589828
  132.1 0.8 copy-start.9
  132.9 1.0 copy-start.15
  132.9 1.0 copy-start.18
  132.9 1.2 copy-start.16
  133.0 1.2 copy-start.17
  134.9 11.6 %copy-start.11 = (f32[768]{0:T(1024)S(1)}, f32[768]{0:T(1024)}, u32[]{:S(2)}) copy-start(f32[768]{0:T(1024)} %param.41) | copy-start | bytes 9220
  136.2 31.8 %all-to-all-start.5 = ((bf16[512,2,256]{2,1,0:T(2,128)(2,1)}), bf16[512,2,256]{2,1,0:T(2,128)(2,1)S(1)}, u32[]{:S(2)}, u32[]{:S(2)}) async-start(bf16[512,2,256]{2,1,0:T(2,128)(2,1)} %reshape.213), calls=%async_computation.5 | async-start | bytes 1048576 | tf_op jit(solution)/shard_map/all_to_all | solution.py:36
  168.3 3.3 %copy-start.1 = (f32[512,768]{1,0:T(8,128)S(1)}, f32[512,768]{1,0:T(8,128)}, u32[]{:S(2)}) copy-start(f32[512,768]{1,0:T(8,128)} %fusion.76) | copy-start | bytes 4718596
  168.3 3.3 %copy-start.5 = (f32[512,256]{1,0:T(8,128)S(1)}, f32[512,256]{1,0:T(8,128)}, u32[]{:S(2)}) copy-start(f32[512,256]{1,0:T(8,128)} %param.22) | copy-start | bytes 1572868

commit v3 on v2

--- a/solution.py
+++ b/solution.py
@@ -3,6 +3,8 @@
 import jax
 import jax.numpy as jnp
 from jax import lax
+from jax.experimental import pallas as pl
+from jax.experimental.pallas import tpu as pltpu
 from jax.sharding import PartitionSpec as P
 
 HEADS = 2
@@ -85,6 +87,111 @@
     ).astype(jnp.bfloat16)
     message = jnp.einsum("jec,cd->jed", hidden, message_out, preferred_element_type=jnp.float32)
     return (embedded, message)
+
+
+def across(left, right):
+    return lax.dot_general(
+        left, right, (((1,), (1,)), ((), ())), preferred_element_type=jnp.float32
+    )
+
+
+def event_kernel(
+    table,
+    lanes,
+    count,
+    slot,
+    code,
+    fixed,
+    query_weight,
+    pair_weight,
+    out_weight,
+    out_bias,
+    message_in,
+    message_out,
+    embedded,
+    slot_sum,
+    turned,
+    values,
+    exponents,
+):
+    rows, width = table.shape
+    pairs = lanes.shape[1]
+    events = pairs // 2
+    head_size = width // HEADS
+    one = jnp.bfloat16(1)
+    none = jnp.bfloat16(0)
+
+    def dot(left, right):
+        return jnp.dot(left, right, preferred_element_type=jnp.float32)
+
+    def number(size):
+        return lax.broadcasted_iota(jnp.int32, (size, pairs), 0).astype(jnp.float32).astype(jnp.bfloat16)
+
+    def near(index, first, size):
+        return jnp.clip(index - first, -1, size).astype(jnp.float32).astype(jnp.bfloat16)
+
+    row = lax.broadcasted_iota(jnp.int32, (width, width), 0)
+    column = lax.broadcasted_iota(jnp.int32, (width, width), 1)
+    unit = jnp.where(row == column, 1.0, 0.0).astype(jnp.bfloat16)
+    for low in range(0, rows, width):
+        turned[:, low : low + width] = across(unit, table[low : low + width, :]).astype(jnp.bfloat16)
+    numbers = number(width)
+
+    def gather(index):
+        total = jnp.zeros((width, pairs), jnp.float32)
+        for low in range(0, rows, width):
+            chosen = jnp.where(numbers == near(index, low, width), one, none)
+            total = total + dot(turned[:, low : low + width], chosen)
+        return total.astype(jnp.bfloat16)
+
+    ends = gather(lanes[K : K + 1, :])
+    queries = dot(query_weight[:, :width], ends) + dot(query_weight[:, width:], fixed[...])
+
+    def neighbour(k, carry):
+        near_rows = gather(lanes[pl.ds(k, 1), :])
+        pair = dot(pair_weight[:, :width], near_rows) + dot(pair_weight[:, width:], code[k])
+        values[k] = pair[width:]
+        product = queries * pair[:width]
+        for head in range(HEADS):
+            scores = jnp.sum(
+                product[head * head_size : (head + 1) * head_size], axis=0, keepdims=True
+            ) / math.sqrt(head_size)
+            exponents[k, head : head + 1, :] = jnp.where(k < count[...], jnp.exp(scores), 0.0)
+        return carry
+
+    lax.fori_loop(0, K, neighbour, 0)
+    pieces = []
+    for head in range(HEADS):
+        low = head * head_size
+        high = low + head_size
+        total = exponents[0, head : head + 1, :]
+        for k in range(1, K):
+            total = total + exponents[k, head : head + 1, :]
+        piece = jnp.zeros((head_size, pairs), jnp.float32)
+        for k in range(K):
+            piece = piece + exponents[k, head : head + 1, :] / total * values[k, low:high, :]
+        pieces.append(piece)
+    attended = jnp.concatenate(pieces, 0).astype(jnp.bfloat16)
+    embeds = jnp.maximum(
+        dot(out_weight[:, :width], attended) + dot(out_weight[:, width:], ends) + out_bias[...], 0.0
+    ).astype(jnp.bfloat16)
+    other = jnp.concatenate([embeds[:, events:], embeds[:, :events]], 1)
+    hidden = jnp.maximum(
+        dot(message_in[:, :width], embeds) + dot(message_in[:, width:], other), 0.0
+    ).astype(jnp.bfloat16)
+    message = dot(message_out[...], hidden)
+    high = message.astype(jnp.bfloat16)
+    low = (message - high.astype(jnp.float32)).astype(jnp.bfloat16)
+    for first in range(0, slot_sum.shape[0], width):
+        chosen = jnp.where(numbers == near(slot[...], first, width), one, none)
+        slot_sum[first : first + width, :] = (across(chosen, high) + across(chosen, low)).astype(
+            jnp.bfloat16
+        )
+    for side in range(2):
+        half = embeds[:, side * events : (side + 1) * events]
+        embedded[:, side * width : (side + 1) * width] = across(
+            unit[:events, :events], half
+        ).astype(jnp.bfloat16)
 
 
 def gru_update(memory, mem_half, totals, counts, input_weight, state_weight, update_bias):
@@ -232,50 +339,82 @@
     table = exchange((near_part + listed_ends).astype(jnp.bfloat16), "dev")
     table = table.reshape(members * CAP, row_width)
 
-    def fetch(table, index):
-        return (
-            jnp.take(table, index[: 2 * K * events], axis=0, mode="clip"),
-            jnp.take(table, index[2 * K * events :], axis=0, mode="clip"),
-        )
+    elapsed = (event_time[None, :] - jnp.transpose(near_time)).astype(jnp.float32)
+    elapsed = elapsed.reshape(2, K, events)
 
     def whole():
         full = jnp.broadcast_to(near_block[None], (members, block, row_width))
         full = exchange(jnp.concatenate([full, end_part], 1), "dev")
-        return fetch(
+        fetched = jnp.take(
             full.reshape(members * places, row_width),
             jnp.where(member >= 0, member * places + place, 0),
+            axis=0,
+            mode="clip",
         )
-
-    near_rows, end_rows = lax.cond(most > CAP, whole, lambda: fetch(table, index))
-    near_rows = near_rows.reshape(2, K, events, row_width)
-    end_rows = end_rows.reshape(2, events, row_width)
-    elapsed = (
-        (event_time[None, :] - jnp.transpose(near_time)).astype(jnp.float32).reshape(2, K, events)
-    )
-    embedded, message = event_block(
-        end_rows,
-        near_rows,
-        elapsed,
-        counted,
-        frequency,
-        phases,
-        query_weight,
-        key_weight,
-        value_weight,
-        out_weight,
-        out_bias,
-        message_in,
-        message_out,
-    )
-    message = message.reshape(-1, row_width)
-    message_high = lax.reduce_precision(message, 8, 7)
-    slot_sum = jnp.dot(
-        end_hot, message_high.astype(jnp.bfloat16), preferred_element_type=jnp.float32
-    ) + jnp.dot(
-        end_hot, (message - message_high).astype(jnp.bfloat16), preferred_element_type=jnp.float32
-    )
+        embedded, message = event_block(
+            fetched[2 * K * events :].reshape(2, events, row_width),
+            fetched[: 2 * K * events].reshape(2, K, events, row_width),
+            elapsed,
+            counted,
+            frequency,
+            phases,
+            query_weight,
+            key_weight,
+            value_weight,
+            out_weight,
+            out_bias,
+            message_in,
+            message_out,
+        )
+        message = message.reshape(-1, row_width)
+        high = lax.reduce_precision(message, 8, 7)
+        slot_sum = jnp.dot(
+            end_hot, high.astype(jnp.bfloat16), preferred_element_type=jnp.float32
+        ) + jnp.dot(
+            end_hot, (message - high).astype(jnp.bfloat16), preferred_element_type=jnp.float32
+        )
+        return jnp.concatenate([embedded[0], embedded[1]], 1), slot_sum.astype(jnp.bfloat16)
+
+    pairs = 2 * events
+    near_lanes = jnp.transpose(index[: 2 * K * events].reshape(2, K, events), (1, 0, 2))
+    lanes = jnp.concatenate(
+        [near_lanes.reshape(K, pairs), index[2 * K * events :].reshape(1, pairs)], 0
+    )
+    elapsed_lanes = jnp.transpose(elapsed, (1, 0, 2)).reshape(K, 1, pairs)
+    code = jnp.cos(elapsed_lanes * frequency[None, :, None] + phases[None, :, None])
+    fixed = jnp.broadcast_to(jnp.cos(phases)[:, None], (phases.shape[0], pairs))
+    operands = (
+        lanes,
+        counted.reshape(1, pairs),
+        end_value.reshape(1, pairs),
+        code.astype(jnp.bfloat16),
+        fixed.astype(jnp.bfloat16),
+        jnp.transpose(query_weight),
+        jnp.transpose(jnp.concatenate([key_weight, value_weight], 1)),
+        jnp.transpose(out_weight),
+        out_bias[:, None],
+        jnp.transpose(message_in),
+        jnp.transpose(message_out),
+    )
+
+    def listed_only():
+        return pl.pallas_call(
+            event_kernel,
+            out_shape=(
+                jax.ShapeDtypeStruct((events, 2 * row_width), jnp.bfloat16),
+                jax.ShapeDtypeStruct((groups * members * CAP_E, row_width), jnp.bfloat16),
+            ),
+            scratch_shapes=[
+                pltpu.VMEM((row_width, table.shape[0]), jnp.bfloat16),
+                pltpu.VMEM((K, row_width, pairs), jnp.float32),
+                pltpu.VMEM((K, 8, pairs), jnp.float32),
+            ],
+            name="event_kernel",
+        )(table, *operands)
+
+    embedded, slot_sum = lax.cond(most > CAP, whole, listed_only)
     news = exchange(
-        slot_sum.astype(jnp.bfloat16).reshape(groups * members, CAP_E, row_width), ("grp", "dev")
+        slot_sum.reshape(groups * members, CAP_E, row_width), ("grp", "dev")
     ).reshape(-1, row_width)
     owned = got_end.reshape(-1)
     owned_hot = hot(owned, nodes, 0)
@@ -289,7 +428,7 @@
     new_memory = gru_update(
         memory, mem_half, totals, counts, input_weight, state_weight, update_bias
     )
-    return (new_memory, jnp.concatenate([embedded[0], embedded[1]], 1))
+    return (new_memory, embedded)
 
 
 def solution(mesh):

time: 175 us -> 177 us (1.011)
  Pallas kernels: 0 us -> 14.1 us
  waiting for transfers between devices: 81.3 us -> 71.9 us
  matrix products: 16.2 us -> 9.7 us
  local copies, waits for them, and re-layouts: 15.4 us -> 18.1 us
    pallas_call x0 -> x1, Pallas kernels: none -> 14.1 us  [listed_only(): pl.pallas_call(event_kernel, out_shape=(jax.ShapeDtypeStruct((events, 2 *...]
    all_to_all x5, waiting for transfers between devices: 81.3 us -> 71.9 us  [exchange(): return lax.all_to_all(x, axis, split_axis=0, concat_axis=0, tiled=True)]
    gather x2 -> x0, local copies, waits for them, and re-layouts: 8.72 us -> none  [the longest x1 7.57 us: fetch(): jnp.take(table, index[:2 * K * events], axis=0, mode='clip')]
    unnamed x39 -> x59, local copies, waits for them, and re-layouts: 0.25 us -> 7.26 us
    dot_general x7 -> x0, matrix products: 5.28 us -> none  [the longest x1 2.03 us: event_block(): jnp.einsum('jkec,cd->jked', near_in, key_weight, preferred_element_type=j...]
    broadcast_in_dim x0 -> x2, local copies, waits for them, and re-layouts: none -> 2.83 us  [the longest x1 1.48 us: local(): out_bias[:, None]]
    convert_element_type x4 -> x3, other arithmetic: 5.44 us -> 6.21 us  [the longest x1 5.41 us: local(): code.astype(jnp.bfloat16)]
  transfers between devices with their start and end apart: 5 -> 5, of which waited for: 5 -> 5; matrix products, arithmetic and copies ran while one was open for 6% -> 11% of each run, Pallas kernels for 0% -> 0%
where the time goes in v3:
time: 177 us; the launch traced here: 176 us
  waiting for transfers between devices  71.9 us (41%)
  starting transfers between devices  41.3 us (23%)
  other arithmetic  19.1 us (11%)
  local copies, waits for them, and re-layouts  18.1 us (10%)
  Pallas kernels  14.1 us (8%)
  matrix products  9.7 us (5%)
    all_to_all x5, waiting for transfers between devices, exchange(): return lax.all_to_all(x, axis, split_axis=0, concat_axis=0, tiled=True)  71.9 us
    all_to_all x5, starting transfers between devices, exchange(): return lax.all_to_all(x, axis, split_axis=0, concat_axis=0, tiled=True)  41.3 us
    pallas_call x1, Pallas kernels, listed_only(): pl.pallas_call(event_kernel, out_shape=(jax.ShapeDtypeStruct((events, 2 *...  14.1 us
    unnamed x59, local copies, waits for them, and re-layouts  7.26 us
    convert_element_type x1, other arithmetic, local(): code.astype(jnp.bfloat16)  5.41 us
  transfers between devices with their start and end apart: 5, of which 5 were waited for; matrix products, arithmetic and copies ran while one was open for 11% of the time, Pallas kernels for 0%

profile of v3, /device:TPU:1, one launch (start us, length us, event | category | flops | bytes accessed | tf_op | source)
XLA Modules:
  0.0 176.1 jit_solution(8012649764566832212)
XLA Ops:
  0.7 0.8 iota_compare_fusion.29
  1.5 0.7 or_bitcast_fusion
  3.6 0.7 fusion.62
  5.9 0.8 reshape.218
  8.3 10.1 %all-to-all-start.1 = ((s32[16,1,128]{2,1,0:T(1,128)}), s32[16,1,128]{2,1,0:T(1,128)S(1)}, u32[]{:S(2)}, u32[]{:S(2)}) async-start(s32[16,1,128]{2,1,0:T(1,128)} %bitcast.30), calls=%async_computation.1 | async-start | bytes 16384 | tf_op jit(solution)/shard_map/all_to_all | solution.py:38
  19.1 6.4 %all-to-all-done.1 = s32[16,1,128]{2,1,0:T(1,128)S(1)} async-done(((s32[16,1,128]{2,1,0:T(1,128)}), s32[16,1,128]{2,1,0:T(1,128)S(1)}, u32[]{:S(2)}, u32[]{:S(2)}) %all-to-all-start.1) | async-done | bytes 8224 | tf_op jit(solution)/shard_map/all_to_all | solution.py:38
  27.8 11.4 %all-to-all-start.2 = ((s32[32,1,128]{2,1,0:T(1,128)}), s32[32,1,128]{2,1,0:T(1,128)S(1)}, u32[]{:S(2)}, u32[]{:S(2)}) async-start(s32[32,1,128]{2,1,0:T(1,128)} %bitcast.35), calls=%async_computation.2 | async-start | bytes 32768 | tf_op jit(solution)/shard_map/all_to_all | solution.py:38
  39.2 8.5 %all-to-all-done.2 = s32[32,1,128]{2,1,0:T(1,128)S(1)} async-done(((s32[32,1,128]{2,1,0:T(1,128)}), s32[32,1,128]{2,1,0:T(1,128)S(1)}, u32[]{:S(2)}, u32[]{:S(2)}) %all-to-all-start.2) | async-done | bytes 16416 | tf_op jit(solution)/shard_map/all_to_all | solution.py:38
  48.8 1.5 fusion.52
  50.2 5.5 %all-to-all-start.3 = ((bf16[16,80,256]{2,1,0:T(8,128)(2,1)}), bf16[16,80,256]{2,1,0:T(8,128)(2,1)S(1)}, u32[]{:S(2)}, u32[]{:S(2)}) async-start(bf16[16,80,256]{2,1,0:T(8,128)(2,1)} %bitcast.44), calls=%async_computation.3 | async-start | bytes 1310720 | tf_op jit(solution)/shard_map/all_to_all | solution.py:38
  55.8 20.0 %all-to-all-done.3 = bf16[16,80,256]{2,1,0:T(8,128)(2,1)S(1)} async-done(((bf16[16,80,256]{2,1,0:T(8,128)(2,1)}), bf16[16,80,256]{2,1,0:T(8,128)(2,1)S(1)}, u32[]{:S(2)}, u32[]{:S(2)}) %all-to-all-start.3) | async-done | bytes 655392 | tf_op jit(solution)/shard_map/all_to_all | solution.py:38
  77.5 1.2 fusion.49
  78.7 1.7 add_convert_fusion
  80.5 4.1 %all-to-all-start.4 = ((bf16[32,88,256]{2,1,0:T(8,128)(2,1)}), bf16[32,88,256]{2,1,0:T(8,128)(2,1)S(1)}, u32[]{:S(2)}, u32[]{:S(2)}) async-start(bf16[32,88,256]{2,1,0:T(8,128)(2,1)} %add_convert_fusion), calls=%async_computation.4 | async-start | bytes 2883584 | tf_op jit(solution)/shard_map/all_to_all | solution.py:38
  88.1 0.9 copy.143
  89.0 1.8 %copy.144 = bf16[512,256]{0,1:T(8,128)(2,1)} copy(bf16[512,256]{1,0:T(8,128)(2,1)} %param.37) | data formatting | bytes 524288 | tf_op args[15]
  90.8 0.8 copy.140
  91.7 0.8 copy.145
  92.4 1.3 pad_add_fusion
  93.8 0.8 maximum_bitcast_fusion
  95.4 5.4 %cosine_convert_fusion.2 = bf16[10,128,256]{2,1,0:T(8,128)(2,1)S(1)} fusion(f32[128]{0:T(128)} %param.31, f32[128]{0:T(128)} %param.30, f32[10,256]{1,0:T(8,128)} %bitcast.144), kind=kLoop, calls=%fused_computation.82 | loop fusion | flops 983040 | bytes 666624 | tf_op jit(solution)/shard_map/convert_element_type | solution.py:390
  102.2 18.1 %all-to-all-done.4 = bf16[32,88,256]{2,1,0:T(8,128)(2,1)S(1)} async-done(((bf16[32,88,256]{2,1,0:T(8,128)(2,1)}), bf16[32,88,256]{2,1,0:T(8,128)(2,1)S(1)}, u32[]{:S(2)}, u32[]{:S(2)}) %all-to-all-start.4) | async-done | bytes 1441824 | tf_op jit(solution)/shard_map/all_to_all | solution.py:38
  120.3 19.0 %conditional.1 = (bf16[128,512]{1,0:T(8,128)(2,1)S(1)}, bf16[512,2,256]{2,1,0:T(2,128)(2,1)}) conditional(s32[]{:T(128)} %convert_element_type.105, (bf16[32,88,256]{2,1,0:T(8,128)(2,1)S(1)}, s32[2,128]{1,0:T(2,128)}, s32[2,128]{1,0:T(2,128)}, bf16[128]{0:T(256)(128)(2,1)}, f32[256]{0:T(256)}, /*index=5*/s32[11,256]{1,0:T(8,128)}, ...), branch_computations={%region_8.9_spmd, %region_9.16_spmd} | conditional | flops 1517137536 | bytes 64909212 | solution.py:415
  120.3 1.5 copy.123.out_bias
  121.8 1.3 broadcast_in_dim.47.fixed
  123.1 14.1 %event_kernel.1 = (bf16[128,512]{1,0:T(8,128)(2,1)S(1)}, bf16[1024,256]{1,0:T(8,128)(2,1)}) custom-call(bf16[2816,256]{1,0:T(8,128)(2,1)S(1)} %bitcast.116, s32[11,256]{1,0:T(8,128)} %get-tuple-element.62.lanes, s32[1,256]{1,0:T(1,128)} %bitcast.154, s32[1,256]{1,0:T(1,128)} %bitcast.150, bf16[10,128,256]{2,1,0:T(8,128)(2,1)S(1)} %get-tuple-element.65.code, ...), custom_call_target="tpu_custom_call" | custom-call | tf_op jit(solution)/shard_map/cond/branch_0_fun/event_kernel/pallas_call | solution.py:401
  137.2 2.0 %reshape.247 = bf16[512,2,256]{2,1,0:T(2,128)(2,1)} reshape(bf16[1024,256]{1,0:T(8,128)(2,1)} %get-tuple-element.106) | data formatting | bytes 1048576 | tf_op jit(solution)/shard_map/reshape | solution.py:417
  139.3 10.3 %all-to-all-start.5 = ((bf16[512,2,256]{2,1,0:T(2,128)(2,1)}), bf16[512,2,256]{2,1,0:T(2,128)(2,1)S(1)}, u32[]{:S(2)}, u32[]{:S(2)}) async-start(bf16[512,2,256]{2,1,0:T(2,128)(2,1)} %get-tuple-element.107), calls=%async_computation.5 | async-start | bytes 1048576 | tf_op jit(solution)/shard_map/all_to_all | solution.py:38
  149.6 1.5 fusion.86
  152.2 18.9 %all-to-all-done.5 = bf16[512,2,256]{2,1,0:T(2,128)(2,1)S(1)} async-done(((bf16[512,2,256]{2,1,0:T(2,128)(2,1)}), bf16[512,2,256]{2,1,0:T(2,128)(2,1)S(1)}, u32[]{:S(2)}, u32[]{:S(2)}) %all-to-all-start.5) | async-done | bytes 524320 | tf_op jit(solution)/shard_map/all_to_all | solution.py:38
  171.4 2.2 %fusion.60 = f32[512,768]{1,0:T(8,128)} fusion(bf16[256,768]{1,0:T(8,128)(2,1)S(1)} %copy-done.35, bf16[1024,256]{1,0:T(8,128)(2,1)S(1)} %reshape.230, s32[1024]{0:T(1024)S(1)} %select_n.97, f32[512]{0:T(512)S(1)} %convert_maximum_fusion), kind=kOutput, calls=%fused_computation.86 | convolution fusion | flops 470548480 | bytes 2496512 | tf_op jit(solution)/shard_map/dot_general | solution.py:200
  173.5 2.6 %fusion.70 = f32[512,256]{1,0:T(8,128)} fusion(f32[512,256]{1,0:T(8,128)S(1)} %copy-done.2, f32[512,768]{1,0:T(8,128)S(1)} %fusion.86, f32[512,768]{1,0:T(8,128)} %fusion.60, f32[256]{0:T(256)S(1)} %get-tuple-element.129, f32[256]{0:T(256)S(1)} %get-tuple-element.130, f32[256]{0:T(256)S(1)} %get-tuple-element.128, pred[512]{0:T(512)(128)(4,1)S(1)} %convert_compare_fusion), kind=kLoop, calls=%fused_computation.98 | loop fusion | flops 2359296 | bytes 4197888 | tf_op jit(solution)/shard_map/jit(_where)/select_n | solution.py:216
  (114 shorter events, 16.6 us)
Async XLA Ops:
  0.6 149.0 %copy-start = (bf16[256,768]{1,0:T(8,128)(2,1)S(1)}, bf16[256,768]{1,0:T(8,128)(2,1)}, u32[]{:S(2)}) copy-start(bf16[256,768]{1,0:T(8,128)(2,1)} %param.40) | copy-start | bytes 1179652
  0.6 6.4 %copy-start.24 = (s32[128,2]{0,1:T(2,128)S(1)}, s32[128,2]{0,1:T(2,128)}, u32[]{:S(2)}) copy-start(s32[128,2]{0,1:T(2,128)} %param.25) | copy-start | bytes 3076
  0.7 6.7 %copy-start.28 = (s32[1,512,2]{1,2,0:T(2,128)S(1)}, s32[1,512,2]{1,2,0:T(2,128)}, u32[]{:S(2)}) copy-start(s32[1,512,2]{1,2,0:T(2,128)} %param.23) | copy-start | bytes 12292
  0.7 48.1 %copy-start.1 = (f32[512,256]{1,0:T(8,128)S(1)}, f32[512,256]{1,0:T(8,128)}, u32[]{:S(2)}) copy-start(f32[512,256]{1,0:T(8,128)} %param.22) | copy-start | bytes 1572868
  3.6 81.0 %copy-start.22 = (s32[2816]{0:T(1024)}, s32[2816]{0:T(1024)S(1)}, u32[]{:S(2)}) copy-start(s32[2816]{0:T(1024)S(1)} %get-tuple-element.135) | copy-start | bytes 33796
  3.6 81.7 %copy-start.19 = (s32[2816]{0:T(1024)}, s32[2816]{0:T(1024)S(1)}, u32[]{:S(2)}) copy-start(s32[2816]{0:T(1024)S(1)} %get-tuple-element.134) | copy-start | bytes 33796
  8.3 17.1 %all-to-all-start.1 = ((s32[16,1,128]{2,1,0:T(1,128)}), s32[16,1,128]{2,1,0:T(1,128)S(1)}, u32[]{:S(2)}, u32[]{:S(2)}) async-start(s32[16,1,128]{2,1,0:T(1,128)} %bitcast.30), calls=%async_computation.1 | async-start | bytes 16384 | tf_op jit(solution)/shard_map/all_to_all | solution.py:38
  27.8 20.0 %all-to-all-start.2 = ((s32[32,1,128]{2,1,0:T(1,128)}), s32[32,1,128]{2,1,0:T(1,128)S(1)}, u32[]{:S(2)}, u32[]{:S(2)}) async-start(s32[32,1,128]{2,1,0:T(1,128)} %bitcast.35), calls=%async_computation.2 | async-start | bytes 32768 | tf_op jit(solution)/shard_map/all_to_all | solution.py:38
  48.4 27.3 %copy-start.13 = (s32[32,32]{0,1:T(8,128)}, s32[32,32]{0,1:T(8,128)S(1)}, u32[]{:S(2)}) copy-start(s32[32,32]{0,1:T(8,128)S(1)} %copy.131) | copy-start | bytes 12292
  50.2 25.5 %all-to-all-start.3 = ((bf16[16,80,256]{2,1,0:T(8,128)(2,1)}), bf16[16,80,256]{2,1,0:T(8,128)(2,1)S(1)}, u32[]{:S(2)}, u32[]{:S(2)}) async-start(bf16[16,80,256]{2,1,0:T(8,128)(2,1)} %bitcast.44), calls=%async_computation.3 | async-start | bytes 1310720 | tf_op jit(solution)/shard_map/all_to_all | solution.py:38
  76.8 0.6 copy-start.3
  80.4 6.1 %copy-start.27 = (s32[128,20]{0,1:T(8,128)S(1)}, s32[128,20]{0,1:T(8,128)}, u32[]{:S(2)}) copy-start(s32[128,20]{0,1:T(8,128)} %param.29) | copy-start | bytes 30724
  80.4 6.1 %copy-start.34 = (s32[128]{0:T(128)S(1)}, s32[128]{0:T(128)}, u32[]{:S(2)}) copy-start(s32[128]{0:T(128)} %param.28) | copy-start | bytes 1540
  80.4 7.3 %copy-start.6 = (bf16[384,256]{1,0:T(8,128)(2,1)S(1)}, bf16[384,256]{1,0:T(8,128)(2,1)}, u32[]{:S(2)}) copy-start(bf16[384,256]{1,0:T(8,128)(2,1)} %param.33) | copy-start | bytes 589828
  80.4 7.5 %copy-start.4 = (bf16[384,256]{1,0:T(8,128)(2,1)S(1)}, bf16[384,256]{1,0:T(8,128)(2,1)}, u32[]{:S(2)}) copy-start(bf16[384,256]{1,0:T(8,128)(2,1)} %param.34) | copy-start | bytes 589828
  80.4 7.7 %copy-start.10 = (bf16[512,256]{1,0:T(8,128)(2,1)S(1)}, bf16[512,256]{1,0:T(8,128)(2,1)}, u32[]{:S(2)}) copy-start(bf16[512,256]{1,0:T(8,128)(2,1)} %param.35) | copy-start | bytes 786436
  80.5 39.8 %all-to-all-start.4 = ((bf16[32,88,256]{2,1,0:T(8,128)(2,1)}), bf16[32,88,256]{2,1,0:T(8,128)(2,1)S(1)}, u32[]{:S(2)}, u32[]{:S(2)}) async-start(bf16[32,88,256]{2,1,0:T(8,128)(2,1)} %add_convert_fusion), calls=%async_computation.4 | async-start | bytes 2883584 | tf_op jit(solution)/shard_map/all_to_all | solution.py:38
  84.6 6.3 %copy-start.8 = (bf16[384,256]{1,0:T(8,128)(2,1)S(1)}, bf16[384,256]{1,0:T(8,128)(2,1)}, u32[]{:S(2)}) copy-start(bf16[384,256]{1,0:T(8,128)(2,1)} %param.32) | copy-start | bytes 589828
  84.6 7.1 %copy-start.15 = (bf16[256,256]{1,0:T(8,128)(2,1)S(1)}, bf16[256,256]{1,0:T(8,128)(2,1)}, u32[]{:S(2)}) copy-start(bf16[256,256]{1,0:T(8,128)(2,1)} %param.38) | copy-start | bytes 393220
  86.6 0.6 copy-start.17
  88.1 6.5 %copy-start.30 = (f32[128]{0:T(128)S(1)}, f32[128]{0:T(128)}, u32[]{:S(2)}) copy-start(f32[128]{0:T(128)} %param.31) | copy-start | bytes 1540
  89.0 6.2 %copy-start.25 = (s32[128,2]{0,1:T(2,128)S(1)}, s32[128,2]{0,1:T(2,128)}, u32[]{:S(2)}) copy-start(s32[128,2]{0,1:T(2,128)} %param.25) | copy-start | bytes 3076
  120.3 29.3 %copy-start.29 = (f32[768]{0:T(1024)S(1)}, f32[768]{0:T(1024)}, u32[]{:S(2)}) copy-start(f32[768]{0:T(1024)} %param.41) | copy-start | bytes 9220
  139.3 10.3 %copy-start.36 = (bf16[128,512]{1,0:T(8,128)(2,1)}, bf16[128,512]{1,0:T(8,128)(2,1)S(1)}, u32[]{:S(2)}) copy-start(bf16[128,512]{1,0:T(8,128)(2,1)S(1)} %get-tuple-element.92) | copy-start | bytes 393220
  139.3 11.8 %copy-start.14 = (s32[32,32]{0,1:T(8,128)S(1)}, s32[32,32]{0,1:T(8,128)}, u32[]{:S(2)}) copy-start(s32[32,32]{0,1:T(8,128)} %copy-done.13) | copy-start | bytes 12292
  139.3 12.2 %copy-start.21 = (s32[32,32]{1,0:T(8,128)S(1)}, s32[32,32]{1,0:T(8,128)}, u32[]{:S(2)}) copy-start(s32[32,32]{1,0:T(8,128)} %get-tuple-element.114) | copy-start | bytes 12292
  139.3 31.8 %all-to-all-start.5 = ((bf16[512,2,256]{2,1,0:T(2,128)(2,1)}), bf16[512,2,256]{2,1,0:T(2,128)(2,1)S(1)}, u32[]{:S(2)}, u32[]{:S(2)}) async-start(bf16[512,2,256]{2,1,0:T(2,128)(2,1)} %get-tuple-element.107), calls=%async_computation.5 | async-start | bytes 1048576 | tf_op jit(solution)/shard_map/all_to_all | solution.py:38
  149.6 21.7 %copy-start.35 = (bf16[256,768]{1,0:T(8,128)(2,1)S(1)}, bf16[256,768]{1,0:T(8,128)(2,1)}, u32[]{:S(2)}) copy-start(bf16[256,768]{1,0:T(8,128)(2,1)} %param.39) | copy-start | bytes 1179652
  171.3 2.2 %copy-start.2 = (f32[512,256]{1,0:T(8,128)S(1)}, f32[512,256]{1,0:T(8,128)}, u32[]{:S(2)}) copy-start(f32[512,256]{1,0:T(8,128)} %param.22) | copy-start | bytes 1572868

commit v4 on v3

--- a/solution.py
+++ b/solution.py
@@ -95,6 +95,82 @@
     )
 
 
+def request_kernel(mine, near_slot, end_slot, count, want_end, want_near, first, rank_or_none):
+    groups = first.shape[0]
+    members, places = rank_or_none.shape
+    events = near_slot.shape[1]
+    owners = groups * members
+    block = groups * CAP_N
+
+    def ones(match):
+        return jnp.where(match, 1.0, 0.0).astype(jnp.bfloat16)
+
+    def numbers(size, width):
+        return lax.broadcasted_iota(jnp.int32, (size, width), 0)
+
+    def lanes(size, width):
+        return lax.broadcasted_iota(jnp.int32, (size, width), 1)
+
+    member_pieces = []
+    place_pieces = []
+    for line in range(2 * K):
+        member, place = split_slot(near_slot[line : line + 1, :], members, CAP_N)
+        side = line // K
+        member = jnp.where(line - side * K < count[side : side + 1, :], member, -1)
+        member_pieces.append(ones(numbers(members, events) == member))
+        place_pieces.append(ones(numbers(places, events) == place))
+    group_pieces = []
+    lane_pieces = []
+    for line in range(2):
+        value = end_slot[line : line + 1, :]
+        member, place = split_slot(value, members, CAP_E)
+        member_pieces.append(ones(numbers(members, events) == member))
+        place_pieces.append(ones(numbers(places, events) == place + block))
+        group = value >> (CAP_E * members).bit_length() - 1
+        group_pieces.append(ones(numbers(groups, events) == group))
+        lane_pieces.append(ones(numbers(LANES, events) == (value & (CAP_E - 1)) * members + member))
+    uses = across(jnp.concatenate(member_pieces, 1), jnp.concatenate(place_pieces, 1))
+    used = ones(uses > 0)
+    before = ones(numbers(places, places) < lanes(places, places))
+    rank = jnp.dot(used, before, preferred_element_type=jnp.float32)
+    rank_or_none[...] = jnp.where(uses > 0, rank, -1.0).astype(jnp.int32)
+    most = jnp.max(jnp.sum(used.astype(jnp.float32), axis=1, keepdims=True)).astype(jnp.int32)
+    times = across(jnp.concatenate(group_pieces, 1), jnp.concatenate(lane_pieces, 1)).astype(jnp.int32)
+
+    group = lanes(groups, owners) >> members.bit_length() - 1
+    own = group == numbers(groups, owners)
+    column = numbers(LANES, owners)
+    owner = lanes(LANES, owners)
+
+    def spread(part):
+        total = jnp.zeros((groups, LANES), jnp.float32)
+        for slot in range(CAP_E):
+            row = part(want_end[slot : slot + 1, :])
+            total = total + across(
+                jnp.where(own, row, 0.0).astype(jnp.bfloat16),
+                ones(column == slot * members + (owner & (members - 1))),
+            )
+        asked = jnp.concatenate(
+            [
+                jnp.zeros((members * CAP_E, owners), jnp.float32),
+                part(want_near[...]),
+                jnp.zeros((LANES - members * CAP_E - CAP_N, owners), jnp.float32),
+            ],
+            0,
+        )
+        return total + across(
+            ones(own & ((lanes(groups, owners) & (members - 1)) == mine[0])),
+            asked.astype(jnp.bfloat16),
+        )
+
+    high = spread(lambda wanted: ((wanted + 1) >> 4).astype(jnp.float32))
+    low = spread(lambda wanted: ((wanted + 1) & 15).astype(jnp.float32))
+    wanted = (16 * high + low).astype(jnp.int32) - 1
+    lane = lanes(groups, LANES)
+    wanted = jnp.where((lane < members * CAP_E) & (wanted >= 0), wanted + SHIFT * times, wanted)
+    first[...] = jnp.where(lane < members * CAP_E + CAP_N, wanted, most)
+
+
 def event_kernel(
     table,
     lanes,
@@ -145,7 +221,9 @@
         return total.astype(jnp.bfloat16)
 
     ends = gather(lanes[K : K + 1, :])
-    queries = dot(query_weight[:, :width], ends) + dot(query_weight[:, width:], fixed[...])
+    queries = dot(query_weight[:, :width], ends) + across(
+        query_weight[:, width:], jnp.broadcast_to(fixed[...], (pairs, fixed.shape[1]))
+    )
 
     def neighbour(k, carry):
         near_rows = gather(lanes[pl.ds(k, 1), :])
@@ -173,7 +251,10 @@
         pieces.append(piece)
     attended = jnp.concatenate(pieces, 0).astype(jnp.bfloat16)
     embeds = jnp.maximum(
-        dot(out_weight[:, :width], attended) + dot(out_weight[:, width:], ends) + out_bias[...], 0.0
+        dot(out_weight[:, :width], attended)
+        + dot(out_weight[:, width:], ends)
+        + jnp.transpose(jnp.broadcast_to(out_bias[...], (pairs, width))),
+        0.0,
     ).astype(jnp.bfloat16)
     other = jnp.concatenate([embeds[:, events:], embeds[:, :events]], 1)
     hidden = jnp.maximum(
@@ -248,25 +329,34 @@
     mem_half = memory.astype(jnp.bfloat16)
     counted = jnp.transpose(near_count)
 
-    near_value = jnp.transpose(near_slot).reshape(-1)
-    end_value = jnp.transpose(end_slot).reshape(-1)
+    near_value = jnp.transpose(near_slot)
+    end_value = jnp.transpose(end_slot)
+    first, rank_or_none = pl.pallas_call(
+        request_kernel,
+        out_shape=(
+            jax.ShapeDtypeStruct((groups, LANES), jnp.int32),
+            jax.ShapeDtypeStruct((members, places), jnp.int32),
+        ),
+        in_specs=[pl.BlockSpec(memory_space=pltpu.SMEM)]
+        + [pl.BlockSpec(memory_space=pltpu.VMEM)] * 5,
+        name="request_kernel",
+    )(
+        lax.axis_index("dev").reshape(1),
+        near_value,
+        end_value,
+        counted,
+        jnp.transpose(want_end.reshape(-1, CAP_E)),
+        jnp.transpose(want_near.reshape(-1, CAP_N)),
+    )
+    first = exchange(first, "grp")
+
+    near_value = near_value.reshape(-1)
+    end_value = end_value.reshape(-1)
     near_member, near_place = split_slot(near_value, members, CAP_N)
     end_member, end_place = split_slot(end_value, members, CAP_E)
     usable = (jnp.arange(K)[None, :, None] < counted[:, None, :]).reshape(-1)
     member = jnp.concatenate([jnp.where(usable, near_member, -1), end_member])
     place = jnp.concatenate([near_place, end_place + block])
-    member_hot = hot(member, members, 0)
-    place_hot = hot(place, places, 0)
-    used = (
-        lax.dot_general(
-            member_hot, place_hot, (((1,), (1,)), ((), ())), preferred_element_type=jnp.float32
-        )
-        > 0
-    )
-    before = (jnp.arange(places)[:, None] < jnp.arange(places)[None, :]).astype(jnp.bfloat16)
-    rank = jnp.dot(used.astype(jnp.bfloat16), before, preferred_element_type=jnp.float32)
-    most = jnp.max(jnp.sum(used.astype(jnp.int32), axis=1))
-    rank_or_none = jnp.where(used, rank.astype(jnp.int32), -1)
     listed = jnp.sum(
         jnp.where(
             rank_or_none[:, None, :] == jnp.arange(CAP)[None, :, None],
@@ -276,34 +366,20 @@
         axis=2,
     )
     ref_rank = jnp.sum(
-        jnp.dot(rank.astype(jnp.bfloat16), place_hot, preferred_element_type=jnp.float32)
-        * member_hot.astype(jnp.float32),
+        jnp.dot(
+            jnp.minimum(rank_or_none, CAP).astype(jnp.bfloat16),
+            hot(place, places, 0),
+            preferred_element_type=jnp.float32,
+        )
+        * hot(member, members, 0).astype(jnp.float32),
         axis=0,
     ).astype(jnp.int32)
     index = jnp.where(member >= 0, member * CAP + jnp.minimum(ref_rank, CAP - 1), 0)
 
-    end_hot = hot(end_value, groups * members * CAP_E, 0)
-    slot_count = jnp.sum(end_hot.astype(jnp.float32), axis=1).astype(jnp.int32)
-    wanted = want_end.reshape(-1)
-    asked = jnp.where(wanted >= 0, wanted + SHIFT * slot_count, -1).reshape(groups, members * CAP_E)
-
-    mine = lax.axis_index("dev")
-    ask_near = lax.dynamic_index_in_dim(
-        want_near.reshape(groups, members, CAP_N), mine, 1, keepdims=False
-    )
-    first = jnp.concatenate(
-        [
-            asked,
-            ask_near,
-            jnp.broadcast_to(most, (groups, LANES - members * CAP_E - CAP_N)),
-        ],
-        1,
-    )
-    first = exchange(first, "grp")
     got_near = first[:, members * CAP_E : members * CAP_E + CAP_N]
     most = jnp.max(first[:, members * CAP_E + CAP_N :])
     passed = jnp.transpose(
-        first[:, : members * CAP_E].reshape(groups, members, CAP_E), (1, 0, 2)
+        first[:, : members * CAP_E].reshape(groups, CAP_E, members), (2, 0, 1)
     ).reshape(members, ends)
     second = jnp.concatenate(
         [
@@ -368,6 +444,7 @@
         )
         message = message.reshape(-1, row_width)
         high = lax.reduce_precision(message, 8, 7)
+        end_hot = hot(end_value, groups * members * CAP_E, 0)
         slot_sum = jnp.dot(
             end_hot, high.astype(jnp.bfloat16), preferred_element_type=jnp.float32
         ) + jnp.dot(
@@ -382,7 +459,7 @@
     )
     elapsed_lanes = jnp.transpose(elapsed, (1, 0, 2)).reshape(K, 1, pairs)
     code = jnp.cos(elapsed_lanes * frequency[None, :, None] + phases[None, :, None])
-    fixed = jnp.broadcast_to(jnp.cos(phases)[:, None], (phases.shape[0], pairs))
+    fixed = jnp.cos(phases)[None, :]
     operands = (
         lanes,
         counted.reshape(1, pairs),
@@ -392,7 +469,7 @@
         jnp.transpose(query_weight),
         jnp.transpose(jnp.concatenate([key_weight, value_weight], 1)),
         jnp.transpose(out_weight),
-        out_bias[:, None],
+        out_bias[None, :],
         jnp.transpose(message_in),
         jnp.transpose(message_out),
     )

time: 177 us -> 170 us (0.960)
  local copies, waits for them, and re-layouts: 18.1 us -> 13.1 us
  other arithmetic: 19.1 us -> 14.9 us
  Pallas kernels: 14.1 us -> 16.5 us
    broadcast_in_dim x3 -> x0, local copies, waits for them, and re-layouts: 3.48 us -> none  [the longest x1 1.48 us: local(): out_bias[:, None]]
    pallas_call x0 -> x1, Pallas kernels: none -> 2.52 us  [local(): pl.pallas_call(request_kernel, out_shape=(jax.ShapeDtypeStruct((groups, L...]
    unnamed x59 -> x50, local copies, waits for them, and re-layouts: 7.26 us -> 7.7 us
where the time goes in v4:
time: 170 us; the launch traced here: 169 us
  waiting for transfers between devices  72 us (42%)
  starting transfers between devices  41.3 us (24%)
  Pallas kernels  16.5 us (10%)
  other arithmetic  14.9 us (9%)
  local copies, waits for them, and re-layouts  13.1 us (8%)
  matrix products  9.78 us (6%)
  between operations  1.77 us (1%)
    all_to_all x5, waiting for transfers between devices, exchange(): return lax.all_to_all(x, axis, split_axis=0, concat_axis=0, tiled=True)  72 us
    all_to_all x5, starting transfers between devices, exchange(): return lax.all_to_all(x, axis, split_axis=0, concat_axis=0, tiled=True)  41.3 us
    pallas_call x1, Pallas kernels, listed_only(): pl.pallas_call(event_kernel, out_shape=(jax.ShapeDtypeStruct((events, 2 *...  14 us
    unnamed x50, local copies, waits for them, and re-layouts  7.7 us
    convert_element_type x1, other arithmetic, local(): code.astype(jnp.bfloat16)  5.4 us
  transfers between devices with their start and end apart: 5, of which 5 were waited for; matrix products, arithmetic and copies ran while one was open for 11% of the time, Pallas kernels for 0%

profile of v4, /device:TPU:1, one launch (start us, length us, event | category | flops | bytes accessed | tf_op | source)
XLA Modules:
  0.0 169.4 jit_solution(3546351141132360632)
XLA Ops:
  0.6 2.5 %request_kernel.1 = (s32[16,128]{1,0:T(8,128)}, s32[32,288]{1,0:T(8,128)}) custom-call(s32[1]{0:T(128)} %bitcast.21.mine, s32[20,128]{1,0:T(8,128)} %bitcast.136, s32[2,128]{1,0:T(2,128)} %bitcast.152, s32[2,128]{1,0:T(2,128)} %bitcast.147, s32[2,512]{1,0:T(2,128)} %bitcast.159, s32[16,512]{1,0:T(8,128)} %bitcast.146), custom_call_target="tpu_custom_call" | custom-call | tf_op jit(solution)/shard_map/request_kernel/pallas_call | solution.py:334
  3.2 10.1 %all-to-all-start.1 = ((s32[16,1,128]{2,1,0:T(1,128)}), s32[16,1,128]{2,1,0:T(1,128)S(1)}, u32[]{:S(2)}, u32[]{:S(2)}) async-start(s32[16,1,128]{2,1,0:T(1,128)} %bitcast.158), calls=%async_computation.1 | async-start | bytes 16384 | tf_op jit(solution)/shard_map/all_to_all | solution.py:38
  13.3 1.4 select_reduce_fusion
  14.7 5.6 %all-to-all-done.1 = s32[16,1,128]{2,1,0:T(1,128)S(1)} async-done(((s32[16,1,128]{2,1,0:T(1,128)}), s32[16,1,128]{2,1,0:T(1,128)S(1)}, u32[]{:S(2)}, u32[]{:S(2)}) %all-to-all-start.1) | async-done | bytes 8224 | tf_op jit(solution)/shard_map/all_to_all | solution.py:38
  20.3 0.7 slice_reduce_fusion.1
  21.1 0.7 broadcast_in_dim.73
  21.9 0.7 add_add_fusion
  22.6 11.4 %all-to-all-start.2 = ((s32[32,1,128]{2,1,0:T(1,128)}), s32[32,1,128]{2,1,0:T(1,128)S(1)}, u32[]{:S(2)}, u32[]{:S(2)}) async-start(s32[32,1,128]{2,1,0:T(1,128)} %bitcast.34), calls=%async_computation.2 | async-start | bytes 32768 | tf_op jit(solution)/shard_map/all_to_all | solution.py:38
  34.0 8.5 %all-to-all-done.2 = s32[32,1,128]{2,1,0:T(1,128)S(1)} async-done(((s32[32,1,128]{2,1,0:T(1,128)}), s32[32,1,128]{2,1,0:T(1,128)S(1)}, u32[]{:S(2)}, u32[]{:S(2)}) %all-to-all-start.2) | async-done | bytes 16416 | tf_op jit(solution)/shard_map/all_to_all | solution.py:38
  43.5 2.5 %fusion.53 = bf16[1280,256]{1,0:T(8,128)(2,1)} fusion(s32[1280]{0:T(1024)S(1)} %eq.107, f32[512,256]{1,0:T(8,128)} %param.22), kind=kOutput, calls=%fused_computation.77 | convolution fusion | flops 336658432 | bytes 1184768 | tf_op jit(solution)/shard_map/dot_general | solution.py:26
  46.0 5.5 %all-to-all-start.3 = ((bf16[16,80,256]{2,1,0:T(8,128)(2,1)}), bf16[16,80,256]{2,1,0:T(8,128)(2,1)S(1)}, u32[]{:S(2)}, u32[]{:S(2)}) async-start(bf16[16,80,256]{2,1,0:T(8,128)(2,1)} %bitcast.43), calls=%async_computation.3 | async-start | bytes 1310720 | tf_op jit(solution)/shard_map/all_to_all | solution.py:38
  51.5 20.0 %all-to-all-done.3 = bf16[16,80,256]{2,1,0:T(8,128)(2,1)S(1)} async-done(((bf16[16,80,256]{2,1,0:T(8,128)(2,1)}), bf16[16,80,256]{2,1,0:T(8,128)(2,1)S(1)}, u32[]{:S(2)}, u32[]{:S(2)}) %all-to-all-start.3) | async-done | bytes 655392 | tf_op jit(solution)/shard_map/all_to_all | solution.py:38
  72.6 1.2 fusion.50
  73.8 1.7 %add_convert_fusion = bf16[32,88,256]{2,1,0:T(8,128)(2,1)} fusion(f32[32,88,256]{2,1,0:T(8,128)S(1)} %fusion.50, bf16[32,32,256]{2,1,0:T(8,128)(2,1)S(1)} %reshape.234, s32[32,88]{1,0:T(8,128)S(1)} %get-tuple-element.115), kind=kOutput, calls=%fused_computation.71 | convolution fusion | flops 47669248 | bytes 4860928 | tf_op jit(solution)/shard_map/dcp,dpw->dcw/dot_general | solution.py:409
  75.6 4.1 %all-to-all-start.4 = ((bf16[32,88,256]{2,1,0:T(8,128)(2,1)}), bf16[32,88,256]{2,1,0:T(8,128)(2,1)S(1)}, u32[]{:S(2)}, u32[]{:S(2)}) async-start(bf16[32,88,256]{2,1,0:T(8,128)(2,1)} %add_convert_fusion), calls=%async_computation.4 | async-start | bytes 2883584 | tf_op jit(solution)/shard_map/all_to_all | solution.py:38
  79.9 0.7 fusion.61
  81.3 0.6 copy.134
  82.3 1.8 %copy.128 = bf16[512,256]{0,1:T(8,128)(2,1)} copy(bf16[512,256]{1,0:T(8,128)(2,1)} %param.35) | data formatting | bytes 524288 | tf_op args[13]
  84.1 1.8 %copy.129 = bf16[512,256]{0,1:T(8,128)(2,1)} copy(bf16[512,256]{1,0:T(8,128)(2,1)} %param.37) | data formatting | bytes 524288 | tf_op args[15]
  85.9 0.8 copy.125
  86.7 1.7 copy.130
  89.1 0.6 cosine_convert_fusion.3
  89.7 5.4 %cosine_convert_fusion.2 = bf16[10,128,256]{2,1,0:T(8,128)(2,1)S(1)} fusion(f32[128]{0:T(128)} %param.31, f32[128]{0:T(128)} %param.30, f32[10,256]{1,0:T(8,128)} %bitcast.144), kind=kLoop, calls=%fused_computation.83 | loop fusion | flops 983040 | bytes 666624 | tf_op jit(solution)/shard_map/convert_element_type | solution.py:467
  95.1 0.7 slice_reduce_fusion
  96.5 19.0 %all-to-all-done.4 = bf16[32,88,256]{2,1,0:T(8,128)(2,1)S(1)} async-done(((bf16[32,88,256]{2,1,0:T(8,128)(2,1)}), bf16[32,88,256]{2,1,0:T(8,128)(2,1)S(1)}, u32[]{:S(2)}, u32[]{:S(2)}) %all-to-all-start.4) | async-done | bytes 1441824 | tf_op jit(solution)/shard_map/all_to_all | solution.py:38
  115.4 14.0 %conditional.1 = ((bf16[128,512]{1,0:T(8,128)(2,1)}, bf16[1024,256]{1,0:T(8,128)(2,1)})) conditional(s32[]{:T(128)} %convert_element_type.81, (bf16[32,88,256]{2,1,0:T(8,128)(2,1)S(1)}, s32[2,128]{1,0:T(2,128)}, s32[2,128]{1,0:T(2,128)}, bf16[128]{0:T(256)(128)(2,1)}, f32[256]{0:T(256)}, /*index=5*/s32[11,256]{1,0:T(8,128)}, ...), branch_computations={%region_5.6_spmd, %region_6.13_spmd} | conditional | flops 1517661824 | bytes 61769664 | solution.py:492
  115.4 14.0 %event_kernel.1 = (bf16[128,512]{1,0:T(8,128)(2,1)}, bf16[1024,256]{1,0:T(8,128)(2,1)}) custom-call(bf16[2816,256]{1,0:T(8,128)(2,1)S(1)} %bitcast.116, s32[11,256]{1,0:T(8,128)} %get-tuple-element.62.lanes, s32[1,256]{1,0:T(1,128)} %bitcast.151, s32[1,256]{1,0:T(1,128)} %bitcast.155, bf16[10,128,256]{2,1,0:T(8,128)(2,1)S(1)} %get-tuple-element.65.code, ...), custom_call_target="tpu_custom_call" | custom-call | tf_op jit(solution)/shard_map/cond/branch_0_fun/event_kernel/pallas_call | solution.py:478
  129.4 2.1 %reshape.239 = bf16[512,2,256]{2,1,0:T(2,128)(2,1)} reshape(bf16[1024,256]{1,0:T(8,128)(2,1)} %get-tuple-element.97) | data formatting | bytes 1048576 | tf_op jit(solution)/shard_map/reshape | solution.py:494
  131.5 10.3 %all-to-all-start.5 = ((bf16[512,2,256]{2,1,0:T(2,128)(2,1)}), bf16[512,2,256]{2,1,0:T(2,128)(2,1)S(1)}, u32[]{:S(2)}, u32[]{:S(2)}) async-start(bf16[512,2,256]{2,1,0:T(2,128)(2,1)} %reshape.239), calls=%async_computation.5 | async-start | bytes 1048576 | tf_op jit(solution)/shard_map/all_to_all | solution.py:38
  144.4 18.9 %all-to-all-done.5 = bf16[512,2,256]{2,1,0:T(2,128)(2,1)S(1)} async-done(((bf16[512,2,256]{2,1,0:T(2,128)(2,1)}), bf16[512,2,256]{2,1,0:T(2,128)(2,1)S(1)}, u32[]{:S(2)}, u32[]{:S(2)}) %all-to-all-start.5) | async-done | bytes 524320 | tf_op jit(solution)/shard_map/all_to_all | solution.py:38
  163.6 3.2 %fusion.60 = f32[512,768]{1,0:T(8,128)} fusion(bf16[256,768]{1,0:T(8,128)(2,1)} %param.39, bf16[1024,256]{1,0:T(8,128)(2,1)S(1)} %reshape.240, s32[1024]{0:T(1024)S(1)} %select_n.80, f32[512]{0:T(512)} %convert_maximum_fusion), kind=kOutput, calls=%fused_computation.87 | convolution fusion | flops 470548480 | bytes 2496512 | tf_op jit(solution)/shard_map/dot_general | solution.py:281
  166.8 2.6 %fusion.68 = f32[512,256]{1,0:T(8,128)} fusion(f32[512,256]{1,0:T(8,128)S(1)} %copy-done.1, f32[512,768]{1,0:T(8,128)S(1)} %fusion.82, f32[512,768]{1,0:T(8,128)} %fusion.60, f32[256]{0:T(256)S(1)} %get-tuple-element.118, f32[256]{0:T(256)S(1)} %get-tuple-element.119, f32[256]{0:T(256)S(1)} %get-tuple-element.117, pred[512]{0:T(512)(128)(4,1)S(1)} %copy-done.28), kind=kLoop, calls=%fused_computation.95 | loop fusion | flops 2359296 | bytes 4197888 | tf_op jit(solution)/shard_map/jit(_where)/select_n | solution.py:297
  (88 shorter events, 6.8 us)
Async XLA Ops:
  0.6 141.2 %copy-start = (bf16[256,768]{1,0:T(8,128)(2,1)S(1)}, bf16[256,768]{1,0:T(8,128)(2,1)}, u32[]{:S(2)}) copy-start(bf16[256,768]{1,0:T(8,128)(2,1)} %param.40) | copy-start | bytes 1179652
  3.2 17.1 %all-to-all-start.1 = ((s32[16,1,128]{2,1,0:T(1,128)}), s32[16,1,128]{2,1,0:T(1,128)S(1)}, u32[]{:S(2)}, u32[]{:S(2)}) async-start(s32[16,1,128]{2,1,0:T(1,128)} %bitcast.158), calls=%async_computation.1 | async-start | bytes 16384 | tf_op jit(solution)/shard_map/all_to_all | solution.py:38
  22.6 20.0 %all-to-all-start.2 = ((s32[32,1,128]{2,1,0:T(1,128)}), s32[32,1,128]{2,1,0:T(1,128)S(1)}, u32[]{:S(2)}, u32[]{:S(2)}) async-start(s32[32,1,128]{2,1,0:T(1,128)} %bitcast.34), calls=%async_computation.2 | async-start | bytes 32768 | tf_op jit(solution)/shard_map/all_to_all | solution.py:38
  43.2 28.4 %copy-start.10 = (s32[32,32]{0,1:T(8,128)}, s32[32,32]{0,1:T(8,128)S(1)}, u32[]{:S(2)}) copy-start(s32[32,32]{0,1:T(8,128)S(1)} %copy.116) | copy-start | bytes 12292
  46.0 25.5 %all-to-all-start.3 = ((bf16[16,80,256]{2,1,0:T(8,128)(2,1)}), bf16[16,80,256]{2,1,0:T(8,128)(2,1)S(1)}, u32[]{:S(2)}, u32[]{:S(2)}) async-start(bf16[16,80,256]{2,1,0:T(8,128)(2,1)} %bitcast.43), calls=%async_computation.3 | async-start | bytes 1310720 | tf_op jit(solution)/shard_map/all_to_all | solution.py:38
  75.6 4.2 %copy-start.22 = (s32[128,2]{0,1:T(2,128)S(1)}, s32[128,2]{0,1:T(2,128)}, u32[]{:S(2)}) copy-start(s32[128,2]{0,1:T(2,128)} %param.27) | copy-start | bytes 3076
  75.6 4.2 %copy-start.24 = (s32[128,2]{0,1:T(2,128)S(1)}, s32[128,2]{0,1:T(2,128)}, u32[]{:S(2)}) copy-start(s32[128,2]{0,1:T(2,128)} %param.25) | copy-start | bytes 3076
  75.6 4.2 %copy-start.15 = (s32[128,20]{0,1:T(8,128)S(1)}, s32[128,20]{0,1:T(8,128)}, u32[]{:S(2)}) copy-start(s32[128,20]{0,1:T(8,128)} %param.26) | copy-start | bytes 30724
  75.6 4.3 %copy-start.19 = (s32[32,288]{1,0:T(8,128)S(1)}, s32[32,288]{1,0:T(8,128)}, u32[]{:S(2)}) copy-start(s32[32,288]{1,0:T(8,128)} %get-tuple-element.96) | copy-start | bytes 110596
  75.6 5.2 %copy-start.26 = (s32[128,20]{0,1:T(8,128)S(1)}, s32[128,20]{0,1:T(8,128)}, u32[]{:S(2)}) copy-start(s32[128,20]{0,1:T(8,128)} %param.29) | copy-start | bytes 30724
  75.6 5.2 %copy-start.33 = (s32[128]{0:T(128)S(1)}, s32[128]{0:T(128)}, u32[]{:S(2)}) copy-start(s32[128]{0:T(128)} %param.28) | copy-start | bytes 1540
  75.6 6.4 %copy-start.4 = (bf16[384,256]{1,0:T(8,128)(2,1)S(1)}, bf16[384,256]{1,0:T(8,128)(2,1)}, u32[]{:S(2)}) copy-start(bf16[384,256]{1,0:T(8,128)(2,1)} %param.33) | copy-start | bytes 589828
  75.6 6.5 %copy-start.2 = (bf16[384,256]{1,0:T(8,128)(2,1)S(1)}, bf16[384,256]{1,0:T(8,128)(2,1)}, u32[]{:S(2)}) copy-start(bf16[384,256]{1,0:T(8,128)(2,1)} %param.34) | copy-start | bytes 589828
  75.6 39.8 %all-to-all-start.4 = ((bf16[32,88,256]{2,1,0:T(8,128)(2,1)}), bf16[32,88,256]{2,1,0:T(8,128)(2,1)S(1)}, u32[]{:S(2)}, u32[]{:S(2)}) async-start(bf16[32,88,256]{2,1,0:T(8,128)(2,1)} %add_convert_fusion), calls=%async_computation.4 | async-start | bytes 2883584 | tf_op jit(solution)/shard_map/all_to_all | solution.py:38
  79.7 6.2 %copy-start.6 = (bf16[384,256]{1,0:T(8,128)(2,1)S(1)}, bf16[384,256]{1,0:T(8,128)(2,1)}, u32[]{:S(2)}) copy-start(bf16[384,256]{1,0:T(8,128)(2,1)} %param.32) | copy-start | bytes 589828
  79.9 0.8 copy-start.16
  79.9 0.9 copy-start.20
  80.6 8.5 %copy-start.29 = (f32[128]{0:T(128)S(1)}, f32[128]{0:T(128)}, u32[]{:S(2)}) copy-start(f32[128]{0:T(128)} %param.31) | copy-start | bytes 1540
  80.7 0.6 copy-start.13
  129.4 12.4 %copy-start.27 = (f32[768]{0:T(1024)S(1)}, f32[768]{0:T(1024)}, u32[]{:S(2)}) copy-start(f32[768]{0:T(1024)} %param.41) | copy-start | bytes 9220
  129.4 12.5 %copy-start.1 = (f32[512,256]{1,0:T(8,128)S(1)}, f32[512,256]{1,0:T(8,128)}, u32[]{:S(2)}) copy-start(f32[512,256]{1,0:T(8,128)} %param.22) | copy-start | bytes 1572868
  131.5 10.7 %copy-start.11 = (s32[32,32]{0,1:T(8,128)S(1)}, s32[32,32]{0,1:T(8,128)}, u32[]{:S(2)}) copy-start(s32[32,32]{0,1:T(8,128)} %copy-done.10) | copy-start | bytes 12292
  131.5 11.1 %copy-start.18 = (s32[32,32]{1,0:T(8,128)S(1)}, s32[32,32]{1,0:T(8,128)}, u32[]{:S(2)}) copy-start(s32[32,32]{1,0:T(8,128)} %get-tuple-element.105) | copy-start | bytes 12292
  131.5 31.8 %all-to-all-start.5 = ((bf16[512,2,256]{2,1,0:T(2,128)(2,1)}), bf16[512,2,256]{2,1,0:T(2,128)(2,1)S(1)}, u32[]{:S(2)}, u32[]{:S(2)}) async-start(bf16[512,2,256]{2,1,0:T(2,128)(2,1)} %reshape.239), calls=%async_computation.5 | async-start | bytes 1048576 | tf_op jit(solution)/shard_map/all_to_all | solution.py:38
  163.6 3.2 %copy-start.28 = (pred[512]{0:T(512)(128)(4,1)S(1)}, pred[512]{0:T(512)(128)(4,1)}, u32[]{:S(2)}) copy-start(pred[512]{0:T(512)(128)(4,1)} %convert_compare_fusion) | copy-start | bytes 1540

commit v5 on v4

--- a/solution.py
+++ b/solution.py
@@ -11,7 +11,9 @@
 K = 10
 CAP_E = 2
 CAP_N = 16
-CAP = 88
+CAP = 87
+CAP_SUM = 24
+CAP_OWN = 31
 LANES = 128
 SHIFT = 65536
 
@@ -32,6 +34,24 @@
     width = slots.bit_length() - 1
     owner = value >> width
     return owner & (members - 1), ((owner >> (members.bit_length() - 1)) << width) | (value & (slots - 1))
+
+
+def ranks(marks):
+    size = marks.shape[1]
+    before = (jnp.arange(size)[:, None] < jnp.arange(size)[None, :]).astype(jnp.bfloat16)
+    rank = jnp.dot(marks.astype(jnp.bfloat16), before, preferred_element_type=jnp.float32)
+    full = jnp.sum(marks.astype(jnp.int32), axis=1) > CAP_OWN
+    return jnp.where(marks, rank.astype(jnp.int32), -1), full.astype(jnp.float32)
+
+
+def listing(rank, value, size):
+    found = rank[:, None, :] == jnp.arange(size)[None, :, None]
+    return jnp.sum(jnp.where(found, value[:, None, :] + 1, 0), axis=2) - 1
+
+
+def flagged(rows, flag):
+    last = jnp.arange(rows.shape[1])[None, :, None] == rows.shape[1] - 1
+    return jnp.where(last, flag.astype(rows.dtype), rows)
 
 
 def exchange(x, axis):
@@ -134,7 +154,13 @@
     before = ones(numbers(places, places) < lanes(places, places))
     rank = jnp.dot(used, before, preferred_element_type=jnp.float32)
     rank_or_none[...] = jnp.where(uses > 0, rank, -1.0).astype(jnp.int32)
-    most = jnp.max(jnp.sum(used.astype(jnp.float32), axis=1, keepdims=True)).astype(jnp.int32)
+    most = jnp.max(jnp.sum(used.astype(jnp.float32), axis=1, keepdims=True))
+    most_ends = jnp.max(
+        jnp.sum(
+            jnp.where(lanes(members, places) >= block, used.astype(jnp.float32), 0.0), axis=1, keepdims=True
+        )
+    )
+    most = jnp.where(most_ends > CAP_SUM, float(places), most).astype(jnp.int32)
     times = across(jnp.concatenate(group_pieces, 1), jnp.concatenate(lane_pieces, 1)).astype(jnp.int32)
 
     group = lanes(groups, owners) >> members.bit_length() - 1
@@ -374,7 +400,12 @@
         * hot(member, members, 0).astype(jnp.float32),
         axis=0,
     ).astype(jnp.int32)
-    index = jnp.where(member >= 0, member * CAP + jnp.minimum(ref_rank, CAP - 1), 0)
+    index = jnp.where(member >= 0, member * (CAP + 1) + jnp.minimum(ref_rank, CAP), 0)
+    near_used = jnp.sum((rank_or_none[:, :block] >= 0).astype(jnp.int32), axis=1)
+    sum_slot = end_member * CAP_SUM + ref_rank[2 * K * events :]
+    sum_slot = sum_slot - jnp.sum(
+        jnp.where(end_member[None, :] == jnp.arange(members)[:, None], near_used[:, None], 0), axis=0
+    )
 
     got_near = first[:, members * CAP_E : members * CAP_E + CAP_N]
     most = jnp.max(first[:, members * CAP_E + CAP_N :])
@@ -397,29 +428,65 @@
     got_end = jnp.where(got_code >= 0, got_code & (SHIFT - 1), -1)
     got_count = jnp.where(got_code >= 0, got_code >> 16, 0)
 
-    row_index = jnp.concatenate([got_near, got_end], 1).reshape(-1)
-    rows = exchange(pick(row_index, mem_half).reshape(groups, -1, row_width), "grp")
-    near_block = rows[:, :CAP_N].reshape(block, row_width)
-    end_part = jnp.transpose(
-        rows[:, CAP_N:].reshape(groups, members, CAP_E, row_width), (1, 0, 2, 3)
-    ).reshape(members, ends, row_width)
-    near_part = jnp.dot(
-        hot(got_listed.reshape(-1), block, 1), near_block, preferred_element_type=jnp.float32
-    ).reshape(members, CAP, row_width)
-    listed_ends = jnp.einsum(
-        "dcp,dpw->dcw",
-        hot(got_listed - block, ends, 2),
-        end_part,
+    own_rank, own_flag = ranks(got_count > 0)
+    own_list = listing(own_rank, got_end, CAP_OWN)
+    flag = jnp.max(own_flag)
+    marked = jnp.any(
+        got_listed[:, None, :] == block + jnp.arange(ends)[None, :, None], axis=2
+    )
+    place_rank = jnp.dot(
+        marked.astype(jnp.bfloat16),
+        (jnp.arange(ends)[:, None] < jnp.arange(ends)[None, :]).astype(jnp.bfloat16),
         preferred_element_type=jnp.float32,
-    )
-    table = exchange((near_part + listed_ends).astype(jnp.bfloat16), "dev")
-    table = table.reshape(members * CAP, row_width)
+    ).astype(jnp.int32)
+
+    def by_group(x):
+        return jnp.transpose(x.reshape(members, groups, CAP_E), (1, 0, 2)).reshape(groups, -1)
+
+    relay_rank, _ = ranks(by_group(marked))
+    sum_row = jnp.arange(members)[:, None] * CAP_SUM + jnp.minimum(place_rank, CAP_SUM - 1)
+    relay_list = listing(relay_rank, by_group(sum_row), CAP_OWN + 1)
+    per_group = CAP_N + CAP_OWN + 1
+    end_row = jnp.arange(groups)[:, None] * per_group + CAP_N + jnp.minimum(relay_rank, CAP_OWN - 1)
+    end_row = jnp.transpose(end_row.reshape(groups, members, CAP_E), (1, 0, 2)).reshape(members, ends)
+    listed_row = jnp.where(
+        got_listed < block,
+        (got_listed // CAP_N) * per_group + got_listed % CAP_N,
+        jnp.sum(
+            jnp.where(
+                got_listed[:, :, None] == block + jnp.arange(ends)[None, None, :],
+                end_row[:, None, :],
+                0,
+            ),
+            axis=2,
+        ),
+    )
+    listed_row = jnp.concatenate([listed_row, jnp.full((members, 1), -1, jnp.int32)], 1)
+
+    row_index = jnp.concatenate([got_near, own_list, jnp.full((groups, 1), -1, jnp.int32)], 1)
+    rows = pick(row_index.reshape(-1), mem_half).reshape(groups, per_group, row_width)
+    rows = exchange(flagged(rows, flag), "grp")
+    flag = jnp.max(rows[:, per_group - 1, 0].astype(jnp.float32))
+    rows = rows.reshape(groups * per_group, row_width)
+    table = pick(listed_row.reshape(-1), rows).reshape(members, CAP + 1, row_width)
+    table = exchange(flagged(table, flag), "dev")
+    flag = jnp.max(table[:, CAP, 0].astype(jnp.float32))
+    table = table.reshape(members * (CAP + 1), row_width)
 
     elapsed = (event_time[None, :] - jnp.transpose(near_time)).astype(jnp.float32)
     elapsed = elapsed.reshape(2, K, events)
 
     def whole():
-        full = jnp.broadcast_to(near_block[None], (members, block, row_width))
+        all_rows = pick(
+            jnp.concatenate([got_near, got_end], 1).reshape(-1), mem_half
+        ).reshape(groups, -1, row_width)
+        all_rows = exchange(all_rows, "grp")
+        full = jnp.broadcast_to(
+            all_rows[:, :CAP_N].reshape(1, block, row_width), (members, block, row_width)
+        )
+        end_part = jnp.transpose(
+            all_rows[:, CAP_N:].reshape(groups, members, CAP_E, row_width), (1, 0, 2, 3)
+        ).reshape(members, ends, row_width)
         full = exchange(jnp.concatenate([full, end_part], 1), "dev")
         fetched = jnp.take(
             full.reshape(members * places, row_width),
@@ -450,7 +517,13 @@
         ) + jnp.dot(
             end_hot, (message - high).astype(jnp.bfloat16), preferred_element_type=jnp.float32
         )
-        return jnp.concatenate([embedded[0], embedded[1]], 1), slot_sum.astype(jnp.bfloat16)
+        news = exchange(
+            slot_sum.astype(jnp.bfloat16).reshape(groups * members, CAP_E, row_width), ("grp", "dev")
+        ).reshape(-1, row_width)
+        totals = jnp.dot(
+            hot(got_end.reshape(-1), nodes, 0), news, preferred_element_type=jnp.float32
+        )
+        return jnp.concatenate([embedded[0], embedded[1]], 1), totals
 
     pairs = 2 * events
     near_lanes = jnp.transpose(index[: 2 * K * events].reshape(2, K, events), (1, 0, 2))
@@ -463,7 +536,7 @@
     operands = (
         lanes,
         counted.reshape(1, pairs),
-        end_value.reshape(1, pairs),
+        sum_slot.reshape(1, pairs),
         code.astype(jnp.bfloat16),
         fixed.astype(jnp.bfloat16),
         jnp.transpose(query_weight),
@@ -475,11 +548,11 @@
     )
 
     def listed_only():
-        return pl.pallas_call(
+        embedded, sums = pl.pallas_call(
             event_kernel,
             out_shape=(
                 jax.ShapeDtypeStruct((events, 2 * row_width), jnp.bfloat16),
-                jax.ShapeDtypeStruct((groups * members * CAP_E, row_width), jnp.bfloat16),
+                jax.ShapeDtypeStruct((members * CAP_SUM, row_width), jnp.bfloat16),
             ),
             scratch_shapes=[
                 pltpu.VMEM((row_width, table.shape[0]), jnp.bfloat16),
@@ -488,14 +561,19 @@
             ],
             name="event_kernel",
         )(table, *operands)
-
-    embedded, slot_sum = lax.cond(most > CAP, whole, listed_only)
-    news = exchange(
-        slot_sum.reshape(groups * members, CAP_E, row_width), ("grp", "dev")
-    ).reshape(-1, row_width)
+        sums = exchange(sums.reshape(members, CAP_SUM, row_width), "dev")
+        sums = pick(relay_list.reshape(-1), sums.reshape(members * CAP_SUM, row_width))
+        news = exchange(sums.reshape(groups, CAP_OWN + 1, row_width), "grp")
+        owned = jnp.concatenate([own_list, jnp.full((groups, 1), -1, jnp.int32)], 1)
+        totals = jnp.dot(
+            hot(owned.reshape(-1), nodes, 0),
+            news.reshape(-1, row_width),
+            preferred_element_type=jnp.float32,
+        )
+        return embedded, totals
+
+    embedded, totals = lax.cond((most > CAP) | (flag > 0), whole, listed_only)
     owned = got_end.reshape(-1)
-    owned_hot = hot(owned, nodes, 0)
-    totals = jnp.dot(owned_hot, news, preferred_element_type=jnp.float32)
     counts = jnp.sum(
         jnp.where(
             owned[None, :] == jnp.arange(nodes)[:, None], got_count.reshape(1, -1), 0

time: 170 us -> 180 us (1.059)
  waiting for transfers between devices: 72 us -> 49.8 us
  other arithmetic: 14.9 us -> 33.3 us
  starting transfers between devices: 41.3 us -> 46.9 us
  local copies, waits for them, and re-layouts: 13.1 us -> 18.4 us
    all_to_all x5 -> x6, waiting for transfers between devices: 72 us -> 49.8 us  [exchange(): return lax.all_to_all(x, axis, split_axis=0, concat_axis=0, tiled=True)]
    all_to_all x5 -> x6, starting transfers between devices: 41.3 us -> 46.9 us  [exchange(): return lax.all_to_all(x, axis, split_axis=0, concat_axis=0, tiled=True)]
    reduce_sum x0 -> x6, other arithmetic: none -> 4.8 us  [the longest x2 1.92 us: listing(): return jnp.sum(jnp.where(found, value[:, None, :] + 1, 0), axis=2) - 1]
    unnamed x50 -> x70, local copies, waits for them, and re-layouts: 7.7 us -> 4.01 us
    reshape x5 -> x4, local copies, waits for them, and re-layouts: 3.26 us -> 0.18 us  [the longest x2 0.1 us: by_group(): jnp.transpose(x.reshape(members, groups, CAP_E), (1, 0, 2))]
    select_n x3 -> x4, other arithmetic: 0.61 us -> 3.49 us  [the longest x2 3.39 us: flagged(): return jnp.where(last, flag.astype(rows.dtype), rows)]
    select_n x3 -> x2, local copies, waits for them, and re-layouts: 0.42 us -> 3.29 us  [local(): got_count = jnp.where(got_code >= 0, got_code >> 16, 0)]
    select_n x5 -> x2, local copies, waits for them, and re-layouts: 0.57 us -> 3.29 us  [local(): got_end = jnp.where(got_code >= 0, got_code & SHIFT - 1, -1)]
  transfers between devices with their start and end apart: 5 -> 6, of which waited for: 5 -> 6; matrix products, arithmetic and copies ran while one was open for 11% -> 22% of each run, Pallas kernels for 0% -> 0%
where the time goes in v5:
time: 180 us; the launch traced here: 178 us
  waiting for transfers between devices  49.8 us (28%)
  starting transfers between devices  46.9 us (26%)
  other arithmetic  33.3 us (18%)
  local copies, waits for them, and re-layouts  18.4 us (10%)
  Pallas kernels  16.7 us (9%)
  matrix products  10.9 us (6%)
  between operations  2.49 us (1%)
    all_to_all x6, waiting for transfers between devices, exchange(): return lax.all_to_all(x, axis, split_axis=0, concat_axis=0, tiled=True)  49.8 us
    all_to_all x6, starting transfers between devices, exchange(): return lax.all_to_all(x, axis, split_axis=0, concat_axis=0, tiled=True)  46.9 us
    pallas_call x1, Pallas kernels, listed_only(): pl.pallas_call(event_kernel, out_shape=(jax.ShapeDtypeStruct((events, 2 *...  14.1 us
    convert_element_type x1, other arithmetic, local(): code.astype(jnp.bfloat16)  5.25 us
    unnamed x70, local copies, waits for them, and re-layouts  4.01 us
    dot_general x3, matrix products, pick(): jnp.dot(hot(index, table.shape[0], 1), table, preferred_element_type=jnp....  3.63 us
  transfers between devices with their start and end apart: 6, of which 6 were waited for; matrix products, arithmetic and copies ran while one was open for 22% of the time, Pallas kernels for 0%

profile of v5, /device:TPU:1, one launch (start us, length us, event | category | flops | bytes accessed | tf_op | source)
XLA Modules:
  0.0 178.4 jit_solution(2394260919988529921)
XLA Ops:
  0.7 2.5 %request_kernel.1 = (s32[16,128]{1,0:T(8,128)}, s32[32,288]{1,0:T(8,128)}) custom-call(s32[1]{0:T(128)} %bitcast.29.mine, s32[20,128]{1,0:T(8,128)} %bitcast.164, s32[2,128]{1,0:T(2,128)} %bitcast.182, s32[2,128]{1,0:T(2,128)} %bitcast.177, s32[2,512]{1,0:T(2,128)} %bitcast.189, s32[16,512]{1,0:T(8,128)} %bitcast.176), custom_call_target="tpu_custom_call" | custom-call | tf_op jit(solution)/shard_map/request_kernel/pallas_call | solution.py:360
  3.2 10.1 %all-to-all-start.5 = ((s32[16,1,128]{2,1,0:T(1,128)}), s32[16,1,128]{2,1,0:T(1,128)S(1)}, u32[]{:S(2)}, u32[]{:S(2)}) async-start(s32[16,1,128]{2,1,0:T(1,128)} %bitcast.187), calls=%async_computation.5 | async-start | bytes 16384 | tf_op jit(solution)/shard_map/all_to_all | solution.py:58
  15.4 2.4 %select_reduce_fusion.2 = s32[32,87]{0,1:T(8,128)S(1)} fusion(s32[32,288]{1,0:T(8,128)} %get-tuple-element.176), kind=kLoop, calls=%fused_computation.92 | loop fusion | flops 2402592 | bytes 48000 | tf_op jit(solution)/shard_map/reduce_sum | solution.py:386
  18.5 1.5 fusion.65
  22.6 11.4 %all-to-all-start.6 = ((s32[32,1,128]{2,1,0:T(1,128)}), s32[32,1,128]{2,1,0:T(1,128)S(1)}, u32[]{:S(2)}, u32[]{:S(2)}) async-start(s32[32,1,128]{2,1,0:T(1,128)} %bitcast.42), calls=%async_computation.6 | async-start | bytes 32768 | tf_op jit(solution)/shard_map/all_to_all | solution.py:58
  34.2 8.4 %all-to-all-done.6 = s32[32,1,128]{2,1,0:T(1,128)S(1)} async-done(((s32[32,1,128]{2,1,0:T(1,128)}), s32[32,1,128]{2,1,0:T(1,128)S(1)}, u32[]{:S(2)}, u32[]{:S(2)}) %all-to-all-start.6) | async-done | bytes 16416 | tf_op jit(solution)/shard_map/all_to_all | solution.py:58
  46.1 1.5 broadcast_select_fusion.1
  47.6 8.5 %all-to-all-start.7 = ((bf16[16,48,256]{2,1,0:T(8,128)(2,1)}), bf16[16,48,256]{2,1,0:T(8,128)(2,1)S(1)}, u32[]{:S(2)}, u32[]{:S(2)}) async-start(bf16[16,48,256]{2,1,0:T(8,128)(2,1)} %broadcast_select_fusion.1), calls=%async_computation.7 | async-start | bytes 786432 | tf_op jit(solution)/shard_map/all_to_all | solution.py:58
  59.3 11.3 %all-to-all-done.7 = bf16[16,48,256]{2,1,0:T(8,128)(2,1)S(1)} async-done(((bf16[16,48,256]{2,1,0:T(8,128)(2,1)}), bf16[16,48,256]{2,1,0:T(8,128)(2,1)S(1)}, u32[]{:S(2)}, u32[]{:S(2)}) %all-to-all-start.7) | async-done | bytes 393248 | tf_op jit(solution)/shard_map/all_to_all | solution.py:58
  70.7 2.1 %fusion.61 = bf16[2816,256]{1,0:T(8,128)(2,1)S(1)} fusion(bf16[768,256]{1,0:T(8,128)(2,1)S(1)} %bitcast.147, s32[2816]{0:T(1024)S(1)} %eq.226), kind=kOutput, calls=%fused_computation.94 | convolution fusion | flops 1110179840 | bytes 1846272 | tf_op jit(solution)/shard_map/dot_general | solution.py:28
  73.4 1.9 %broadcast_select_fusion = bf16[32,88,256]{2,1,0:T(8,128)(2,1)} fusion(bf16[32,88,256]{2,1,0:T(8,128)(2,1)S(1)} %bitcast.137, pred[88]{0:T(512)(128)(4,1)S(1)} %iota_compare_fusion.39, bf16[]{:T(256)} %slice_reduce_fusion.2), kind=kLoop, calls=%fused_computation.102 | loop fusion | flops 720896 | bytes 2883674 | tf_op jit(solution)/shard_map/jit(_where)/select_n | solution.py:54
  75.3 4.1 %all-to-all-start.8 = ((bf16[32,88,256]{2,1,0:T(8,128)(2,1)}), bf16[32,88,256]{2,1,0:T(8,128)(2,1)S(1)}, u32[]{:S(2)}, u32[]{:S(2)}) async-start(bf16[32,88,256]{2,1,0:T(8,128)(2,1)} %broadcast_select_fusion), calls=%async_computation.8 | async-start | bytes 2883584 | tf_op jit(solution)/shard_map/all_to_all | solution.py:58
  86.4 5.3 %cosine_convert_fusion.2 = bf16[10,128,256]{2,1,0:T(8,128)(2,1)} fusion(f32[128]{0:T(128)S(1)} %copy-done.41, f32[128]{0:T(128)S(1)} %copy-done.43, f32[10,256]{1,0:T(8,128)S(1)} %bitcast.173), kind=kLoop, calls=%fused_computation.103 | loop fusion | flops 983040 | bytes 666624 | tf_op jit(solution)/shard_map/convert_element_type | solution.py:540
  91.7 1.3 fusion.107
  93.7 1.4 copy.237
  95.1 1.6 copy.216
  96.7 1.7 select_n.120
  98.4 1.6 copy.217
  100.0 1.7 select_n.122
  103.1 1.3 broadcast_compare_fusion.1
  107.0 8.8 %all-to-all-done.8 = bf16[32,88,256]{2,1,0:T(8,128)(2,1)S(1)} async-done(((bf16[32,88,256]{2,1,0:T(8,128)(2,1)}), bf16[32,88,256]{2,1,0:T(8,128)(2,1)S(1)}, u32[]{:S(2)}, u32[]{:S(2)}) %all-to-all-start.8) | async-done | bytes 1441824 | tf_op jit(solution)/shard_map/all_to_all | solution.py:58
  119.1 56.4 %conditional.1 = (bf16[128,512]{1,0:T(8,128)(2,1)}, f32[512,256]{1,0:T(8,128)}) conditional(s32[]{:T(128)} %convert_element_type.128, (bf16[32,88,256]{2,1,0:T(8,128)(2,1)S(1)}, s32[2,128]{1,0:T(2,128)}, s32[256]{0:T(256)}, s32[2816]{0:T(1024)}, s32[2,128]{1,0:T(2,128)}, /*index=5*/s32[32,256]{1,0:T(8,128)}, s32[32,256]{1,0:T(8,128)}, ...), branch_computations={%region_12.16_spmd, %region_16.23_spmd} | conditional | flops 2123152256 | bytes 73265176 | solution.py:575
  121.5 1.3 add_subtract_fusion
  122.8 14.1 %event_kernel.1 = (bf16[128,512]{1,0:T(8,128)(2,1)}, bf16[768,256]{1,0:T(8,128)(2,1)}) custom-call(bf16[2816,256]{1,0:T(8,128)(2,1)S(1)} %bitcast.135, s32[11,256]{1,0:T(8,128)} %get-tuple-element.128.lanes, s32[1,256]{1,0:T(1,128)} %bitcast.181, s32[1,256]{1,0:T(1,128)} %bitcast.188, bf16[10,128,256]{2,1,0:T(8,128)(2,1)} %get-tuple-element.136.code, ...), custom_call_target="tpu_custom_call" | custom-call | tf_op jit(solution)/shard_map/cond/branch_0_fun/event_kernel/pallas_call | solution.py:551
  136.9 6.2 %all-to-all-start = ((bf16[32,24,256]{2,1,0:T(8,128)(2,1)}), bf16[32,24,256]{2,1,0:T(8,128)(2,1)S(1)}, u32[]{:S(2)}, u32[]{:S(2)}) async-start(bf16[32,24,256]{2,1,0:T(8,128)(2,1)} %bitcast.153), calls=%async_computation | async-start | bytes 786432 | tf_op jit(solution)/shard_map/cond/branch_0_fun/all_to_all | solution.py:58
  144.0 1.3 select_reduce_fusion
  145.4 9.5 %all-to-all-done = bf16[32,24,256]{2,1,0:T(8,128)(2,1)S(1)} async-done(((bf16[32,24,256]{2,1,0:T(8,128)(2,1)}), bf16[32,24,256]{2,1,0:T(8,128)(2,1)S(1)}, u32[]{:S(2)}, u32[]{:S(2)}) %all-to-all-start) | async-done | bytes 393248 | tf_op jit(solution)/shard_map/cond/branch_0_fun/all_to_all | solution.py:58
  154.9 1.1 fusion.1
  156.0 6.6 %all-to-all-start.1 = ((bf16[16,32,256]{2,1,0:T(8,128)(2,1)}), bf16[16,32,256]{2,1,0:T(8,128)(2,1)S(1)}, u32[]{:S(2)}, u32[]{:S(2)}) async-start(bf16[16,32,256]{2,1,0:T(8,128)(2,1)} %bitcast.9), calls=%async_computation.1 | async-start | bytes 524288 | tf_op jit(solution)/shard_map/cond/branch_0_fun/all_to_all | solution.py:58
  162.8 11.6 %all-to-all-done.1 = bf16[16,32,256]{2,1,0:T(8,128)(2,1)S(1)} async-done(((bf16[16,32,256]{2,1,0:T(8,128)(2,1)}), bf16[16,32,256]{2,1,0:T(8,128)(2,1)S(1)}, u32[]{:S(2)}, u32[]{:S(2)}) %all-to-all-start.1) | async-done | bytes 262176 | tf_op jit(solution)/shard_map/cond/branch_0_fun/all_to_all | solution.py:58
  175.5 1.6 fusion.87
  177.2 1.2 fusion.75
  (158 shorter events, 31.0 us)
Async XLA Ops:
  0.6 91.0 %copy-start = (bf16[256,768]{1,0:T(8,128)(2,1)S(1)}, bf16[256,768]{1,0:T(8,128)(2,1)}, u32[]{:S(2)}) copy-start(bf16[256,768]{1,0:T(8,128)(2,1)} %param.40) | copy-start | bytes 1179652
  0.6 33.4 %copy-start.1 = (f32[512,256]{1,0:T(8,128)S(1)}, f32[512,256]{1,0:T(8,128)}, u32[]{:S(2)}) copy-start(f32[512,256]{1,0:T(8,128)} %param.22) | copy-start | bytes 1572868
  3.2 17.1 %all-to-all-start.5 = ((s32[16,1,128]{2,1,0:T(1,128)}), s32[16,1,128]{2,1,0:T(1,128)S(1)}, u32[]{:S(2)}, u32[]{:S(2)}) async-start(s32[16,1,128]{2,1,0:T(1,128)} %bitcast.187), calls=%async_computation.5 | async-start | bytes 16384 | tf_op jit(solution)/shard_map/all_to_all | solution.py:58
  14.7 28.1 %copy-start.35 = (s32[256]{0:T(256)}, s32[256]{0:T(256)S(1)}, u32[]{:S(2)}) copy-start(s32[256]{0:T(256)S(1)} %get-tuple-element.480) | copy-start | bytes 3076
  18.5 15.5 %copy-start.22 = (s32[2816]{0:T(1024)}, s32[2816]{0:T(1024)S(1)}, u32[]{:S(2)}) copy-start(s32[2816]{0:T(1024)S(1)} %get-tuple-element.484) | copy-start | bytes 33796
  18.5 27.6 %copy-start.28 = (s32[2816]{0:T(1024)}, s32[2816]{0:T(1024)S(1)}, u32[]{:S(2)}) copy-start(s32[2816]{0:T(1024)S(1)} %get-tuple-element.483) | copy-start | bytes 33796
  22.6 20.0 %all-to-all-start.6 = ((s32[32,1,128]{2,1,0:T(1,128)}), s32[32,1,128]{2,1,0:T(1,128)S(1)}, u32[]{:S(2)}, u32[]{:S(2)}) async-start(s32[32,1,128]{2,1,0:T(1,128)} %bitcast.42), calls=%async_computation.6 | async-start | bytes 32768 | tf_op jit(solution)/shard_map/all_to_all | solution.py:58
  34.1 22.2 %copy-start.3 = (bf16[512,256]{1,0:T(8,128)(2,1)}, bf16[512,256]{1,0:T(8,128)(2,1)S(1)}, u32[]{:S(2)}) copy-start(bf16[512,256]{1,0:T(8,128)(2,1)S(1)} %convert_element_type.124) | copy-start | bytes 786436
  34.2 10.5 %copy-start.24 = (s32[16,16]{1,0:T(8,128)}, s32[16,16]{1,0:T(8,128)S(1)}, u32[]{:S(2)}) copy-start(s32[16,16]{1,0:T(8,128)S(1)} %slice.138) | copy-start | bytes 3076
  42.7 2.0 %copy-start.10 = (s32[16,32,2]{0,2,1:T(2,128)}, s32[16,32,2]{0,2,1:T(2,128)S(1)}, u32[]{:S(2)}) copy-start(s32[16,32,2]{0,2,1:T(2,128)S(1)} %copy.218) | copy-start | bytes 12292
  42.8 2.0 %copy-start.25 = (s32[16,64]{1,0:T(8,128)}, s32[16,64]{1,0:T(8,128)S(1)}, u32[]{:S(2)}) copy-start(s32[16,64]{1,0:T(8,128)S(1)} %copy.219) | copy-start | bytes 12292
  47.6 23.0 %all-to-all-start.7 = ((bf16[16,48,256]{2,1,0:T(8,128)(2,1)}), bf16[16,48,256]{2,1,0:T(8,128)(2,1)S(1)}, u32[]{:S(2)}, u32[]{:S(2)}) async-start(bf16[16,48,256]{2,1,0:T(8,128)(2,1)} %broadcast_select_fusion.1), calls=%async_computation.7 | async-start | bytes 786432 | tf_op jit(solution)/shard_map/all_to_all | solution.py:58
  75.3 4.2 %copy-start.34 = (s32[128,20]{0,1:T(8,128)S(1)}, s32[128,20]{0,1:T(8,128)}, u32[]{:S(2)}) copy-start(s32[128,20]{0,1:T(8,128)} %param.29) | copy-start | bytes 30724
  75.3 4.2 %copy-start.46 = (s32[128]{0:T(128)S(1)}, s32[128]{0:T(128)}, u32[]{:S(2)}) copy-start(s32[128]{0:T(128)} %param.28) | copy-start | bytes 1540
  75.3 4.9 %copy-start.6 = (bf16[384,256]{1,0:T(8,128)(2,1)S(1)}, bf16[384,256]{1,0:T(8,128)(2,1)}, u32[]{:S(2)}) copy-start(bf16[384,256]{1,0:T(8,128)(2,1)} %param.33) | copy-start | bytes 589828
  75.3 5.1 %copy-start.4 = (bf16[384,256]{1,0:T(8,128)(2,1)S(1)}, bf16[384,256]{1,0:T(8,128)(2,1)}, u32[]{:S(2)}) copy-start(bf16[384,256]{1,0:T(8,128)(2,1)} %param.34) | copy-start | bytes 589828
  75.3 5.3 %copy-start.11 = (bf16[512,256]{1,0:T(8,128)(2,1)S(1)}, bf16[512,256]{1,0:T(8,128)(2,1)}, u32[]{:S(2)}) copy-start(bf16[512,256]{1,0:T(8,128)(2,1)} %param.35) | copy-start | bytes 786436
  75.3 6.2 %copy-start.13 = (bf16[512,256]{1,0:T(8,128)(2,1)S(1)}, bf16[512,256]{1,0:T(8,128)(2,1)}, u32[]{:S(2)}) copy-start(bf16[512,256]{1,0:T(8,128)(2,1)} %param.37) | copy-start | bytes 786436
  75.3 40.6 %all-to-all-start.8 = ((bf16[32,88,256]{2,1,0:T(8,128)(2,1)}), bf16[32,88,256]{2,1,0:T(8,128)(2,1)S(1)}, u32[]{:S(2)}, u32[]{:S(2)}) async-start(bf16[32,88,256]{2,1,0:T(8,128)(2,1)} %broadcast_select_fusion), calls=%async_computation.8 | async-start | bytes 2883584 | tf_op jit(solution)/shard_map/all_to_all | solution.py:58
  79.4 2.9 %copy-start.8 = (bf16[384,256]{1,0:T(8,128)(2,1)S(1)}, bf16[384,256]{1,0:T(8,128)(2,1)}, u32[]{:S(2)}) copy-start(bf16[384,256]{1,0:T(8,128)(2,1)} %param.32) | copy-start | bytes 589828
  79.4 3.7 %copy-start.18 = (bf16[256,256]{1,0:T(8,128)(2,1)S(1)}, bf16[256,256]{1,0:T(8,128)(2,1)}, u32[]{:S(2)}) copy-start(bf16[256,256]{1,0:T(8,128)(2,1)} %param.38) | copy-start | bytes 393220
  80.2 4.5 %copy-start.41 = (f32[128]{0:T(128)S(1)}, f32[128]{0:T(128)}, u32[]{:S(2)}) copy-start(f32[128]{0:T(128)} %param.31) | copy-start | bytes 1540
  80.2 5.0 %copy-start.39 = (f32[768]{0:T(1024)S(1)}, f32[768]{0:T(1024)}, u32[]{:S(2)}) copy-start(f32[768]{0:T(1024)} %param.41) | copy-start | bytes 9220
  80.2 5.6 %copy-start.17 = (s32[32,288]{1,0:T(8,128)S(1)}, s32[32,288]{1,0:T(8,128)}, u32[]{:S(2)}) copy-start(s32[32,288]{1,0:T(8,128)} %get-tuple-element.176) | copy-start | bytes 110596
  80.4 6.0 %copy-start.43 = (f32[128]{0:T(128)S(1)}, f32[128]{0:T(128)}, u32[]{:S(2)}) copy-start(f32[128]{0:T(128)} %param.30) | copy-start | bytes 1540
  84.7 8.3 %copy-start.33 = (pred[32,32]{1,0:T(8,128)(4,1)S(1)}, pred[32,32]{1,0:T(8,128)(4,1)}, u32[]{:S(2)}) copy-start(pred[32,32]{1,0:T(8,128)(4,1)} %copy-done.32) | copy-start | bytes 3076
  136.9 25.7 %copy-start.16 = (s32[16,31]{0,1:T(8,128)S(1)}, s32[16,31]{0,1:T(8,128)}, u32[]{:S(2)}) copy-start(s32[16,31]{0,1:T(8,128)} %get-tuple-element.436) | copy-start | bytes 5956 | tf_op jit(solution)/shard_map/cond
  136.9 18.0 %all-to-all-start = ((bf16[32,24,256]{2,1,0:T(8,128)(2,1)}), bf16[32,24,256]{2,1,0:T(8,128)(2,1)S(1)}, u32[]{:S(2)}, u32[]{:S(2)}) async-start(bf16[32,24,256]{2,1,0:T(8,128)(2,1)} %bitcast.153), calls=%async_computation | async-start | bytes 786432 | tf_op jit(solution)/shard_map/cond/branch_0_fun/all_to_all | solution.py:58
  156.0 18.4 %all-to-all-start.1 = ((bf16[16,32,256]{2,1,0:T(8,128)(2,1)}), bf16[16,32,256]{2,1,0:T(8,128)(2,1)S(1)}, u32[]{:S(2)}, u32[]{:S(2)}) async-start(bf16[16,32,256]{2,1,0:T(8,128)(2,1)} %bitcast.9), calls=%async_computation.1 | async-start | bytes 524288 | tf_op jit(solution)/shard_map/cond/branch_0_fun/all_to_all | solution.py:58
  175.5 1.7 copy-start.37
  175.5 1.7 copy-start.38
  175.5 1.7 copy-start.40
  (5 other events, 5.2 us)

commit v6 on v4

--- a/solution.py
+++ b/solution.py
@@ -172,8 +172,8 @@
 
 
 def event_kernel(
+    lanes,
     table,
-    lanes,
     count,
     slot,
     code,
@@ -186,12 +186,16 @@
     message_out,
     embedded,
     slot_sum,
-    turned,
+    halves,
+    even_left,
+    even_right,
+    odd_left,
+    odd_right,
     values,
     exponents,
 ):
     rows, width = table.shape
-    pairs = lanes.shape[1]
+    pairs = count.shape[1]
     events = pairs // 2
     head_size = width // HEADS
     one = jnp.bfloat16(1)
@@ -200,9 +204,6 @@
     def dot(left, right):
         return jnp.dot(left, right, preferred_element_type=jnp.float32)
 
-    def number(size):
-        return lax.broadcasted_iota(jnp.int32, (size, pairs), 0).astype(jnp.float32).astype(jnp.bfloat16)
-
     def near(index, first, size):
         return jnp.clip(index - first, -1, size).astype(jnp.float32).astype(jnp.bfloat16)
 
@@ -210,24 +211,33 @@
     column = lax.broadcasted_iota(jnp.int32, (width, width), 1)
     unit = jnp.where(row == column, 1.0, 0.0).astype(jnp.bfloat16)
     for low in range(0, rows, width):
-        turned[:, low : low + width] = across(unit, table[low : low + width, :]).astype(jnp.bfloat16)
-    numbers = number(width)
-
-    def gather(index):
-        total = jnp.zeros((width, pairs), jnp.float32)
-        for low in range(0, rows, width):
-            chosen = jnp.where(numbers == near(index, low, width), one, none)
-            total = total + dot(turned[:, low : low + width], chosen)
-        return total.astype(jnp.bfloat16)
-
-    ends = gather(lanes[K : K + 1, :])
+        part = table[low : low + width, :].astype(jnp.float32)
+        halves[0, low : low + width, :] = part[:, :LANES]
+        halves[1, low : low + width, :] = part[:, LANES:]
+
+    def fetch(line, left, right):
+        for lane in range(pairs):
+            index = lanes[line * pairs + lane]
+            left[lane : lane + 1, :] = halves[0, pl.ds(index, 1), :]
+            right[lane : lane + 1, :] = halves[1, pl.ds(index, 1), :]
+
+    def fetched(left, right):
+        return jnp.concatenate(
+            [left[...].astype(jnp.bfloat16), right[...].astype(jnp.bfloat16)], 1
+        )
+
+    fetch(K, odd_left, odd_right)
+    fetch(0, even_left, even_right)
+    end_rows = fetched(odd_left, odd_right)
+    ends = across(unit, end_rows).astype(jnp.bfloat16)
     queries = dot(query_weight[:, :width], ends) + across(
         query_weight[:, width:], jnp.broadcast_to(fixed[...], (pairs, fixed.shape[1]))
     )
 
-    def neighbour(k, carry):
-        near_rows = gather(lanes[pl.ds(k, 1), :])
-        pair = dot(pair_weight[:, :width], near_rows) + dot(pair_weight[:, width:], code[k])
+    def neighbour(k, left, right):
+        pair = across(pair_weight[:, :width], fetched(left, right)) + dot(
+            pair_weight[:, width:], code[k]
+        )
         values[k] = pair[width:]
         product = queries * pair[:width]
         for head in range(HEADS):
@@ -235,9 +245,16 @@
                 product[head * head_size : (head + 1) * head_size], axis=0, keepdims=True
             ) / math.sqrt(head_size)
             exponents[k, head : head + 1, :] = jnp.where(k < count[...], jnp.exp(scores), 0.0)
+
+    def two(step, carry):
+        k = 2 * step
+        fetch(k + 1, odd_left, odd_right)
+        neighbour(k, even_left, even_right)
+        fetch(k + 2, even_left, even_right)
+        neighbour(k + 1, odd_left, odd_right)
         return carry
 
-    lax.fori_loop(0, K, neighbour, 0)
+    lax.fori_loop(0, K // 2, two, 0)
     pieces = []
     for head in range(HEADS):
         low = head * head_size
@@ -261,6 +278,8 @@
         dot(message_in[:, :width], embeds) + dot(message_in[:, width:], other), 0.0
     ).astype(jnp.bfloat16)
     message = dot(message_out[...], hidden)
+    numbers = lax.broadcasted_iota(jnp.int32, (width, pairs), 0).astype(jnp.float32)
+    numbers = numbers.astype(jnp.bfloat16)
     high = message.astype(jnp.bfloat16)
     low = (message - high.astype(jnp.float32)).astype(jnp.bfloat16)
     for first in range(0, slot_sum.shape[0], width):
@@ -275,26 +294,30 @@
         ).astype(jnp.bfloat16)
 
 
-def gru_update(memory, mem_half, totals, counts, input_weight, state_weight, update_bias):
-    row_width = memory.shape[1]
-    averaged = (totals / jnp.maximum(counts, 1.0)[:, None]).astype(jnp.bfloat16)
-    from_msg = jnp.dot(averaged, input_weight, preferred_element_type=jnp.float32)
-    from_state = jnp.dot(mem_half, state_weight, preferred_element_type=jnp.float32)
-    update_gate = jax.nn.sigmoid(
-        from_msg[:, :row_width] + from_state[:, :row_width] + update_bias[:row_width]
-    )
-    reset_gate = jax.nn.sigmoid(
-        from_msg[:, row_width : 2 * row_width]
-        + from_state[:, row_width : 2 * row_width]
-        + update_bias[row_width : 2 * row_width]
-    )
-    candidate = jnp.tanh(
-        from_msg[:, 2 * row_width :]
-        + update_bias[2 * row_width :]
-        + reset_gate * from_state[:, 2 * row_width :]
-    )
-    updated = (1.0 - update_gate) * candidate + update_gate * memory
-    return jnp.where((counts > 0)[:, None], updated, memory)
+def gru_kernel(news, owned, counts, memory, from_state, input_weight, bias, new_memory):
+    nodes, width = memory.shape
+    one = jnp.bfloat16(1)
+    none = jnp.bfloat16(0)
+    size = 128
+    numbers = lax.broadcasted_iota(jnp.int32, (size, owned.shape[1]), 0).astype(jnp.float32)
+    numbers = numbers.astype(jnp.bfloat16)
+    for low in range(0, nodes, size):
+        here = slice(low, low + size)
+        index = jnp.clip(owned[...] - low, -1, size).astype(jnp.float32).astype(jnp.bfloat16)
+        totals = jnp.dot(
+            jnp.where(numbers == index, one, none), news[...], preferred_element_type=jnp.float32
+        )
+        count = jnp.concatenate([counts[here, :]] * (width // LANES), 1)
+        averaged = (totals / jnp.maximum(count, 1.0)).astype(jnp.bfloat16)
+        from_msg = jnp.dot(averaged, input_weight[...], preferred_element_type=jnp.float32)
+        update, reset, last = (slice(i * width, (i + 1) * width) for i in range(3))
+        update_gate = jax.nn.sigmoid(from_msg[:, update] + from_state[here, update] + bias[:, update])
+        reset_gate = jax.nn.sigmoid(from_msg[:, reset] + from_state[here, reset] + bias[:, reset])
+        candidate = jnp.tanh(
+            from_msg[:, last] + bias[:, last] + reset_gate * from_state[here, last]
+        )
+        updated = (1.0 - update_gate) * candidate + update_gate * memory[here, :]
+        new_memory[here, :] = jnp.where(count > 0, updated, memory[here, :])
 
 
 def local(
@@ -418,6 +441,9 @@
     elapsed = (event_time[None, :] - jnp.transpose(near_time)).astype(jnp.float32)
     elapsed = elapsed.reshape(2, K, events)
 
+    def by_owner(sums):
+        return sums.reshape(groups * members, CAP_E, row_width)
+
     def whole():
         full = jnp.broadcast_to(near_block[None], (members, block, row_width))
         full = exchange(jnp.concatenate([full, end_part], 1), "dev")
@@ -450,18 +476,15 @@
         ) + jnp.dot(
             end_hot, (message - high).astype(jnp.bfloat16), preferred_element_type=jnp.float32
         )
-        return jnp.concatenate([embedded[0], embedded[1]], 1), slot_sum.astype(jnp.bfloat16)
+        return jnp.concatenate([embedded[0], embedded[1]], 1), by_owner(slot_sum.astype(jnp.bfloat16))
 
     pairs = 2 * events
     near_lanes = jnp.transpose(index[: 2 * K * events].reshape(2, K, events), (1, 0, 2))
-    lanes = jnp.concatenate(
-        [near_lanes.reshape(K, pairs), index[2 * K * events :].reshape(1, pairs)], 0
-    )
+    lanes = jnp.concatenate([near_lanes.reshape(-1), index[2 * K * events :]])
     elapsed_lanes = jnp.transpose(elapsed, (1, 0, 2)).reshape(K, 1, pairs)
     code = jnp.cos(elapsed_lanes * frequency[None, :, None] + phases[None, :, None])
     fixed = jnp.cos(phases)[None, :]
     operands = (
-        lanes,
         counted.reshape(1, pairs),
         end_value.reshape(1, pairs),
         code.astype(jnp.bfloat16),
@@ -475,35 +498,47 @@
     )
 
     def listed_only():
-        return pl.pallas_call(
+        embedded, slot_sum = pl.pallas_call(
             event_kernel,
             out_shape=(
                 jax.ShapeDtypeStruct((events, 2 * row_width), jnp.bfloat16),
                 jax.ShapeDtypeStruct((groups * members * CAP_E, row_width), jnp.bfloat16),
             ),
-            scratch_shapes=[
-                pltpu.VMEM((row_width, table.shape[0]), jnp.bfloat16),
+            in_specs=[pl.BlockSpec(memory_space=pltpu.SMEM)]
+            + [pl.BlockSpec(memory_space=pltpu.VMEM)] * (1 + len(operands)),
+            scratch_shapes=[pltpu.VMEM((row_width // LANES, table.shape[0], LANES), jnp.float32)]
+            + [pltpu.VMEM((pairs, LANES), jnp.float32)] * 4
+            + [
                 pltpu.VMEM((K, row_width, pairs), jnp.float32),
                 pltpu.VMEM((K, 8, pairs), jnp.float32),
             ],
             name="event_kernel",
-        )(table, *operands)
+        )(lanes, table, *operands)
+        return embedded, by_owner(slot_sum)
 
     embedded, slot_sum = lax.cond(most > CAP, whole, listed_only)
     news = exchange(
-        slot_sum.reshape(groups * members, CAP_E, row_width), ("grp", "dev")
+        slot_sum, ("grp", "dev")
     ).reshape(-1, row_width)
     owned = got_end.reshape(-1)
-    owned_hot = hot(owned, nodes, 0)
-    totals = jnp.dot(owned_hot, news, preferred_element_type=jnp.float32)
     counts = jnp.sum(
         jnp.where(
             owned[None, :] == jnp.arange(nodes)[:, None], got_count.reshape(1, -1), 0
         ),
         axis=1,
     ).astype(jnp.float32)
-    new_memory = gru_update(
-        memory, mem_half, totals, counts, input_weight, state_weight, update_bias
+    new_memory = pl.pallas_call(
+        gru_kernel,
+        out_shape=jax.ShapeDtypeStruct(memory.shape, memory.dtype),
+        name="gru_kernel",
+    )(
+        news,
+        owned[None, :],
+        jnp.broadcast_to(counts[:, None], (nodes, LANES)),
+        memory,
+        jnp.dot(mem_half, state_weight, preferred_element_type=jnp.float32),
+        input_weight,
+        update_bias[None, :],
     )
     return (new_memory, embedded)
 

time: 170 us -> 164 us (0.965)
  other arithmetic: 14.9 us -> 11.3 us
  matrix products: 9.78 us -> 7.76 us
  local copies, waits for them, and re-layouts: 13.1 us -> 14.9 us
    pallas_call x1, Pallas kernels: 14 us -> 9.31 us  [listed_only(): pl.pallas_call(event_kernel, out_shape=(jax.ShapeDtypeStruct((events, 2 *...]
    pallas_call x0 -> x1, Pallas kernels: none -> 4.2 us  [local(): pl.pallas_call(gru_kernel, out_shape=jax.ShapeDtypeStruct(memory.shape, m...]
    select_n x1 -> x0, other arithmetic: 2.55 us -> none  [gru_update(): return jnp.where((counts > 0)[:, None], updated, memory)]
    dot_general x2 -> x1, matrix products: 3.6 us -> 1.54 us  [local(): jnp.dot(mem_half, state_weight, preferred_element_type=jnp.float32)]
    unnamed x50 -> x46, local copies, waits for them, and re-layouts: 7.7 us -> 7.66 us
  transfers between devices with their start and end apart: 5 -> 5, of which waited for: 5 -> 5; matrix products, arithmetic and copies ran while one was open for 11% -> 13% of each run, Pallas kernels for 0% -> 0%
where the time goes in v6:
time: 164 us
  waiting for transfers between devices  70.7 us (43%)
  starting transfers between devices  41.3 us (25%)
  Pallas kernels  16 us (10%)
  local copies, waits for them, and re-layouts  14.9 us (9%)
  other arithmetic  11.3 us (7%)
  matrix products  7.76 us (5%)
  between operations  1.71 us (1%)
    all_to_all x5, waiting for transfers between devices, exchange(): return lax.all_to_all(x, axis, split_axis=0, concat_axis=0, tiled=True)  70.7 us
    all_to_all x5, starting transfers between devices, exchange(): return lax.all_to_all(x, axis, split_axis=0, concat_axis=0, tiled=True)  41.3 us
    pallas_call x1, Pallas kernels, listed_only(): pl.pallas_call(event_kernel, out_shape=(jax.ShapeDtypeStruct((events, 2 *...  9.31 us
    unnamed x46, local copies, waits for them, and re-layouts  7.66 us
    convert_element_type x1, other arithmetic, local(): code.astype(jnp.bfloat16)  5.4 us
    pallas_call x1, Pallas kernels, local(): pl.pallas_call(gru_kernel, out_shape=jax.ShapeDtypeStruct(memory.shape, m...  4.2 us
  transfers between devices with their start and end apart: 5, of which 5 were waited for; matrix products, arithmetic and copies ran while one was open for 13% of the time, Pallas kernels for 0%

profile of v6, /device:TPU:1, one launch (start us, length us, event | category | flops | bytes accessed | tf_op | source)
XLA Modules:
  0.0 163.7 jit_solution(2586322460222196078)
XLA Ops:
  0.6 2.5 %request_kernel.1 = (s32[16,128]{1,0:T(8,128)}, s32[32,288]{1,0:T(8,128)}) custom-call(s32[1]{0:T(128)} %bitcast.21.mine, s32[20,128]{1,0:T(8,128)} %bitcast.132, s32[2,128]{1,0:T(2,128)} %bitcast.146, s32[2,128]{1,0:T(2,128)} %bitcast.141, s32[2,512]{1,0:T(2,128)} %bitcast.153, s32[16,512]{1,0:T(8,128)} %bitcast.140), custom_call_target="tpu_custom_call" | custom-call | tf_op jit(solution)/shard_map/request_kernel/pallas_call | solution.py:357
  3.2 10.1 %all-to-all-start.1 = ((s32[16,1,128]{2,1,0:T(1,128)}), s32[16,1,128]{2,1,0:T(1,128)S(1)}, u32[]{:S(2)}, u32[]{:S(2)}) async-start(s32[16,1,128]{2,1,0:T(1,128)} %bitcast.152), calls=%async_computation.1 | async-start | bytes 16384 | tf_op jit(solution)/shard_map/all_to_all | solution.py:38
  13.3 1.4 select_reduce_fusion
  14.7 5.6 %all-to-all-done.1 = s32[16,1,128]{2,1,0:T(1,128)S(1)} async-done(((s32[16,1,128]{2,1,0:T(1,128)}), s32[16,1,128]{2,1,0:T(1,128)S(1)}, u32[]{:S(2)}, u32[]{:S(2)}) %all-to-all-start.1) | async-done | bytes 8224 | tf_op jit(solution)/shard_map/all_to_all | solution.py:38
  20.3 0.7 slice_reduce_fusion.1
  21.9 0.7 add_add_fusion
  22.6 11.4 %all-to-all-start.2 = ((s32[32,1,128]{2,1,0:T(1,128)}), s32[32,1,128]{2,1,0:T(1,128)S(1)}, u32[]{:S(2)}, u32[]{:S(2)}) async-start(s32[32,1,128]{2,1,0:T(1,128)} %bitcast.34), calls=%async_computation.2 | async-start | bytes 32768 | tf_op jit(solution)/shard_map/all_to_all | solution.py:38
  34.0 8.5 %all-to-all-done.2 = s32[32,1,128]{2,1,0:T(1,128)S(1)} async-done(((s32[32,1,128]{2,1,0:T(1,128)}), s32[32,1,128]{2,1,0:T(1,128)S(1)}, u32[]{:S(2)}, u32[]{:S(2)}) %all-to-all-start.2) | async-done | bytes 16416 | tf_op jit(solution)/shard_map/all_to_all | solution.py:38
  43.5 2.5 %fusion.53 = bf16[1280,256]{1,0:T(8,128)(2,1)} fusion(s32[1280]{0:T(1024)S(1)} %eq.100, f32[512,256]{1,0:T(8,128)} %memory.1), kind=kOutput, calls=%fused_computation.77 | convolution fusion | flops 336658432 | bytes 1184768 | tf_op jit(solution)/shard_map/dot_general | solution.py:26
  46.0 5.5 %all-to-all-start.3 = ((bf16[16,80,256]{2,1,0:T(8,128)(2,1)}), bf16[16,80,256]{2,1,0:T(8,128)(2,1)S(1)}, u32[]{:S(2)}, u32[]{:S(2)}) async-start(bf16[16,80,256]{2,1,0:T(8,128)(2,1)} %bitcast.40), calls=%async_computation.3 | async-start | bytes 1310720 | tf_op jit(solution)/shard_map/all_to_all | solution.py:38
  51.5 20.0 %all-to-all-done.3 = bf16[16,80,256]{2,1,0:T(8,128)(2,1)S(1)} async-done(((bf16[16,80,256]{2,1,0:T(8,128)(2,1)}), bf16[16,80,256]{2,1,0:T(8,128)(2,1)S(1)}, u32[]{:S(2)}, u32[]{:S(2)}) %all-to-all-start.3) | async-done | bytes 655392 | tf_op jit(solution)/shard_map/all_to_all | solution.py:38
  72.6 1.2 fusion.50
  73.8 1.8 %add_convert_fusion = bf16[32,88,256]{2,1,0:T(8,128)(2,1)} fusion(f32[32,88,256]{2,1,0:T(8,128)S(1)} %fusion.50, bf16[32,32,256]{2,1,0:T(8,128)(2,1)S(1)} %reshape.252, s32[32,88]{1,0:T(8,128)S(1)} %get-tuple-element.117), kind=kOutput, calls=%fused_computation.71 | convolution fusion | flops 47669248 | bytes 4860928 | tf_op jit(solution)/shard_map/dcp,dpw->dcw/dot_general | solution.py:432
  75.6 4.1 %all-to-all-start.4 = ((bf16[32,88,256]{2,1,0:T(8,128)(2,1)}), bf16[32,88,256]{2,1,0:T(8,128)(2,1)S(1)}, u32[]{:S(2)}, u32[]{:S(2)}) async-start(bf16[32,88,256]{2,1,0:T(8,128)(2,1)} %add_convert_fusion), calls=%async_computation.4 | async-start | bytes 2883584 | tf_op jit(solution)/shard_map/all_to_all | solution.py:38
  79.9 0.7 fusion.57
  82.3 1.8 %copy.131 = bf16[512,256]{0,1:T(8,128)(2,1)} copy(bf16[512,256]{1,0:T(8,128)(2,1)} %param.35) | data formatting | bytes 524288 | tf_op args[13]
  84.1 1.8 %copy.132 = bf16[512,256]{0,1:T(8,128)(2,1)} copy(bf16[512,256]{1,0:T(8,128)(2,1)} %param.37) | data formatting | bytes 524288 | tf_op args[15]
  85.9 0.8 copy.128
  86.8 1.7 %copy.133 = bf16[256,256]{0,1:T(8,128)(2,1)} copy(bf16[256,256]{1,0:T(8,128)(2,1)} %param.38) | data formatting | bytes 262144 | tf_op args[16]
  89.7 5.4 %cosine_convert_fusion.2 = bf16[10,128,256]{2,1,0:T(8,128)(2,1)S(1)} fusion(f32[128]{0:T(128)} %param.31, f32[128]{0:T(128)} %param.30, f32[10,256]{1,0:T(8,128)} %bitcast.138), kind=kLoop, calls=%fused_computation.82 | loop fusion | flops 983040 | bytes 666624 | tf_op jit(solution)/shard_map/convert_element_type | solution.py:490
  95.1 0.7 slice_reduce_fusion
  96.5 19.0 %all-to-all-done.4 = bf16[32,88,256]{2,1,0:T(8,128)(2,1)S(1)} async-done(((bf16[32,88,256]{2,1,0:T(8,128)(2,1)}), bf16[32,88,256]{2,1,0:T(8,128)(2,1)S(1)}, u32[]{:S(2)}, u32[]{:S(2)}) %all-to-all-start.4) | async-done | bytes 1441824 | tf_op jit(solution)/shard_map/all_to_all | solution.py:38
  115.5 9.3 %conditional.1 = ((bf16[128,512]{1,0:T(8,128)(2,1)}, bf16[1024,256]{1,0:T(8,128)(2,1)S(1)})) conditional(s32[]{:T(128)} %convert_element_type.73, (bf16[32,88,256]{2,1,0:T(8,128)(2,1)S(1)}, s32[2,128]{1,0:T(2,128)}, s32[2,128]{1,0:T(2,128)}, bf16[128]{0:T(256)(128)(2,1)}, f32[256]{0:T(256)}, /*index=5*/s32[2816]{0:T(1024)}, ...), branch_computations={%region_4.5_spmd, %region_5.12_spmd} | conditional | flops 1517661824 | bytes 61769664 | solution.py:519
  115.5 9.3 %event_kernel.1 = (bf16[128,512]{1,0:T(8,128)(2,1)}, bf16[1024,256]{1,0:T(8,128)(2,1)S(1)}) custom-call(s32[2816]{0:T(1024)} %get-tuple-element.63.lanes, bf16[2816,256]{1,0:T(8,128)(2,1)S(1)} %bitcast.112, s32[1,256]{1,0:T(1,128)} %bitcast.145, s32[1,256]{1,0:T(1,128)} %bitcast.149, bf16[10,128,256]{2,1,0:T(8,128)(2,1)S(1)} %get-tuple-element.67.code, ...), custom_call_target="tpu_custom_call" | custom-call | tf_op jit(solution)/shard_map/cond/branch_0_fun/event_kernel/pallas_call | solution.py:501
  124.8 1.0 reshape.256
  125.8 10.3 %all-to-all-start.5 = ((bf16[512,2,256]{2,1,0:T(2,128)(2,1)}), bf16[512,2,256]{2,1,0:T(2,128)(2,1)S(1)}, u32[]{:S(2)}, u32[]{:S(2)}) async-start(bf16[512,2,256]{2,1,0:T(2,128)(2,1)} %reshape.256), calls=%async_computation.5 | async-start | bytes 1048576 | tf_op jit(solution)/shard_map/all_to_all | solution.py:38
  136.7 1.5 fusion.60.from_state
  138.6 0.8 select_n.88.owned
  140.1 17.6 %all-to-all-done.5 = bf16[512,2,256]{2,1,0:T(2,128)(2,1)S(1)} async-done(((bf16[512,2,256]{2,1,0:T(2,128)(2,1)}), bf16[512,2,256]{2,1,0:T(2,128)(2,1)S(1)}, u32[]{:S(2)}, u32[]{:S(2)}) %all-to-all-start.5) | async-done | bytes 524320 | tf_op jit(solution)/shard_map/all_to_all | solution.py:38
  157.7 1.0 reshape.257.news
  158.6 0.8 broadcast_in_dim.97.counts
  159.5 4.2 %gru_kernel.1 = f32[512,256]{1,0:T(8,128)} custom-call(bf16[1024,256]{1,0:T(8,128)(2,1)} %reshape.257.news, s32[1,1024]{1,0:T(1,128)} %select_n.88.owned, f32[512,128]{1,0:T(8,128)} %broadcast_in_dim.97.counts, f32[512,256]{1,0:T(8,128)} %memory.1, f32[512,768]{1,0:T(8,128)} %fusion.60.from_state, bf16[256,768]{1,0:T(8,128)(2,1)} %input_weight.1, ...), custom_call_target="tpu_custom_call" | custom-call | tf_op jit(solution)/shard_map/gru_kernel/pallas_call | solution.py:530
  (85 shorter events, 7.6 us)
Async XLA Ops:
  0.6 136.1 %copy-start = (bf16[256,768]{1,0:T(8,128)(2,1)S(1)}, bf16[256,768]{1,0:T(8,128)(2,1)}, u32[]{:S(2)}) copy-start(bf16[256,768]{1,0:T(8,128)(2,1)} %param.40) | copy-start | bytes 1179652
  3.2 17.1 %all-to-all-start.1 = ((s32[16,1,128]{2,1,0:T(1,128)}), s32[16,1,128]{2,1,0:T(1,128)S(1)}, u32[]{:S(2)}, u32[]{:S(2)}) async-start(s32[16,1,128]{2,1,0:T(1,128)} %bitcast.152), calls=%async_computation.1 | async-start | bytes 16384 | tf_op jit(solution)/shard_map/all_to_all | solution.py:38
  22.6 20.0 %all-to-all-start.2 = ((s32[32,1,128]{2,1,0:T(1,128)}), s32[32,1,128]{2,1,0:T(1,128)S(1)}, u32[]{:S(2)}, u32[]{:S(2)}) async-start(s32[32,1,128]{2,1,0:T(1,128)} %bitcast.34), calls=%async_computation.2 | async-start | bytes 32768 | tf_op jit(solution)/shard_map/all_to_all | solution.py:38
  43.2 28.4 %copy-start.10 = (s32[32,32]{0,1:T(8,128)}, s32[32,32]{0,1:T(8,128)S(1)}, u32[]{:S(2)}) copy-start(s32[32,32]{0,1:T(8,128)S(1)} %copy.122) | copy-start | bytes 12292
  46.0 25.5 %all-to-all-start.3 = ((bf16[16,80,256]{2,1,0:T(8,128)(2,1)}), bf16[16,80,256]{2,1,0:T(8,128)(2,1)S(1)}, u32[]{:S(2)}, u32[]{:S(2)}) async-start(bf16[16,80,256]{2,1,0:T(8,128)(2,1)} %bitcast.40), calls=%async_computation.3 | async-start | bytes 1310720 | tf_op jit(solution)/shard_map/all_to_all | solution.py:38
  75.6 4.2 %copy-start.22 = (s32[128,2]{0,1:T(2,128)S(1)}, s32[128,2]{0,1:T(2,128)}, u32[]{:S(2)}) copy-start(s32[128,2]{0,1:T(2,128)} %param.27) | copy-start | bytes 3076
  75.6 4.2 %copy-start.24 = (s32[128,2]{0,1:T(2,128)S(1)}, s32[128,2]{0,1:T(2,128)}, u32[]{:S(2)}) copy-start(s32[128,2]{0,1:T(2,128)} %param.25) | copy-start | bytes 3076
  75.6 4.2 %copy-start.15 = (s32[128,20]{0,1:T(8,128)S(1)}, s32[128,20]{0,1:T(8,128)}, u32[]{:S(2)}) copy-start(s32[128,20]{0,1:T(8,128)} %param.26) | copy-start | bytes 30724
  75.6 4.3 %copy-start.19 = (s32[32,288]{1,0:T(8,128)S(1)}, s32[32,288]{1,0:T(8,128)}, u32[]{:S(2)}) copy-start(s32[32,288]{1,0:T(8,128)} %get-tuple-element.98) | copy-start | bytes 110596
  75.6 5.1 %copy-start.26 = (s32[128,20]{0,1:T(8,128)S(1)}, s32[128,20]{0,1:T(8,128)}, u32[]{:S(2)}) copy-start(s32[128,20]{0,1:T(8,128)} %param.29) | copy-start | bytes 30724
  75.6 5.1 %copy-start.32 = (s32[128]{0:T(128)S(1)}, s32[128]{0:T(128)}, u32[]{:S(2)}) copy-start(s32[128]{0:T(128)} %param.28) | copy-start | bytes 1540
  75.6 6.4 %copy-start.4 = (bf16[384,256]{1,0:T(8,128)(2,1)S(1)}, bf16[384,256]{1,0:T(8,128)(2,1)}, u32[]{:S(2)}) copy-start(bf16[384,256]{1,0:T(8,128)(2,1)} %param.33) | copy-start | bytes 589828
  75.6 6.5 %copy-start.2 = (bf16[384,256]{1,0:T(8,128)(2,1)S(1)}, bf16[384,256]{1,0:T(8,128)(2,1)}, u32[]{:S(2)}) copy-start(bf16[384,256]{1,0:T(8,128)(2,1)} %param.34) | copy-start | bytes 589828
  75.6 39.8 %all-to-all-start.4 = ((bf16[32,88,256]{2,1,0:T(8,128)(2,1)}), bf16[32,88,256]{2,1,0:T(8,128)(2,1)S(1)}, u32[]{:S(2)}, u32[]{:S(2)}) async-start(bf16[32,88,256]{2,1,0:T(8,128)(2,1)} %add_convert_fusion), calls=%async_computation.4 | async-start | bytes 2883584 | tf_op jit(solution)/shard_map/all_to_all | solution.py:38
  79.8 6.2 %copy-start.6 = (bf16[384,256]{1,0:T(8,128)(2,1)S(1)}, bf16[384,256]{1,0:T(8,128)(2,1)}, u32[]{:S(2)}) copy-start(bf16[384,256]{1,0:T(8,128)(2,1)} %param.32) | copy-start | bytes 589828
  79.9 0.8 copy-start.16
  79.9 0.9 copy-start.20
  80.6 8.4 %copy-start.28 = (f32[128]{0:T(128)S(1)}, f32[128]{0:T(128)}, u32[]{:S(2)}) copy-start(f32[128]{0:T(128)} %param.31) | copy-start | bytes 1540
  80.8 0.6 copy-start.13
  124.8 11.3 %copy-start.27 = (f32[768]{0:T(1024)S(1)}, f32[768]{0:T(1024)}, u32[]{:S(2)}) copy-start(f32[768]{0:T(1024)} %param.41) | copy-start | bytes 9220
  124.8 11.9 %copy-start.1 = (f32[512,256]{1,0:T(8,128)S(1)}, f32[512,256]{1,0:T(8,128)}, u32[]{:S(2)}) copy-start(f32[512,256]{1,0:T(8,128)} %memory.1) | copy-start | bytes 1572868
  125.8 12.5 %copy-start.11 = (s32[32,32]{0,1:T(8,128)S(1)}, s32[32,32]{0,1:T(8,128)}, u32[]{:S(2)}) copy-start(s32[32,32]{0,1:T(8,128)} %copy-done.10) | copy-start | bytes 12292
  125.8 13.6 %copy-start.18 = (s32[32,32]{1,0:T(8,128)S(1)}, s32[32,32]{1,0:T(8,128)}, u32[]{:S(2)}) copy-start(s32[32,32]{1,0:T(8,128)} %get-tuple-element.107) | copy-start | bytes 12292
  125.8 31.9 %all-to-all-start.5 = ((bf16[512,2,256]{2,1,0:T(2,128)(2,1)}), bf16[512,2,256]{2,1,0:T(2,128)(2,1)S(1)}, u32[]{:S(2)}, u32[]{:S(2)}) async-start(bf16[512,2,256]{2,1,0:T(2,128)(2,1)} %reshape.256), calls=%async_computation.5 | async-start | bytes 1048576 | tf_op jit(solution)/shard_map/all_to_all | solution.py:38

commit v7 on v6

--- a/solution.py
+++ b/solution.py
@@ -294,30 +294,24 @@
         ).astype(jnp.bfloat16)
 
 
-def gru_kernel(news, owned, counts, memory, from_state, input_weight, bias, new_memory):
+def gru_kernel(news, owned, times, memory, from_state, input_weight, bias, new_memory):
     nodes, width = memory.shape
-    one = jnp.bfloat16(1)
-    none = jnp.bfloat16(0)
-    size = 128
-    numbers = lax.broadcasted_iota(jnp.int32, (size, owned.shape[1]), 0).astype(jnp.float32)
-    numbers = numbers.astype(jnp.bfloat16)
-    for low in range(0, nodes, size):
-        here = slice(low, low + size)
-        index = jnp.clip(owned[...] - low, -1, size).astype(jnp.float32).astype(jnp.bfloat16)
-        totals = jnp.dot(
-            jnp.where(numbers == index, one, none), news[...], preferred_element_type=jnp.float32
-        )
-        count = jnp.concatenate([counts[here, :]] * (width // LANES), 1)
-        averaged = (totals / jnp.maximum(count, 1.0)).astype(jnp.bfloat16)
-        from_msg = jnp.dot(averaged, input_weight[...], preferred_element_type=jnp.float32)
-        update, reset, last = (slice(i * width, (i + 1) * width) for i in range(3))
-        update_gate = jax.nn.sigmoid(from_msg[:, update] + from_state[here, update] + bias[:, update])
-        reset_gate = jax.nn.sigmoid(from_msg[:, reset] + from_state[here, reset] + bias[:, reset])
-        candidate = jnp.tanh(
-            from_msg[:, last] + bias[:, last] + reset_gate * from_state[here, last]
-        )
-        updated = (1.0 - update_gate) * candidate + update_gate * memory[here, :]
-        new_memory[here, :] = jnp.where(count > 0, updated, memory[here, :])
+    low = pl.program_id(0) * nodes
+    numbers = lax.broadcasted_iota(jnp.int32, (nodes, owned.shape[1]), 0).astype(jnp.float32)
+    index = jnp.clip(owned[...] - low, -1, nodes).astype(jnp.float32).astype(jnp.bfloat16)
+    chosen = jnp.where(numbers.astype(jnp.bfloat16) == index, jnp.bfloat16(1), jnp.bfloat16(0))
+    totals = jnp.dot(chosen, news[...], preferred_element_type=jnp.float32)
+    repeated = jnp.broadcast_to(times[...].astype(jnp.float32), (LANES, times.shape[1]))
+    count = across(chosen, repeated.astype(jnp.bfloat16))
+    count = jnp.concatenate([count] * (width // LANES), 1)
+    averaged = (totals / jnp.maximum(count, 1.0)).astype(jnp.bfloat16)
+    from_msg = jnp.dot(averaged, input_weight[...], preferred_element_type=jnp.float32)
+    update, reset, last = (slice(i * width, (i + 1) * width) for i in range(3))
+    update_gate = jax.nn.sigmoid(from_msg[:, update] + from_state[:, update] + bias[:, update])
+    reset_gate = jax.nn.sigmoid(from_msg[:, reset] + from_state[:, reset] + bias[:, reset])
+    candidate = jnp.tanh(from_msg[:, last] + bias[:, last] + reset_gate * from_state[:, last])
+    updated = (1.0 - update_gate) * candidate + update_gate * memory[...]
+    new_memory[...] = jnp.where(count > 0, updated, memory[...])
 
 
 def local(
@@ -405,13 +399,9 @@
         first[:, : members * CAP_E].reshape(groups, CAP_E, members), (2, 0, 1)
     ).reshape(members, ends)
     second = jnp.concatenate(
-        [
-            passed,
-            listed,
-            jnp.broadcast_to(most, (members, LANES - ends - CAP)),
-        ],
-        1,
-    )
+        [passed, listed, jnp.zeros((members, LANES - ends - CAP), jnp.int32)], 1
+    )
+    second = jnp.where(jnp.arange(LANES)[None, :] < ends + CAP, second, most)
     second = exchange(second, "dev")
     got_listed = second[:, ends : ends + CAP]
     most = jnp.max(second[:, ends + CAP :])
@@ -521,20 +511,26 @@
         slot_sum, ("grp", "dev")
     ).reshape(-1, row_width)
     owned = got_end.reshape(-1)
-    counts = jnp.sum(
-        jnp.where(
-            owned[None, :] == jnp.arange(nodes)[:, None], got_count.reshape(1, -1), 0
-        ),
-        axis=1,
-    ).astype(jnp.float32)
+    step = 128
     new_memory = pl.pallas_call(
         gru_kernel,
+        grid=(nodes // step,),
         out_shape=jax.ShapeDtypeStruct(memory.shape, memory.dtype),
+        in_specs=[
+            pl.BlockSpec(news.shape, lambda i: (0, 0)),
+            pl.BlockSpec((1, owned.shape[0]), lambda i: (0, 0)),
+            pl.BlockSpec((1, owned.shape[0]), lambda i: (0, 0)),
+            pl.BlockSpec((step, row_width), lambda i: (i, 0)),
+            pl.BlockSpec((step, 3 * row_width), lambda i: (i, 0)),
+            pl.BlockSpec(input_weight.shape, lambda i: (0, 0)),
+            pl.BlockSpec((1, 3 * row_width), lambda i: (0, 0)),
+        ],
+        out_specs=pl.BlockSpec((step, row_width), lambda i: (i, 0)),
         name="gru_kernel",
     )(
         news,
         owned[None, :],
-        jnp.broadcast_to(counts[:, None], (nodes, LANES)),
+        got_count.reshape(1, -1),
         memory,
         jnp.dot(mem_half, state_weight, preferred_element_type=jnp.float32),
         input_weight,

time: 164 us -> 164 us (level)
  no operation moved by 1% of the time
where the time goes in v7:
time: 164 us; the launch traced here: 163 us
  waiting for transfers between devices  70.5 us (43%)
  starting transfers between devices  41.3 us (25%)
  Pallas kernels  16.6 us (10%)
  local copies, waits for them, and re-layouts  13.9 us (8%)
  other arithmetic  11.7 us (7%)
  matrix products  7.74 us (5%)
  between operations  1.72 us (1%)
    all_to_all x5, waiting for transfers between devices, exchange(): return lax.all_to_all(x, axis, split_axis=0, concat_axis=0, tiled=True)  70.5 us
    all_to_all x5, starting transfers between devices, exchange(): return lax.all_to_all(x, axis, split_axis=0, concat_axis=0, tiled=True)  41.3 us
    pallas_call x1, Pallas kernels, listed_only(): pl.pallas_call(event_kernel, out_shape=(jax.ShapeDtypeStruct((events, 2 *...  9.32 us
    unnamed x46, local copies, waits for them, and re-layouts  7.65 us
    convert_element_type x1, other arithmetic, local(): code.astype(jnp.bfloat16)  5.4 us
    pallas_call x1, Pallas kernels, local(): pl.pallas_call(gru_kernel, grid=(nodes // step,), out_shape=jax.ShapeDtyp...  4.77 us
  transfers between devices with their start and end apart: 5, of which 5 were waited for; matrix products, arithmetic and copies ran while one was open for 13% of the time, Pallas kernels for 0%

profile of v7, /device:TPU:1, one launch (start us, length us, event | category | flops | bytes accessed | tf_op | source)
XLA Modules:
  0.0 163.4 jit_solution(9171198733780294931)
XLA Ops:
  0.6 2.5 %request_kernel.1 = (s32[16,128]{1,0:T(8,128)}, s32[32,288]{1,0:T(8,128)}) custom-call(s32[1]{0:T(128)} %bitcast.21.mine, s32[20,128]{1,0:T(8,128)} %bitcast.133, s32[2,128]{1,0:T(2,128)} %bitcast.148, s32[2,128]{1,0:T(2,128)} %bitcast.143, s32[2,512]{1,0:T(2,128)} %bitcast.155, s32[16,512]{1,0:T(8,128)} %bitcast.142), custom_call_target="tpu_custom_call" | custom-call | tf_op jit(solution)/shard_map/request_kernel/pallas_call | solution.py:351
  3.2 10.1 %all-to-all-start.1 = ((s32[16,1,128]{2,1,0:T(1,128)}), s32[16,1,128]{2,1,0:T(1,128)S(1)}, u32[]{:S(2)}, u32[]{:S(2)}) async-start(s32[16,1,128]{2,1,0:T(1,128)} %bitcast.154), calls=%async_computation.1 | async-start | bytes 16384 | tf_op jit(solution)/shard_map/all_to_all | solution.py:38
  13.3 1.4 select_reduce_fusion
  14.8 5.5 %all-to-all-done.1 = s32[16,1,128]{2,1,0:T(1,128)S(1)} async-done(((s32[16,1,128]{2,1,0:T(1,128)}), s32[16,1,128]{2,1,0:T(1,128)S(1)}, u32[]{:S(2)}, u32[]{:S(2)}) %all-to-all-start.1) | async-done | bytes 8224 | tf_op jit(solution)/shard_map/all_to_all | solution.py:38
  20.3 0.8 slice_reduce_fusion.1
  21.2 1.4 add_select_fusion.1
  22.6 11.4 %all-to-all-start.2 = ((s32[32,1,128]{2,1,0:T(1,128)}), s32[32,1,128]{2,1,0:T(1,128)S(1)}, u32[]{:S(2)}, u32[]{:S(2)}) async-start(s32[32,1,128]{2,1,0:T(1,128)} %bitcast.35), calls=%async_computation.2 | async-start | bytes 32768 | tf_op jit(solution)/shard_map/all_to_all | solution.py:38
  34.0 8.5 %all-to-all-done.2 = s32[32,1,128]{2,1,0:T(1,128)S(1)} async-done(((s32[32,1,128]{2,1,0:T(1,128)}), s32[32,1,128]{2,1,0:T(1,128)S(1)}, u32[]{:S(2)}, u32[]{:S(2)}) %all-to-all-start.2) | async-done | bytes 16416 | tf_op jit(solution)/shard_map/all_to_all | solution.py:38
  43.5 2.5 %fusion.53 = bf16[1280,256]{1,0:T(8,128)(2,1)} fusion(s32[1280]{0:T(1024)S(1)} %eq.87, f32[512,256]{1,0:T(8,128)} %memory.1), kind=kOutput, calls=%fused_computation.77 | convolution fusion | flops 336658432 | bytes 1184768 | tf_op jit(solution)/shard_map/dot_general | solution.py:26
  46.0 5.5 %all-to-all-start.3 = ((bf16[16,80,256]{2,1,0:T(8,128)(2,1)}), bf16[16,80,256]{2,1,0:T(8,128)(2,1)S(1)}, u32[]{:S(2)}, u32[]{:S(2)}) async-start(bf16[16,80,256]{2,1,0:T(8,128)(2,1)} %bitcast.41), calls=%async_computation.3 | async-start | bytes 1310720 | tf_op jit(solution)/shard_map/all_to_all | solution.py:38
  51.6 20.0 %all-to-all-done.3 = bf16[16,80,256]{2,1,0:T(8,128)(2,1)S(1)} async-done(((bf16[16,80,256]{2,1,0:T(8,128)(2,1)}), bf16[16,80,256]{2,1,0:T(8,128)(2,1)S(1)}, u32[]{:S(2)}, u32[]{:S(2)}) %all-to-all-start.3) | async-done | bytes 655392 | tf_op jit(solution)/shard_map/all_to_all | solution.py:38
  72.6 1.2 fusion.50
  73.9 1.7 %add_convert_fusion = bf16[32,88,256]{2,1,0:T(8,128)(2,1)} fusion(f32[32,88,256]{2,1,0:T(8,128)S(1)} %fusion.50, bf16[32,32,256]{2,1,0:T(8,128)(2,1)S(1)} %reshape.300, s32[32,88]{1,0:T(8,128)S(1)} %get-tuple-element.117), kind=kOutput, calls=%fused_computation.71 | convolution fusion | flops 47669248 | bytes 4860928 | tf_op jit(solution)/shard_map/dcp,dpw->dcw/dot_general | solution.py:422
  75.7 4.1 %all-to-all-start.4 = ((bf16[32,88,256]{2,1,0:T(8,128)(2,1)}), bf16[32,88,256]{2,1,0:T(8,128)(2,1)S(1)}, u32[]{:S(2)}, u32[]{:S(2)}) async-start(bf16[32,88,256]{2,1,0:T(8,128)(2,1)} %add_convert_fusion), calls=%async_computation.4 | async-start | bytes 2883584 | tf_op jit(solution)/shard_map/all_to_all | solution.py:38
  79.9 0.7 fusion.57
  82.3 1.8 %copy.136 = bf16[512,256]{0,1:T(8,128)(2,1)} copy(bf16[512,256]{1,0:T(8,128)(2,1)} %param.35) | data formatting | bytes 524288 | tf_op args[13]
  84.1 1.8 %copy.137 = bf16[512,256]{0,1:T(8,128)(2,1)} copy(bf16[512,256]{1,0:T(8,128)(2,1)} %param.37) | data formatting | bytes 524288 | tf_op args[15]
  85.9 0.8 copy.133
  86.8 1.7 %copy.138 = bf16[256,256]{0,1:T(8,128)(2,1)} copy(bf16[256,256]{1,0:T(8,128)(2,1)} %param.38) | data formatting | bytes 262144 | tf_op args[16]
  89.6 5.4 %cosine_convert_fusion.2 = bf16[10,128,256]{2,1,0:T(8,128)(2,1)S(1)} fusion(f32[128]{0:T(128)} %param.31, f32[128]{0:T(128)} %param.30, f32[10,256]{1,0:T(8,128)} %bitcast.140), kind=kLoop, calls=%fused_computation.80 | loop fusion | flops 983040 | bytes 666624 | tf_op jit(solution)/shard_map/convert_element_type | solution.py:480
  95.0 0.7 slice_reduce_fusion
  96.4 19.1 %all-to-all-done.4 = bf16[32,88,256]{2,1,0:T(8,128)(2,1)S(1)} async-done(((bf16[32,88,256]{2,1,0:T(8,128)(2,1)}), bf16[32,88,256]{2,1,0:T(8,128)(2,1)S(1)}, u32[]{:S(2)}, u32[]{:S(2)}) %all-to-all-start.4) | async-done | bytes 1441824 | tf_op jit(solution)/shard_map/all_to_all | solution.py:38
  115.5 9.3 %conditional.1 = ((bf16[128,512]{1,0:T(8,128)(2,1)}, bf16[1024,256]{1,0:T(8,128)(2,1)S(1)})) conditional(s32[]{:T(128)} %convert_element_type.66, (bf16[32,88,256]{2,1,0:T(8,128)(2,1)S(1)}, s32[2,128]{1,0:T(2,128)}, s32[2,128]{1,0:T(2,128)}, bf16[128]{0:T(256)(128)(2,1)}, f32[256]{0:T(256)}, /*index=5*/s32[2816]{0:T(1024)}, ...), branch_computations={%region_4.5_spmd, %region_5.12_spmd} | conditional | flops 1517661824 | bytes 61769664 | solution.py:509
  115.5 9.3 %event_kernel.1 = (bf16[128,512]{1,0:T(8,128)(2,1)}, bf16[1024,256]{1,0:T(8,128)(2,1)S(1)}) custom-call(s32[2816]{0:T(1024)} %get-tuple-element.63.lanes, bf16[2816,256]{1,0:T(8,128)(2,1)S(1)} %bitcast.113, s32[1,256]{1,0:T(1,128)} %bitcast.147, s32[1,256]{1,0:T(1,128)} %bitcast.151, bf16[10,128,256]{2,1,0:T(8,128)(2,1)S(1)} %get-tuple-element.67.code, ...), custom_call_target="tpu_custom_call" | custom-call | tf_op jit(solution)/shard_map/cond/branch_0_fun/event_kernel/pallas_call | solution.py:491
  124.8 1.0 reshape.304
  125.8 10.3 %all-to-all-start.5 = ((bf16[512,2,256]{2,1,0:T(2,128)(2,1)}), bf16[512,2,256]{2,1,0:T(2,128)(2,1)S(1)}, u32[]{:S(2)}, u32[]{:S(2)}) async-start(bf16[512,2,256]{2,1,0:T(2,128)(2,1)} %reshape.304), calls=%async_computation.5 | async-start | bytes 1048576 | tf_op jit(solution)/shard_map/all_to_all | solution.py:38
  136.7 1.6 fusion.60.from_state
  138.5 0.8 select_n.93.owned
  139.5 0.8 select_n.97.times
  140.3 17.4 %all-to-all-done.5 = bf16[512,2,256]{2,1,0:T(2,128)(2,1)S(1)} async-done(((bf16[512,2,256]{2,1,0:T(2,128)(2,1)}), bf16[512,2,256]{2,1,0:T(2,128)(2,1)S(1)}, u32[]{:S(2)}, u32[]{:S(2)}) %all-to-all-start.5) | async-done | bytes 524320 | tf_op jit(solution)/shard_map/all_to_all | solution.py:38
  157.7 1.0 reshape.305.news
  158.6 4.8 %gru_kernel.1 = f32[512,256]{1,0:T(8,128)} custom-call(bf16[1024,256]{1,0:T(8,128)(2,1)} %reshape.305.news, s32[1,1024]{1,0:T(1,128)} %select_n.93.owned, s32[1,1024]{1,0:T(1,128)} %select_n.97.times, f32[512,256]{1,0:T(8,128)} %memory.1, f32[512,768]{1,0:T(8,128)} %fusion.60.from_state, bf16[256,768]{1,0:T(8,128)(2,1)} %input_weight.1, ...), custom_call_target="tpu_custom_call" | custom-call | tf_op jit(solution)/shard_map/gru_kernel/pallas_call | solution.py:515
  (82 shorter events, 6.3 us)
Async XLA Ops:
  0.6 136.1 %copy-start = (bf16[256,768]{1,0:T(8,128)(2,1)S(1)}, bf16[256,768]{1,0:T(8,128)(2,1)}, u32[]{:S(2)}) copy-start(bf16[256,768]{1,0:T(8,128)(2,1)} %param.40) | copy-start | bytes 1179652
  3.2 17.1 %all-to-all-start.1 = ((s32[16,1,128]{2,1,0:T(1,128)}), s32[16,1,128]{2,1,0:T(1,128)S(1)}, u32[]{:S(2)}, u32[]{:S(2)}) async-start(s32[16,1,128]{2,1,0:T(1,128)} %bitcast.154), calls=%async_computation.1 | async-start | bytes 16384 | tf_op jit(solution)/shard_map/all_to_all | solution.py:38
  22.6 20.0 %all-to-all-start.2 = ((s32[32,1,128]{2,1,0:T(1,128)}), s32[32,1,128]{2,1,0:T(1,128)S(1)}, u32[]{:S(2)}, u32[]{:S(2)}) async-start(s32[32,1,128]{2,1,0:T(1,128)} %bitcast.35), calls=%async_computation.2 | async-start | bytes 32768 | tf_op jit(solution)/shard_map/all_to_all | solution.py:38
  43.2 28.3 %copy-start.10 = (s32[32,32]{0,1:T(8,128)}, s32[32,32]{0,1:T(8,128)S(1)}, u32[]{:S(2)}) copy-start(s32[32,32]{0,1:T(8,128)S(1)} %copy.127) | copy-start | bytes 12292
  46.0 25.5 %all-to-all-start.3 = ((bf16[16,80,256]{2,1,0:T(8,128)(2,1)}), bf16[16,80,256]{2,1,0:T(8,128)(2,1)S(1)}, u32[]{:S(2)}, u32[]{:S(2)}) async-start(bf16[16,80,256]{2,1,0:T(8,128)(2,1)} %bitcast.41), calls=%async_computation.3 | async-start | bytes 1310720 | tf_op jit(solution)/shard_map/all_to_all | solution.py:38
  75.6 4.2 %copy-start.22 = (s32[128,2]{0,1:T(2,128)S(1)}, s32[128,2]{0,1:T(2,128)}, u32[]{:S(2)}) copy-start(s32[128,2]{0,1:T(2,128)} %param.27) | copy-start | bytes 3076
  75.6 4.2 %copy-start.24 = (s32[128,2]{0,1:T(2,128)S(1)}, s32[128,2]{0,1:T(2,128)}, u32[]{:S(2)}) copy-start(s32[128,2]{0,1:T(2,128)} %param.25) | copy-start | bytes 3076
  75.6 4.2 %copy-start.15 = (s32[128,20]{0,1:T(8,128)S(1)}, s32[128,20]{0,1:T(8,128)}, u32[]{:S(2)}) copy-start(s32[128,20]{0,1:T(8,128)} %param.26) | copy-start | bytes 30724
  75.6 4.3 %copy-start.19 = (s32[32,288]{1,0:T(8,128)S(1)}, s32[32,288]{1,0:T(8,128)}, u32[]{:S(2)}) copy-start(s32[32,288]{1,0:T(8,128)} %get-tuple-element.98) | copy-start | bytes 110596
  75.6 5.1 %copy-start.26 = (s32[128,20]{0,1:T(8,128)S(1)}, s32[128,20]{0,1:T(8,128)}, u32[]{:S(2)}) copy-start(s32[128,20]{0,1:T(8,128)} %param.29) | copy-start | bytes 30724
  75.6 5.1 %copy-start.32 = (s32[128]{0:T(128)S(1)}, s32[128]{0:T(128)}, u32[]{:S(2)}) copy-start(s32[128]{0:T(128)} %param.28) | copy-start | bytes 1540
  75.6 6.4 %copy-start.4 = (bf16[384,256]{1,0:T(8,128)(2,1)S(1)}, bf16[384,256]{1,0:T(8,128)(2,1)}, u32[]{:S(2)}) copy-start(bf16[384,256]{1,0:T(8,128)(2,1)} %param.33) | copy-start | bytes 589828
  75.6 6.5 %copy-start.2 = (bf16[384,256]{1,0:T(8,128)(2,1)S(1)}, bf16[384,256]{1,0:T(8,128)(2,1)}, u32[]{:S(2)}) copy-start(bf16[384,256]{1,0:T(8,128)(2,1)} %param.34) | copy-start | bytes 589828
  75.7 39.8 %all-to-all-start.4 = ((bf16[32,88,256]{2,1,0:T(8,128)(2,1)}), bf16[32,88,256]{2,1,0:T(8,128)(2,1)S(1)}, u32[]{:S(2)}, u32[]{:S(2)}) async-start(bf16[32,88,256]{2,1,0:T(8,128)(2,1)} %add_convert_fusion), calls=%async_computation.4 | async-start | bytes 2883584 | tf_op jit(solution)/shard_map/all_to_all | solution.py:38
  79.8 6.2 %copy-start.6 = (bf16[384,256]{1,0:T(8,128)(2,1)S(1)}, bf16[384,256]{1,0:T(8,128)(2,1)}, u32[]{:S(2)}) copy-start(bf16[384,256]{1,0:T(8,128)(2,1)} %param.32) | copy-start | bytes 589828
  79.9 0.8 copy-start.16
  79.9 0.9 copy-start.20
  80.6 8.4 %copy-start.28 = (f32[128]{0:T(128)S(1)}, f32[128]{0:T(128)}, u32[]{:S(2)}) copy-start(f32[128]{0:T(128)} %param.31) | copy-start | bytes 1540
  80.8 0.6 copy-start.13
  124.8 11.3 %copy-start.27 = (f32[768]{0:T(1024)S(1)}, f32[768]{0:T(1024)}, u32[]{:S(2)}) copy-start(f32[768]{0:T(1024)} %param.41) | copy-start | bytes 9220
  124.8 11.9 %copy-start.1 = (f32[512,256]{1,0:T(8,128)S(1)}, f32[512,256]{1,0:T(8,128)}, u32[]{:S(2)}) copy-start(f32[512,256]{1,0:T(8,128)} %memory.1) | copy-start | bytes 1572868
  125.8 12.5 %copy-start.11 = (s32[32,32]{0,1:T(8,128)S(1)}, s32[32,32]{0,1:T(8,128)}, u32[]{:S(2)}) copy-start(s32[32,32]{0,1:T(8,128)} %copy-done.10) | copy-start | bytes 12292
  125.8 13.4 %copy-start.18 = (s32[32,32]{1,0:T(8,128)S(1)}, s32[32,32]{1,0:T(8,128)}, u32[]{:S(2)}) copy-start(s32[32,32]{1,0:T(8,128)} %get-tuple-element.107) | copy-start | bytes 12292
  125.8 31.8 %all-to-all-start.5 = ((bf16[512,2,256]{2,1,0:T(2,128)(2,1)}), bf16[512,2,256]{2,1,0:T(2,128)(2,1)S(1)}, u32[]{:S(2)}, u32[]{:S(2)}) async-start(bf16[512,2,256]{2,1,0:T(2,128)(2,1)} %reshape.304), calls=%async_computation.5 | async-start | bytes 1048576 | tf_op jit(solution)/shard_map/all_to_all | solution.py:38

commit v8 on v7

--- a/solution.py
+++ b/solution.py
@@ -343,7 +343,7 @@
     block = groups * CAP_N
     ends = groups * CAP_E
     places = block + ends
-    mem_half = memory.astype(jnp.bfloat16)
+    mem_half = lax.optimization_barrier(memory.astype(jnp.bfloat16))
     counted = jnp.transpose(near_count)
 
     near_value = jnp.transpose(near_slot)
@@ -416,16 +416,14 @@
     end_part = jnp.transpose(
         rows[:, CAP_N:].reshape(groups, members, CAP_E, row_width), (1, 0, 2, 3)
     ).reshape(members, ends, row_width)
-    near_part = jnp.dot(
-        hot(got_listed.reshape(-1), block, 1), near_block, preferred_element_type=jnp.float32
-    ).reshape(members, CAP, row_width)
+    near_part = pick(got_listed.reshape(-1), near_block).reshape(members, CAP, row_width)
     listed_ends = jnp.einsum(
         "dcp,dpw->dcw",
         hot(got_listed - block, ends, 2),
         end_part,
         preferred_element_type=jnp.float32,
     )
-    table = exchange((near_part + listed_ends).astype(jnp.bfloat16), "dev")
+    table = exchange(near_part + listed_ends.astype(jnp.bfloat16), "dev")
     table = table.reshape(members * CAP, row_width)
 
     elapsed = (event_time[None, :] - jnp.transpose(near_time)).astype(jnp.float32)

time: 164 us -> 163 us (level)
    unnamed x46 -> x50, local copies, waits for them, and re-layouts: 7.65 us -> 7.66 us
  transfers between devices with their start and end apart: 5 -> 5, of which waited for: 5 -> 5; matrix products, arithmetic and copies ran while one was open for 13% -> 14% of each run, Pallas kernels for 0% -> 0%
where the time goes in v8:
time: 163 us; the launch traced here: 162 us
  waiting for transfers between devices  69.3 us (43%)
  starting transfers between devices  41.4 us (25%)
  Pallas kernels  15.9 us (10%)
  local copies, waits for them, and re-layouts  13.9 us (9%)
  other arithmetic  12.7 us (8%)
  matrix products  7.01 us (4%)
  between operations  1.73 us (1%)
    all_to_all x5, waiting for transfers between devices, exchange(): return lax.all_to_all(x, axis, split_axis=0, concat_axis=0, tiled=True)  69.3 us
    all_to_all x5, starting transfers between devices, exchange(): return lax.all_to_all(x, axis, split_axis=0, concat_axis=0, tiled=True)  41.4 us
    pallas_call x1, Pallas kernels, listed_only(): pl.pallas_call(event_kernel, out_shape=(jax.ShapeDtypeStruct((events, 2 *...  8.65 us
    unnamed x50, local copies, waits for them, and re-layouts  7.66 us
    convert_element_type x1, other arithmetic, local(): code.astype(jnp.bfloat16)  5.4 us
    pallas_call x1, Pallas kernels, local(): pl.pallas_call(gru_kernel, grid=(nodes // step,), out_shape=jax.ShapeDtyp...  4.77 us
  transfers between devices with their start and end apart: 5, of which 5 were waited for; matrix products, arithmetic and copies ran while one was open for 14% of the time, Pallas kernels for 0%

profile of v8, /device:TPU:1, one launch (start us, length us, event | category | flops | bytes accessed | tf_op | source)
XLA Modules:
  0.0 162.2 jit_solution(10241741859954904576)
XLA Ops:
  0.6 2.5 %request_kernel.1 = (s32[16,128]{1,0:T(8,128)}, s32[32,288]{1,0:T(8,128)}) custom-call(s32[1]{0:T(128)} %bitcast.21.mine, s32[20,128]{1,0:T(8,128)} %bitcast.132, s32[2,128]{1,0:T(2,128)} %bitcast.147, s32[2,128]{1,0:T(2,128)} %bitcast.142, s32[2,512]{1,0:T(2,128)} %bitcast.154, s32[16,512]{1,0:T(8,128)} %bitcast.141), custom_call_target="tpu_custom_call" | custom-call | tf_op jit(solution)/shard_map/request_kernel/pallas_call | solution.py:351
  3.2 10.1 %all-to-all-start.1 = ((s32[16,1,128]{2,1,0:T(1,128)}), s32[16,1,128]{2,1,0:T(1,128)S(1)}, u32[]{:S(2)}, u32[]{:S(2)}) async-start(s32[16,1,128]{2,1,0:T(1,128)} %bitcast.153), calls=%async_computation.1 | async-start | bytes 16384 | tf_op jit(solution)/shard_map/all_to_all | solution.py:38
  13.3 1.4 select_reduce_fusion
  14.8 5.5 %all-to-all-done.1 = s32[16,1,128]{2,1,0:T(1,128)S(1)} async-done(((s32[16,1,128]{2,1,0:T(1,128)}), s32[16,1,128]{2,1,0:T(1,128)S(1)}, u32[]{:S(2)}, u32[]{:S(2)}) %all-to-all-start.1) | async-done | bytes 8224 | tf_op jit(solution)/shard_map/all_to_all | solution.py:38
  20.3 0.8 slice_reduce_fusion.1
  21.2 1.3 add_select_fusion.1
  22.5 11.4 %all-to-all-start.2 = ((s32[32,1,128]{2,1,0:T(1,128)}), s32[32,1,128]{2,1,0:T(1,128)S(1)}, u32[]{:S(2)}, u32[]{:S(2)}) async-start(s32[32,1,128]{2,1,0:T(1,128)} %bitcast.35), calls=%async_computation.2 | async-start | bytes 32768 | tf_op jit(solution)/shard_map/all_to_all | solution.py:38
  33.9 1.1 convert_element_type.70
  35.0 7.4 %all-to-all-done.2 = s32[32,1,128]{2,1,0:T(1,128)S(1)} async-done(((s32[32,1,128]{2,1,0:T(1,128)}), s32[32,1,128]{2,1,0:T(1,128)S(1)}, u32[]{:S(2)}, u32[]{:S(2)}) %all-to-all-start.2) | async-done | bytes 16416 | tf_op jit(solution)/shard_map/all_to_all | solution.py:38
  43.5 1.4 fusion.50
  44.9 5.5 %all-to-all-start.3 = ((bf16[16,80,256]{2,1,0:T(8,128)(2,1)}), bf16[16,80,256]{2,1,0:T(8,128)(2,1)S(1)}, u32[]{:S(2)}, u32[]{:S(2)}) async-start(bf16[16,80,256]{2,1,0:T(8,128)(2,1)} %bitcast.40), calls=%async_computation.3 | async-start | bytes 1310720 | tf_op jit(solution)/shard_map/all_to_all | solution.py:38
  50.6 19.9 %all-to-all-done.3 = bf16[16,80,256]{2,1,0:T(8,128)(2,1)S(1)} async-done(((bf16[16,80,256]{2,1,0:T(8,128)(2,1)}), bf16[16,80,256]{2,1,0:T(8,128)(2,1)S(1)}, u32[]{:S(2)}, u32[]{:S(2)}) %all-to-all-start.3) | async-done | bytes 655392 | tf_op jit(solution)/shard_map/all_to_all | solution.py:38
  71.5 1.5 convolution_convert_fusion
  73.0 1.7 %fusion.52 = bf16[32,88,256]{2,1,0:T(8,128)(2,1)} fusion(bf16[32,88,256]{2,1,0:T(8,128)(2,1)S(1)} %bitcast.113, bf16[32,32,256]{2,1,0:T(8,128)(2,1)S(1)} %reshape.283, s32[32,88]{1,0:T(8,128)S(1)} %get-tuple-element.117), kind=kOutput, calls=%fused_computation.78 | convolution fusion | flops 47669248 | bytes 3419136 | tf_op jit(solution)/shard_map/dcp,dpw->dcw/dot_general | solution.py:420
  74.9 4.1 %all-to-all-start.4 = ((bf16[32,88,256]{2,1,0:T(8,128)(2,1)}), bf16[32,88,256]{2,1,0:T(8,128)(2,1)S(1)}, u32[]{:S(2)}, u32[]{:S(2)}) async-start(bf16[32,88,256]{2,1,0:T(8,128)(2,1)} %fusion.52), calls=%async_computation.4 | async-start | bytes 2883584 | tf_op jit(solution)/shard_map/all_to_all | solution.py:38
  81.5 1.8 %copy.135 = bf16[512,256]{0,1:T(8,128)(2,1)} copy(bf16[512,256]{1,0:T(8,128)(2,1)} %param.35) | data formatting | bytes 524288 | tf_op args[13]
  83.3 1.8 %copy.136 = bf16[512,256]{0,1:T(8,128)(2,1)} copy(bf16[512,256]{1,0:T(8,128)(2,1)} %param.37) | data formatting | bytes 524288 | tf_op args[15]
  85.1 0.8 copy.132
  86.0 1.7 %copy.137 = bf16[256,256]{0,1:T(8,128)(2,1)} copy(bf16[256,256]{1,0:T(8,128)(2,1)} %param.38) | data formatting | bytes 262144 | tf_op args[16]
  88.8 5.4 %cosine_convert_fusion.2 = bf16[10,128,256]{2,1,0:T(8,128)(2,1)S(1)} fusion(f32[128]{0:T(128)} %param.31, f32[128]{0:T(128)} %param.30, f32[10,256]{1,0:T(8,128)} %bitcast.139), kind=kLoop, calls=%fused_computation.80 | loop fusion | flops 983040 | bytes 666624 | tf_op jit(solution)/shard_map/convert_element_type | solution.py:478
  94.2 0.7 slice_reduce_fusion
  95.6 19.1 %all-to-all-done.4 = bf16[32,88,256]{2,1,0:T(8,128)(2,1)S(1)} async-done(((bf16[32,88,256]{2,1,0:T(8,128)(2,1)}), bf16[32,88,256]{2,1,0:T(8,128)(2,1)S(1)}, u32[]{:S(2)}, u32[]{:S(2)}) %all-to-all-start.4) | async-done | bytes 1441824 | tf_op jit(solution)/shard_map/all_to_all | solution.py:38
  114.7 8.9 %conditional.1 = ((bf16[128,512]{1,0:T(8,128)(2,1)S(1)}, bf16[1024,256]{1,0:T(8,128)(2,1)S(1)})) conditional(s32[]{:T(128)} %convert_element_type.69, (bf16[32,88,256]{2,1,0:T(8,128)(2,1)S(1)}, s32[2,128]{1,0:T(2,128)}, s32[2,128]{1,0:T(2,128)}, bf16[128]{0:T(256)(128)(2,1)}, f32[256]{0:T(256)}, /*index=5*/s32[2816]{0:T(1024)}, ...), branch_computations={%region_4.5_spmd, %region_5.12_spmd} | conditional | flops 1517661824 | bytes 61769664 | solution.py:507
  114.7 8.6 %event_kernel.1 = (bf16[128,512]{1,0:T(8,128)(2,1)S(1)}, bf16[1024,256]{1,0:T(8,128)(2,1)S(1)}) custom-call(s32[2816]{0:T(1024)} %get-tuple-element.63.lanes, bf16[2816,256]{1,0:T(8,128)(2,1)S(1)} %bitcast.111, s32[1,256]{1,0:T(1,128)} %bitcast.146, s32[1,256]{1,0:T(1,128)} %bitcast.150, bf16[10,128,256]{2,1,0:T(8,128)(2,1)S(1)} %get-tuple-element.67.code, ...), custom_call_target="tpu_custom_call" | custom-call | tf_op jit(solution)/shard_map/cond/branch_0_fun/event_kernel/pallas_call | solution.py:489
  123.6 1.0 reshape.287
  124.6 10.3 %all-to-all-start.5 = ((bf16[512,2,256]{2,1,0:T(2,128)(2,1)}), bf16[512,2,256]{2,1,0:T(2,128)(2,1)S(1)}, u32[]{:S(2)}, u32[]{:S(2)}) async-start(bf16[512,2,256]{2,1,0:T(2,128)(2,1)} %reshape.287), calls=%async_computation.5 | async-start | bytes 1048576 | tf_op jit(solution)/shard_map/all_to_all | solution.py:38
  135.6 1.6 fusion.61.from_state
  137.3 0.8 select_n.93.owned
  138.3 0.8 select_n.97.times
  139.1 17.4 %all-to-all-done.5 = bf16[512,2,256]{2,1,0:T(2,128)(2,1)S(1)} async-done(((bf16[512,2,256]{2,1,0:T(2,128)(2,1)}), bf16[512,2,256]{2,1,0:T(2,128)(2,1)S(1)}, u32[]{:S(2)}, u32[]{:S(2)}) %all-to-all-start.5) | async-done | bytes 524320 | tf_op jit(solution)/shard_map/all_to_all | solution.py:38
  156.5 1.0 reshape.288.news
  157.5 4.8 %gru_kernel.1 = f32[512,256]{1,0:T(8,128)} custom-call(bf16[1024,256]{1,0:T(8,128)(2,1)} %reshape.288.news, s32[1,1024]{1,0:T(1,128)} %select_n.93.owned, s32[1,1024]{1,0:T(1,128)} %select_n.97.times, f32[512,256]{1,0:T(8,128)} %memory.1, f32[512,768]{1,0:T(8,128)} %fusion.61.from_state, bf16[256,768]{1,0:T(8,128)(2,1)} %input_weight.1, ...), custom_call_target="tpu_custom_call" | custom-call | tf_op jit(solution)/shard_map/gru_kernel/pallas_call | solution.py:513
  (88 shorter events, 7.1 us)
Async XLA Ops:
  0.6 134.9 %copy-start = (bf16[256,768]{1,0:T(8,128)(2,1)S(1)}, bf16[256,768]{1,0:T(8,128)(2,1)}, u32[]{:S(2)}) copy-start(bf16[256,768]{1,0:T(8,128)(2,1)} %param.40) | copy-start | bytes 1179652
  3.2 17.1 %all-to-all-start.1 = ((s32[16,1,128]{2,1,0:T(1,128)}), s32[16,1,128]{2,1,0:T(1,128)S(1)}, u32[]{:S(2)}, u32[]{:S(2)}) async-start(s32[16,1,128]{2,1,0:T(1,128)} %bitcast.153), calls=%async_computation.1 | async-start | bytes 16384 | tf_op jit(solution)/shard_map/all_to_all | solution.py:38
  22.5 20.0 %all-to-all-start.2 = ((s32[32,1,128]{2,1,0:T(1,128)}), s32[32,1,128]{2,1,0:T(1,128)S(1)}, u32[]{:S(2)}, u32[]{:S(2)}) async-start(s32[32,1,128]{2,1,0:T(1,128)} %bitcast.35), calls=%async_computation.2 | async-start | bytes 32768 | tf_op jit(solution)/shard_map/all_to_all | solution.py:38
  35.0 10.0 %copy-start.1 = (bf16[512,256]{1,0:T(8,128)(2,1)}, bf16[512,256]{1,0:T(8,128)(2,1)S(1)}, u32[]{:S(2)}) copy-start(bf16[512,256]{1,0:T(8,128)(2,1)S(1)} %convert_element_type.70) | copy-start | bytes 786436
  43.2 27.3 %copy-start.11 = (s32[32,32]{0,1:T(8,128)}, s32[32,32]{0,1:T(8,128)S(1)}, u32[]{:S(2)}) copy-start(s32[32,32]{0,1:T(8,128)S(1)} %copy.126) | copy-start | bytes 12292
  44.9 25.5 %all-to-all-start.3 = ((bf16[16,80,256]{2,1,0:T(8,128)(2,1)}), bf16[16,80,256]{2,1,0:T(8,128)(2,1)S(1)}, u32[]{:S(2)}, u32[]{:S(2)}) async-start(bf16[16,80,256]{2,1,0:T(8,128)(2,1)} %bitcast.40), calls=%async_computation.3 | async-start | bytes 1310720 | tf_op jit(solution)/shard_map/all_to_all | solution.py:38
  74.8 4.2 %copy-start.23 = (s32[128,2]{0,1:T(2,128)S(1)}, s32[128,2]{0,1:T(2,128)}, u32[]{:S(2)}) copy-start(s32[128,2]{0,1:T(2,128)} %param.27) | copy-start | bytes 3076
  74.8 4.2 %copy-start.25 = (s32[128,2]{0,1:T(2,128)S(1)}, s32[128,2]{0,1:T(2,128)}, u32[]{:S(2)}) copy-start(s32[128,2]{0,1:T(2,128)} %param.25) | copy-start | bytes 3076
  74.8 4.2 %copy-start.16 = (s32[128,20]{0,1:T(8,128)S(1)}, s32[128,20]{0,1:T(8,128)}, u32[]{:S(2)}) copy-start(s32[128,20]{0,1:T(8,128)} %param.26) | copy-start | bytes 30724
  74.8 4.3 %copy-start.20 = (s32[32,288]{1,0:T(8,128)S(1)}, s32[32,288]{1,0:T(8,128)}, u32[]{:S(2)}) copy-start(s32[32,288]{1,0:T(8,128)} %get-tuple-element.98) | copy-start | bytes 110596
  74.8 5.1 %copy-start.27 = (s32[128,20]{0,1:T(8,128)S(1)}, s32[128,20]{0,1:T(8,128)}, u32[]{:S(2)}) copy-start(s32[128,20]{0,1:T(8,128)} %param.29) | copy-start | bytes 30724
  74.8 5.1 %copy-start.33 = (s32[128]{0:T(128)S(1)}, s32[128]{0:T(128)}, u32[]{:S(2)}) copy-start(s32[128]{0:T(128)} %param.28) | copy-start | bytes 1540
  74.8 6.4 %copy-start.5 = (bf16[384,256]{1,0:T(8,128)(2,1)S(1)}, bf16[384,256]{1,0:T(8,128)(2,1)}, u32[]{:S(2)}) copy-start(bf16[384,256]{1,0:T(8,128)(2,1)} %param.33) | copy-start | bytes 589828
  74.8 6.5 %copy-start.3 = (bf16[384,256]{1,0:T(8,128)(2,1)S(1)}, bf16[384,256]{1,0:T(8,128)(2,1)}, u32[]{:S(2)}) copy-start(bf16[384,256]{1,0:T(8,128)(2,1)} %param.34) | copy-start | bytes 589828
  74.9 39.8 %all-to-all-start.4 = ((bf16[32,88,256]{2,1,0:T(8,128)(2,1)}), bf16[32,88,256]{2,1,0:T(8,128)(2,1)S(1)}, u32[]{:S(2)}, u32[]{:S(2)}) async-start(bf16[32,88,256]{2,1,0:T(8,128)(2,1)} %fusion.52), calls=%async_computation.4 | async-start | bytes 2883584 | tf_op jit(solution)/shard_map/all_to_all | solution.py:38
  79.0 6.1 %copy-start.7 = (bf16[384,256]{1,0:T(8,128)(2,1)S(1)}, bf16[384,256]{1,0:T(8,128)(2,1)}, u32[]{:S(2)}) copy-start(bf16[384,256]{1,0:T(8,128)(2,1)} %param.32) | copy-start | bytes 589828
  79.1 0.8 copy-start.17
  79.1 0.9 copy-start.21
  79.9 8.4 %copy-start.29 = (f32[128]{0:T(128)S(1)}, f32[128]{0:T(128)}, u32[]{:S(2)}) copy-start(f32[128]{0:T(128)} %param.31) | copy-start | bytes 1540
  80.0 0.6 copy-start.14
  123.6 13.5 %copy-start.34 = (bf16[128,512]{1,0:T(8,128)(2,1)}, bf16[128,512]{1,0:T(8,128)(2,1)S(1)}, u32[]{:S(2)}) copy-start(bf16[128,512]{1,0:T(8,128)(2,1)S(1)} %get-tuple-element.96) | copy-start | bytes 393220
  123.6 11.4 %copy-start.28 = (f32[768]{0:T(1024)S(1)}, f32[768]{0:T(1024)}, u32[]{:S(2)}) copy-start(f32[768]{0:T(1024)} %param.41) | copy-start | bytes 9220
  123.6 12.0 %copy-start.2 = (bf16[512,256]{1,0:T(8,128)(2,1)S(1)}, bf16[512,256]{1,0:T(8,128)(2,1)}, u32[]{:S(2)}) copy-start(bf16[512,256]{1,0:T(8,128)(2,1)} %copy-done.1) | copy-start | bytes 786436
  123.6 13.5 %copy-start.12 = (s32[32,32]{0,1:T(8,128)S(1)}, s32[32,32]{0,1:T(8,128)}, u32[]{:S(2)}) copy-start(s32[32,32]{0,1:T(8,128)} %copy-done.11) | copy-start | bytes 12292
  124.6 13.5 %copy-start.19 = (s32[32,32]{1,0:T(8,128)S(1)}, s32[32,32]{1,0:T(8,128)}, u32[]{:S(2)}) copy-start(s32[32,32]{1,0:T(8,128)} %get-tuple-element.107) | copy-start | bytes 12292
  124.6 31.9 %all-to-all-start.5 = ((bf16[512,2,256]{2,1,0:T(2,128)(2,1)}), bf16[512,2,256]{2,1,0:T(2,128)(2,1)S(1)}, u32[]{:S(2)}, u32[]{:S(2)}) async-start(bf16[512,2,256]{2,1,0:T(2,128)(2,1)} %reshape.287), calls=%async_computation.5 | async-start | bytes 1048576 | tf_op jit(solution)/shard_map/all_to_all | solution.py:38
